TPU v7x, 32 devices: a whole 2x2x4 slice. The times are simulated.
32 devices in a mesh: region: 2 (over x), rows: 8 (over z, y), section: 2 (over core).
Axes of the slice: x: 2, y: 2, z: 4, core: 2. Of those that a mesh axis runs over, the one named last changes fastest.
Arguments:
- transitions: float32 [4, 4, 4096, 4096], P(('region', 'section'), None, 'rows'), parts along dimension 0, may hold values from 0 to 1, as said below
- gain: float32 [4, 4, 4096], P(('region', 'section'), None, 'rows'), parts along dimension 0, may hold values from 0 to 1
- cost: float32 [4, 4, 8], P(('region', 'section')), parts along dimension 0, may hold values from 0 to 1
- price_class: int32 [2048], P('region'), parts along dimension 0, may hold values from 0 to 7
- terminal: float32 [8192, 1024], P(('region', 'rows')), parts along dimension 0, may hold values from 0.5 to 3.5
Outputs:
- values: float32 [4, 4096, 1024], P(('region', 'section'), 'rows'), parts along dimension 0
There are 2 independent parts, one for each index of `region`. A program takes and returns all parts, laid end to end along the dimension named above; each array names one. Nothing has to cross between parts.
Inputs may be any that keep to these rules, and one draw needn't show every extreme that they name: `transitions`: entries are nonnegative.
All inputs are finite; a program needn't handle non-finite values.
Results may differ from a plain program's by a relative error of at most 0.0001.
Values sent between devices are 32-bit elements; how exact they have to be, the bound alone decides.
No kernel may reach another device: no remote copies, remote signals or barrier semaphores. Data moves between devices by JAX's collectives and lax.ppermute only.
A program may use at most 128 MiB of HBM per device.

v0:
```python
import jax
import jax.numpy as jnp
from jax import lax
from jax.sharding import PartitionSpec as P


def from_behind(value, axis, by):
    size = lax.axis_size(axis)
    pairs = [(i, i + by) for i in range(size) if 0 <= i + by < size]
    return lax.ppermute(value, axis, pairs)


def shards(transitions, gain, cost, price_class, terminal):
    num_groups = lax.axis_size("section")
    my_group = lax.axis_index("section")
    kernel = transitions[0]
    action_count, rows_here, state_count = kernel.shape
    scenarios = terminal.shape[1]
    price_levels = cost.shape[2]
    batch_count = 4
    batch_width = scenarios // batch_count
    levels = jnp.arange(price_levels, dtype=jnp.int32)
    onehot = (price_class[None, :] == levels[:, None]).astype(jnp.float32)
    charge = jnp.dot(cost[0], onehot, precision=lax.Precision.HIGHEST)
    gains = gain[0]
    is_last = my_group == num_groups - 1

    def accumulate(panel):
        return jnp.einsum(
            "arn,nc->arc",
            kernel,
            panel,
            precision=lax.Precision.HIGHEST,
            preferred_element_type=jnp.float32,
        )

    def advance(step_index, carry):
        incoming, results = carry
        batch_index = step_index - (num_groups - 1 - my_group)
        is_live = (batch_index >= 0) & (batch_index < batch_count)
        clamped = jnp.clip(batch_index, 0, batch_count - 1)
        first_col = clamped * batch_width
        from_end = lax.dynamic_slice_in_dim(terminal, first_col, batch_width, 1)
        current = jnp.where(is_last, from_end, incoming)
        summed = accumulate(lax.all_gather(current, "rows", axis=0, tiled=True))
        batch_charge = lax.dynamic_slice_in_dim(charge, first_col, batch_width, 1)
        action_value = summed + gains[:, :, None] - batch_charge[:, None, :]
        values_now = jnp.max(action_value, axis=0)
        previous = lax.dynamic_slice_in_dim(results, first_col, batch_width, 1)
        results = lax.dynamic_update_slice_in_dim(
            results, jnp.where(is_live, values_now, previous), first_col, 1
        )
        handed = from_behind(values_now, "section", -1)
        return (handed, results)

    step_total = batch_count + num_groups - 1
    start_carry = (
        jnp.zeros((rows_here, batch_width), jnp.float32),
        jnp.zeros((rows_here, scenarios), jnp.float32),
    )
    final_carry = lax.fori_loop(0, step_total, advance, start_carry)
    return final_carry[1][None]


def solution(mesh):
    return jax.shard_map(
        shards,
        mesh=mesh,
        in_specs=(
            P(("region", "section"), None, "rows", None),
            P(("region", "section"), None, "rows"),
            P(("region", "section"), None, None),
            P("region"),
            P(("region", "rows"), None),
        ),
        out_specs=P(("region", "section"), "rows", None),
        check_vma=False,
    )
```

profile of v0, /device:TPU:0, one launch (start us, length us, event | category | flops | bytes accessed | tf_op | source)
XLA Modules:
  0.0 577.6 jit_solution(10681932668837966376)
XLA Ops:
  8.1 1.6 broadcast_in_dim.15.clone
  9.7 561.4 %while.17 = (s32[]{:T(128)}, f32[512,256]{0,1:T(8,128)S(1)}, f32[512,1024]{1,0:T(8,128)}, pred[]{:T(512)}, s32[]{:T(128)}, /*index=5*/f32[512,1024]{1,0:T(8,128)...) while((s32[]{:T(128)}, f32[512,256]{0,1:T(8,128)S(1)}, ...), condition=%wide.region_2.3_spmd, body=%wide.region_0.2_spmd.sunk | while | flops 25771507712 | bytes 63983956 | solution.py:61
  9.7 1.1 constant_dynamic-slice_fusion.6
  11.0 0.9 broadcast_select_fusion.4
  11.9 76.9 %all-gather.2.cloned.1.call-done = f32[4096,256]{0,1:T(8,128)} async-done(((f32[512,256]{0,1:T(8,128)}), f32[4096,256]{0,1:T(8,128)}) %all-gather.2.cloned.1.call-update) | async-done | bytes 4194320 | tf_op jit(solution)/shard_map/while/body/eval_jaxpr/all_gather | solution.py:45
  88.8 32.4 %fusion.13 = f32[512,256]{0,1:T(8,128)S(1)} fusion(f32[4,512,4096]{2,1,0:T(8,128)} %get-tuple-element.345, f32[4096,256]{0,1:T(8,128)} %all-gather.2.cloned.1.call-done, f32[4,256]{1,0:T(4,128)S(1)} %constant_dynamic-slice_fusion.7, f32[4,512]{1,0:T(4,128)S(1)} %bitcast.27), kind=kOutput, calls=%fused_computation.3.clone.1 | convolution fusion | flops 25771245568 | bytes 38285312 | tf_op jit(solution)/shard_map/while/body/eval_jaxpr/arn,nc->arc/dot_general | solution.py:29
  121.2 1.3 collective-permute-start
  122.6 1.1 constant_dynamic-slice_fusion.8
  125.1 1.1 constant_dynamic-slice_fusion.6
  126.3 0.9 broadcast_select_fusion.4
  127.3 73.2 %all-gather.2.cloned.1.call-done = f32[4096,256]{0,1:T(8,128)} async-done(((f32[512,256]{0,1:T(8,128)}), f32[4096,256]{0,1:T(8,128)}) %all-gather.2.cloned.1.call-update) | async-done | bytes 4194320 | tf_op jit(solution)/shard_map/while/body/eval_jaxpr/all_gather | solution.py:45
  200.5 32.4 %fusion.13 = f32[512,256]{0,1:T(8,128)S(1)} fusion(f32[4,512,4096]{2,1,0:T(8,128)} %get-tuple-element.345, f32[4096,256]{0,1:T(8,128)} %all-gather.2.cloned.1.call-done, f32[4,256]{1,0:T(4,128)S(1)} %constant_dynamic-slice_fusion.7, f32[4,512]{1,0:T(4,128)S(1)} %bitcast.27), kind=kOutput, calls=%fused_computation.3.clone.1 | convolution fusion | flops 25771245568 | bytes 38285312 | tf_op jit(solution)/shard_map/while/body/eval_jaxpr/arn,nc->arc/dot_general | solution.py:29
  232.9 1.3 collective-permute-start
  234.2 1.1 constant_dynamic-slice_fusion.8
  236.7 1.1 constant_dynamic-slice_fusion.6
  238.0 0.9 broadcast_select_fusion.4
  238.9 73.2 %all-gather.2.cloned.1.call-done = f32[4096,256]{0,1:T(8,128)} async-done(((f32[512,256]{0,1:T(8,128)}), f32[4096,256]{0,1:T(8,128)}) %all-gather.2.cloned.1.call-update) | async-done | bytes 4194320 | tf_op jit(solution)/shard_map/while/body/eval_jaxpr/all_gather | solution.py:45
  312.1 32.4 %fusion.13 = f32[512,256]{0,1:T(8,128)S(1)} fusion(f32[4,512,4096]{2,1,0:T(8,128)} %get-tuple-element.345, f32[4096,256]{0,1:T(8,128)} %all-gather.2.cloned.1.call-done, f32[4,256]{1,0:T(4,128)S(1)} %constant_dynamic-slice_fusion.7, f32[4,512]{1,0:T(4,128)S(1)} %bitcast.27), kind=kOutput, calls=%fused_computation.3.clone.1 | convolution fusion | flops 25771245568 | bytes 38285312 | tf_op jit(solution)/shard_map/while/body/eval_jaxpr/arn,nc->arc/dot_general | solution.py:29
  344.6 1.3 collective-permute-start
  345.9 1.1 constant_dynamic-slice_fusion.8
  348.4 1.1 constant_dynamic-slice_fusion.6
  349.7 0.9 broadcast_select_fusion.4
  350.6 72.9 %all-gather.2.cloned.1.call-done = f32[4096,256]{0,1:T(8,128)} async-done(((f32[512,256]{0,1:T(8,128)}), f32[4096,256]{0,1:T(8,128)}) %all-gather.2.cloned.1.call-update) | async-done | bytes 4194320 | tf_op jit(solution)/shard_map/while/body/eval_jaxpr/all_gather | solution.py:45
  423.5 32.4 %fusion.13 = f32[512,256]{0,1:T(8,128)S(1)} fusion(f32[4,512,4096]{2,1,0:T(8,128)} %get-tuple-element.345, f32[4096,256]{0,1:T(8,128)} %all-gather.2.cloned.1.call-done, f32[4,256]{1,0:T(4,128)S(1)} %constant_dynamic-slice_fusion.7, f32[4,512]{1,0:T(4,128)S(1)} %bitcast.27), kind=kOutput, calls=%fused_computation.3.clone.1 | convolution fusion | flops 25771245568 | bytes 38285312 | tf_op jit(solution)/shard_map/while/body/eval_jaxpr/arn,nc->arc/dot_general | solution.py:29
  455.9 1.3 collective-permute-start
  457.2 1.1 constant_dynamic-slice_fusion.8
  459.7 1.1 constant_dynamic-slice_fusion.6
  461.0 0.9 broadcast_select_fusion.4
  462.0 72.9 %all-gather.2.cloned.1.call-done = f32[4096,256]{0,1:T(8,128)} async-done(((f32[512,256]{0,1:T(8,128)}), f32[4096,256]{0,1:T(8,128)}) %all-gather.2.cloned.1.call-update) | async-done | bytes 4194320 | tf_op jit(solution)/shard_map/while/body/eval_jaxpr/all_gather | solution.py:45
  534.9 32.4 %fusion.13 = f32[512,256]{0,1:T(8,128)S(1)} fusion(f32[4,512,4096]{2,1,0:T(8,128)} %get-tuple-element.345, f32[4096,256]{0,1:T(8,128)} %all-gather.2.cloned.1.call-done, f32[4,256]{1,0:T(4,128)S(1)} %constant_dynamic-slice_fusion.7, f32[4,512]{1,0:T(4,128)S(1)} %bitcast.27), kind=kOutput, calls=%fused_computation.3.clone.1 | convolution fusion | flops 25771245568 | bytes 38285312 | tf_op jit(solution)/shard_map/while/body/eval_jaxpr/arn,nc->arc/dot_general | solution.py:29
  567.3 1.3 collective-permute-start
  568.6 1.1 constant_dynamic-slice_fusion.8
  (51 shorter events, 9.6 us)
Async XLA Ops:
  6.5 0.7 copy-start
  6.5 3.1 copy-start.1
  9.7 79.1 %all-gather.2.cloned.1.call-start = ((), (), s32[]{:S(2)}) async-start(), calls=%async_computation | async-start | bytes 4718592 | tf_op jit(solution)/shard_map/while/body/eval_jaxpr/all_gather | solution.py:45
  121.2 3.8 collective-permute-start
  125.0 75.4 %all-gather.2.cloned.1.call-start = ((), (), s32[]{:S(2)}) async-start(), calls=%async_computation | async-start | bytes 4718592 | tf_op jit(solution)/shard_map/while/body/eval_jaxpr/all_gather | solution.py:45
  232.9 3.8 collective-permute-start
  236.7 75.4 %all-gather.2.cloned.1.call-start = ((), (), s32[]{:S(2)}) async-start(), calls=%async_computation | async-start | bytes 4718592 | tf_op jit(solution)/shard_map/while/body/eval_jaxpr/all_gather | solution.py:45
  344.6 3.8 collective-permute-start
  348.4 75.1 %all-gather.2.cloned.1.call-start = ((), (), s32[]{:S(2)}) async-start(), calls=%async_computation | async-start | bytes 4718592 | tf_op jit(solution)/shard_map/while/body/eval_jaxpr/all_gather | solution.py:45
  455.9 3.8 collective-permute-start
  459.7 75.1 %all-gather.2.cloned.1.call-start = ((), (), s32[]{:S(2)}) async-start(), calls=%async_computation | async-start | bytes 4718592 | tf_op jit(solution)/shard_map/while/body/eval_jaxpr/all_gather | solution.py:45
  567.3 3.8 collective-permute-start
Sparse Core Ops, SparseCore 0:
  12.7 76.0 all-gather.1
  128.1 72.3 all-gather.1
  239.7 72.3 all-gather.1
  351.1 72.3 all-gather.1
  462.4 72.3 all-gather.1
where the time goes:
time: 579 us; the launch traced here: 578 us
  waiting for transfers between devices  369 us (64%)
  matrix products  163 us (28%)
  local copies, waits for them, and re-layouts  20.3 us (4%)
  between operations  13.1 us (2%)
  starting transfers between devices  6.47 us (1%)
    all_gather x5, waiting for transfers between devices, advance(): summed = accumulate(lax.all_gather(current, 'rows', axis=0, tiled=True))  369 us
    dot_general x5, matrix products, accumulate(): jnp.einsum('arn,nc->arc', kernel, panel, precision=lax.Precision.HIGHEST,...  162 us
  transfers between devices with their start and end apart: 10, of which 10 were waited for; matrix products, arithmetic and copies ran while one was open for 2% of the time, Pallas kernels for 0%

commit v1 on v0

v1 whole, which is shorter than its diff:
```python
import functools

import jax
import jax.numpy as jnp
from jax import lax
from jax.experimental import pallas as pl
from jax.experimental.pallas import tpu as pltpu
from jax.sharding import PartitionSpec as P

WIDTHS = (1, 1)
MINOR = 2
WINDOW = 2


def after(value, *others):
    return lax.optimization_barrier((value, *others))[0]


def split(x):
    high = x.astype(jnp.bfloat16)
    return high, (x - high.astype(jnp.float32)).astype(jnp.bfloat16)


def part_kernel(count, tile, first, last, first_col, order, kernel_hbm, *rest):
    gain_ref, charge_ref = rest[:2] if last else (None, None)
    rest = rest[2:] if last else rest
    blocks, rest = rest[:count], rest[count:]
    total_hbm, rest = (None, rest) if first else (rest[0], rest[1:])
    if last:
        batch_hbm, result_hbm, *rest = rest[-12:]
    else:
        sum_hbm, *rest = rest
    staged, x_high, x_low, tiles, totals, outs, x_sem, t_sem, a_sem, o_sem = rest
    actions, rows, _ = kernel_hbm.shape
    depth, width = blocks[0].shape
    tile_count = rows // tile

    def stage_copy(i):
        return pltpu.make_async_copy(blocks[i], staged.at[i], x_sem.at[i])

    def in_copies(t, slot):
        here = pl.ds(pl.multiple_of(t * tile, tile), tile)
        copies = [
            pltpu.make_async_copy(
                kernel_hbm.at[:, here, pl.ds(pl.multiple_of(order[1 + i] * depth, depth), depth)],
                tiles.at[slot, :, :, pl.ds(i * depth, depth)],
                t_sem.at[slot, i],
            )
            for i in range(count)
        ]
        if not first:
            copies.append(pltpu.make_async_copy(total_hbm.at[:, here, :], totals.at[slot], a_sem.at[slot]))
        return copies

    def out_copies(t, slot):
        here = pl.ds(pl.multiple_of(t * tile, tile), tile)
        if not last:
            return [pltpu.make_async_copy(outs.at[slot], sum_hbm.at[:, here, :], o_sem.at[slot, 0])]
        return [
            pltpu.make_async_copy(outs.at[slot, 0], batch_hbm.at[here, :], o_sem.at[slot, 0]),
            pltpu.make_async_copy(outs.at[slot, 0], result_hbm.at[0, here, pl.ds(first_col, width)], o_sem.at[slot, 1]),
        ]

    @pl.when(order[0] == 1)
    def _():
        for i in range(count):
            stage_copy(i).start()
        for copy in in_copies(0, 0):
            copy.start()
        for i in range(count):
            stage_copy(i).wait()
            high, low = split(staged[i])
            x_high[pl.ds(i * depth, depth), :] = high
            x_low[pl.ds(i * depth, depth), :] = low

        @pl.loop(0, tile_count)
        def _(t):
            slot = lax.rem(t, 2)

            @pl.when(t + 1 < tile_count)
            def _():
                for copy in in_copies(t + 1, 1 - slot):
                    copy.start()

            for copy in in_copies(t, slot):
                copy.wait()

            @pl.when(t >= 2)
            def _():
                for copy in out_copies(t - 2, slot):
                    copy.wait()

            high, low = split(tiles[slot].reshape(actions * tile, count * depth))
            dot = functools.partial(jnp.dot, preferred_element_type=jnp.float32)
            summed = dot(high, x_high[...]) + (dot(high, x_low[...]) + dot(low, x_high[...]))
            summed = summed.reshape(actions, tile, width)
            if not first:
                summed = summed + totals[slot]
            if not last:
                outs[slot] = summed
            else:
                gains = gain_ref[pl.ds(pl.multiple_of(t * tile, tile), tile), :]
                best = None
                for a in range(actions):
                    here = summed[a] + gains[:, a : a + 1] - charge_ref[a : a + 1, :]
                    best = here if best is None else jnp.maximum(best, here)
                outs[slot, 0] = best
            for copy in out_copies(t, slot):
                copy.start()

        for t in range(max(tile_count - 2, 0), tile_count):
            for copy in out_copies(t, t % 2):
                copy.wait()


def part(order, kernel, gains, charge, blocks, total, result, first_col, last):
    first = total is None
    fresh = isinstance(result, tuple)
    actions, rows, _ = kernel.shape
    count = len(blocks)
    depth, width = blocks[0].shape
    tile = min(rows, 128)
    hbm = pl.BlockSpec(memory_space=pl.ANY)
    vmem = pl.BlockSpec(memory_space=pltpu.VMEM)
    operands, specs = [order, kernel], [pl.BlockSpec(memory_space=pltpu.SMEM), hbm]
    if last:
        operands += [gains, charge]
        specs += [vmem, vmem]
    operands += blocks
    specs += [hbm] * count
    if not first:
        operands.append(total)
        specs.append(hbm)
    aliases = {}
    if last:
        if not fresh:
            aliases = {len(operands): 1}
            operands.append(result)
            specs.append(hbm)
        out_shape = (
            jax.ShapeDtypeStruct((rows, width), jnp.float32),
            jax.ShapeDtypeStruct(result if fresh else result.shape, jnp.float32),
        )
    else:
        out_shape = (jax.ShapeDtypeStruct((actions, rows, width), jnp.float32),)
    return pl.pallas_call(
        functools.partial(part_kernel, count, tile, first, last, first_col),
        out_shape=out_shape,
        in_specs=specs,
        out_specs=tuple([hbm] * len(out_shape)),
        scratch_shapes=[
            pltpu.VMEM((count, depth, width), jnp.float32),
            pltpu.VMEM((count * depth, width), jnp.bfloat16),
            pltpu.VMEM((count * depth, width), jnp.bfloat16),
            pltpu.VMEM((2, actions, tile, count * depth), jnp.float32),
            pltpu.VMEM((2, actions, tile, width) if not first else (2, 1, 8, 128), jnp.float32),
            pltpu.VMEM((2, 1 if last else actions, tile, width), jnp.float32),
            pltpu.SemaphoreType.DMA((count,)),
            pltpu.SemaphoreType.DMA((2, count)),
            pltpu.SemaphoreType.DMA((2,)),
            pltpu.SemaphoreType.DMA((2, 2)),
        ],
        input_output_aliases=aliases,
        compiler_params=pltpu.CompilerParams(vmem_limit_bytes=40 * 1024 * 1024),
        cost_estimate=pl.CostEstimate(
            flops=6 * actions * rows * count * depth * width,
            bytes_accessed=4 * actions * rows * count * depth,
            transcendentals=0,
        ),
        name="part",
    )(*operands)


class Lane:
    def __init__(self):
        self.done = []

    def send(self, value, pairs, *behind):
        behind = list(behind)
        if len(self.done) >= WINDOW:
            behind.append(self.done[-WINDOW])
        if behind:
            value = after(value, *behind)
        value = lax.ppermute(value, ("rows", "section"), pairs)
        self.done.append(value)
        return value


def shards(transitions, gain, cost, price_class, terminal):
    groups = lax.axis_size("section")
    my_group = lax.axis_index("section")
    row_count = lax.axis_size("rows")
    minor = MINOR if row_count % MINOR == 0 else 1
    major = row_count // minor
    me = lax.axis_index("rows")
    z, y = me // minor, me % minor

    def pairs(by, across, begin, target):
        return [
            (
                (i * minor + j) * groups + begin,
                ((i + by) % major * minor + (j + across) % minor) * groups + target,
            )
            for i in range(major)
            for j in range(minor)
        ]

    kernel = transitions[0]
    rows_here = kernel.shape[1]
    scenarios = terminal.shape[1]
    levels = jnp.arange(cost.shape[2], dtype=jnp.int32)
    onehot = price_class[None, :] == levels[:, None]
    charge = jnp.sum(jnp.where(onehot[None], cost[0][:, :, None], 0.0), axis=1)
    gains = gain[0].T
    bounds = [0]
    for share in WIDTHS:
        bounds.append(bounds[-1] + scenarios * share // sum(WIDTHS))
    spans = list(zip(bounds[:-1], bounds[1:]))
    result = (1, rows_here, scenarios)
    batches = [terminal[:, a:b] for a, b in spans]
    shifts = [0, 1, *([major - 1] if major > 2 else []), *range(2, major - 1)]
    for group in range(groups - 1, -1, -1):
        live = (my_group == group).astype(jnp.int32)
        lengthwise, crosswise = Lane(), Lane()
        for b, (a0, a1) in enumerate(spans):
            own = batches[b]
            if group < groups - 1:
                own = lax.ppermute(own, ("rows", "section"), pairs(0, 0, group + 1, group))
            line = [own]
            crossed = [crosswise.send(own, pairs(0, c, group, group)) for c in range(1, minor)]
            for by in shifts[1:]:
                line.append(lengthwise.send(own, pairs(by, 0, group, group)))
            for value in line[1:]:
                crossed += [crosswise.send(value, pairs(0, c, group, group)) for c in range(1, minor)]
            line_order = [((z - by) % major) * minor + y for by in shifts]
            crossed_order = [
                ((z - by) % major) * minor + (y - c) % minor for by in shifts for c in range(1, minor)
            ]
            batch_charge = charge[:, a0:a1]

            def table(order):
                return jnp.stack([live] + [jnp.asarray(i, jnp.int32) for i in order])

            (total,) = part(table(line_order), kernel, gains, batch_charge, line, None, None, a0, False)
            batches[b], result = part(
                table(crossed_order), kernel, gains, batch_charge, crossed, total, result, a0, True
            )
    return result


def solution(mesh):
    return jax.shard_map(
        shards,
        mesh=mesh,
        in_specs=(
            P(("region", "section"), None, "rows", None),
            P(("region", "section"), None, "rows"),
            P(("region", "section"), None, None),
            P("region"),
            P(("region", "rows"), None),
        ),
        out_specs=P(("region", "section"), "rows", None),
        check_vma=False,
    )
```

time: 579 us -> 285 us (0.49)
  waiting for transfers between devices: 369 us -> 143 us
  matrix products: 163 us -> 0 us
  Pallas kernels: 0 us -> 74.8 us
  starting transfers between devices: 6.47 us -> 62.4 us
  local copies, waits for them, and re-layouts: 20.3 us -> 3.23 us
  between operations: 13.1 us -> 0.76 us
    all_gather x5 -> x0, waiting for transfers between devices: 369 us -> none  [advance(): summed = accumulate(lax.all_gather(current, 'rows', axis=0, tiled=True))]
    dot_general x6 -> x0, matrix products: 163 us -> none  [the longest x5 162 us: accumulate(): jnp.einsum('arn,nc->arc', kernel, panel, precision=lax.Precision.HIGHEST,...]
    ppermute x5 -> x30, waiting for transfers between devices: 0.37 us -> 143 us  [the longest x2 107 us: shards(): own = lax.ppermute(own, ('rows', 'section'), pairs(0, 0, group + 1, group))]
    pallas_call x0 -> x8, Pallas kernels: none -> 74.8 us  [part(): pl.pallas_call(functools.partial(part_kernel, count, tile, first, last, f...]
    ppermute x5 -> x30, starting transfers between devices: 6.46 us -> 62.4 us  [the longest x28 59.9 us: send(): value = lax.ppermute(value, ('rows', 'section'), pairs)]
    dynamic_slice x25 -> x0, local copies, waits for them, and re-layouts: 12.8 us -> none  [the longest x10 6.4 us: advance(): previous = lax.dynamic_slice_in_dim(results, first_col, batch_width, 1)]
  transfers between devices with their start and end apart: 10 -> 30, of which waited for: 10 -> 6; matrix products, arithmetic and copies ran while one was open for 2% -> 0% of each run, Pallas kernels for 0% -> 20%
where the time goes in v1:
time: 285 us; the launch traced here: 284 us
  waiting for transfers between devices  143 us (50%)
  Pallas kernels  74.8 us (26%)
  starting transfers between devices  62.4 us (22%)
  local copies, waits for them, and re-layouts  3.23 us (1%)
    ppermute x2, waiting for transfers between devices, shards(): own = lax.ppermute(own, ('rows', 'section'), pairs(0, 0, group + 1, group))  107 us
    pallas_call x8, Pallas kernels, part(): pl.pallas_call(functools.partial(part_kernel, count, tile, first, last, f...  74.8 us
    ppermute x28, starting transfers between devices, send(): value = lax.ppermute(value, ('rows', 'section'), pairs)  59.9 us
    ppermute x28, waiting for transfers between devices, send(): value = lax.ppermute(value, ('rows', 'section'), pairs)  35.2 us
  transfers between devices with their start and end apart: 30, of which 6 were waited for; matrix products, arithmetic and copies ran while one was open for 0% of the time, Pallas kernels for 20%

profile of v1, /device:TPU:0, one launch (start us, length us, event | category | flops | bytes accessed | tf_op | source)
XLA Modules:
  0.0 283.9 jit_solution(240776841874015690)
XLA Ops:
  0.0 1.8 fusion
  1.8 1.6 collective-permute-start.5
  4.1 1.7 collective-permute-start
  5.8 1.7 collective-permute-start.6
  7.5 1.6 collective-permute-start.7
  10.1 1.6 collective-permute-start.2
  18.2 1.3 collective-permute-start.15
  21.0 100.0 %collective-permute-done.15.rest_0_ = f32[512,512]{1,0:T(8,128)S(1)} collective-permute-done((f32[512,512]{1,0:T(8,128)S(1)}, f32[512,512]{1,0:T(8,128)S(1)}, u32[]{:S(2)}, u32[]{:S(2)}) %collective-permute-start.15) | collective-permute-done | bytes 1048608 | tf_op jit(solution)/shard_map/ppermute | solution.py:228
  121.1 3.6 %collective-permute-start.21 = (f32[512,512]{1,0:T(8,128)S(1)}, f32[512,512]{1,0:T(8,128)}, u32[]{:S(2)}, u32[]{:S(2)}) collective-permute-start(f32[512,512]{1,0:T(8,128)S(1)} %collective-permute-done.15.rest_0_), channel_id=1, source_target_pairs={{0,4},{2,6},{4,8},{6,10},{8,12},{10,14},{12,0},{14,2},{16,20},{18,... | collective-permute-start | bytes 3145736 | tf_op jit(solution)/shard_map/ppermute | solution.py:184
  125.4 2.4 collective-permute-start.17
  127.8 4.0 %collective-permute-start.16 = (f32[512,512]{1,0:T(8,128)S(1)}, f32[512,512]{1,0:T(8,128)}, u32[]{:S(2)}, u32[]{:S(2)}) collective-permute-start(f32[512,512]{1,0:T(8,128)S(1)} %collective-permute-done.15.rest_0_), channel_id=1, source_target_pairs={{0,12},{2,14},{4,0},{6,2},{8,4},{10,6},{12,8},{14,10},{16,28},{18,... | collective-permute-start | bytes 3145736 | tf_op jit(solution)/shard_map/ppermute | solution.py:184
  131.8 8.0 %collective-permute-done.21.rest_1_ = f32[512,512]{1,0:T(8,128)} collective-permute-done((f32[512,512]{1,0:T(8,128)S(1)}, f32[512,512]{1,0:T(8,128)}, u32[]{:S(2)}, u32[]{:S(2)}) %collective-permute-start.21) | collective-permute-done | bytes 1048608 | tf_op jit(solution)/shard_map/ppermute | solution.py:184
  139.8 2.6 collective-permute-start.22
  142.4 2.4 collective-permute-start.23
  145.7 1.3 collective-permute-start.14
  147.0 6.4 %collective-permute-done.17.rest_2_ = f32[512,512]{1,0:T(8,128)S(1)} collective-permute-done((f32[512,512]{1,0:T(8,128)S(1)}, f32[512,512]{1,0:T(8,128)S(1)}, u32[]{:S(2)}, u32[]{:S(2)}) %collective-permute-start.17) | collective-permute-done | bytes 1048608 | tf_op jit(solution)/shard_map/ppermute | solution.py:184
  153.4 2.4 collective-permute-start.18
  156.0 17.4 %collective-permute-done.22.rest_3_ = f32[512,512]{1,0:T(8,128)} collective-permute-done((f32[512,512]{1,0:T(8,128)S(1)}, f32[512,512]{1,0:T(8,128)}, u32[]{:S(2)}, u32[]{:S(2)}) %collective-permute-start.22) | collective-permute-done | bytes 1048608 | tf_op jit(solution)/shard_map/ppermute | solution.py:184
  173.3 2.4 collective-permute-start.24
  175.7 7.3 %collective-permute-done.14.rest_0_ = f32[512,512]{1,0:T(8,128)} collective-permute-done((f32[512,512]{1,0:T(8,128)}, f32[512,512]{1,0:T(8,128)}, u32[]{:S(2)}, u32[]{:S(2)}) %collective-permute-start.14) | collective-permute-done | bytes 1048608 | tf_op jit(solution)/shard_map/ppermute | solution.py:228
  183.1 2.4 collective-permute-start.19
  185.5 2.4 collective-permute-start.20
  187.9 5.2 %collective-permute-start.26 = (f32[512,512]{1,0:T(8,128)}, f32[512,512]{1,0:T(8,128)S(1)}, u32[]{:S(2)}, u32[]{:S(2)}) collective-permute-start(f32[512,512]{1,0:T(8,128)} %collective-permute-done.14.rest_0_), channel_id=1, source_target_pairs={{0,12},{2,14},{4,0},{6,2},{8,4},{10,6},{12,8},{14,10},{16,28},{18,... | collective-permute-start | bytes 3145736 | tf_op jit(solution)/shard_map/ppermute | solution.py:184
  193.2 18.0 %part.13.rest_6_ = f32[4,512,512]{2,1,0:T(8,128)S(1)} custom-call(s32[5]{0:T(128)S(1)} %stack.97.order, f32[4,512,4096]{2,1,0:T(8,128)} %bitcast.24, f32[512,512]{1,0:T(8,128)S(1)} %collective-permute-done.15.rest_0_, f32[512,512]{1,0:T(8,128)} %collective-permute-done.21.rest_1_, f32[512,512]{1,0:T(8,128)} %collective-permute-done.16.rest_2_, ...), custom_call_target="tpu_custom_call" | custom-call | flops 12884901888 | bytes 16777216 | tf_op jit(solution)/shard_map/part/pallas_call | solution.py:146
  211.1 3.5 %collective-permute-start.25 = (f32[512,512]{1,0:T(8,128)S(1)}, f32[512,512]{1,0:T(8,128)S(1)}, u32[]{:S(2)}, u32[]{:S(2)}) collective-permute-start(f32[512,512]{1,0:T(8,128)S(1)} %collective-permute-done.20.rest_1_), channel_id=1, source_target_pairs={{0,2},{2,0},{4,6},{6,4},{8,10},{10,8},{12,14},{14,12},{16,18},{18,... | collective-permute-start | bytes 3145736 | tf_op jit(solution)/shard_map/ppermute | solution.py:184
  214.6 7.0 %collective-permute-start.28 = (f32[512,512]{1,0:T(8,128)}, f32[512,512]{1,0:T(8,128)S(1)}, u32[]{:S(2)}, u32[]{:S(2)}) collective-permute-start(f32[512,512]{1,0:T(8,128)} %collective-permute-done.14.rest_0_), channel_id=1, source_target_pairs={{0,8},{2,10},{4,12},{6,14},{8,0},{10,2},{12,4},{14,6},{16,24},{18,... | collective-permute-start | bytes 3145736 | tf_op jit(solution)/shard_map/ppermute | solution.py:184
  221.6 2.4 collective-permute-start.27
  224.1 18.4 %part.14 = (f32[512,512]{1,0:T(8,128)}, f32[1,512,1024]{2,1,0:T(8,128)}) custom-call(s32[5]{0:T(128)S(1)} %stack.40.order, f32[4,512,4096]{2,1,0:T(8,128)} %bitcast.25, f32[512,4]{1,0:T(8,128)S(1)} %bitcast.17, f32[4,512]{1,0:T(4,128)S(1)} %get-tuple-element.59.rest_1_, ...), custom_call_target="tpu_custom_call", output_to_operand_aliasing={{1}: (9, {})} | custom-call | flops 12884901888 | bytes 16777216 | tf_op jit(solution)/shard_map/part/pallas_call | solution.py:146
  242.4 3.4 %collective-permute-done.28.rest_3_ = f32[512,512]{1,0:T(8,128)S(1)} collective-permute-done((f32[512,512]{1,0:T(8,128)}, f32[512,512]{1,0:T(8,128)S(1)}, u32[]{:S(2)}, u32[]{:S(2)}) %collective-permute-start.28) | collective-permute-done | bytes 1048608 | tf_op jit(solution)/shard_map/ppermute | solution.py:184
  245.8 2.4 collective-permute-start.29
  248.2 17.6 %part.12.rest_6_ = f32[4,512,512]{2,1,0:T(8,128)S(1)} custom-call(s32[5]{0:T(128)S(1)} %stack.97.order, f32[4,512,4096]{2,1,0:T(8,128)} %bitcast.26, f32[512,512]{1,0:T(8,128)} %collective-permute-done.14.rest_0_, f32[512,512]{1,0:T(8,128)S(1)} %collective-permute-done.20.rest_1_, f32[512,512]{1,0:T(8,128)S(1)} %collective-permute-done.26.rest_2_, ...), custom_call_target="tpu_custom_call" | custom-call | flops 12884901888 | bytes 16777216 | tf_op jit(solution)/shard_map/part/pallas_call | solution.py:146
  265.8 17.9 %part.15 = (f32[512,512]{1,0:T(8,128)}, f32[1,512,1024]{2,1,0:T(8,128)}) custom-call(s32[5]{0:T(128)S(1)} %stack.40.order, f32[4,512,4096]{2,1,0:T(8,128)} %bitcast.27, f32[512,4]{1,0:T(8,128)S(1)} %bitcast.18, f32[4,512]{1,0:T(4,128)S(1)} %get-tuple-element.60.rest_1_, ...), custom_call_target="tpu_custom_call", output_to_operand_aliasing={{1}: (9, {})} | custom-call | flops 12884901888 | bytes 16777216 | tf_op jit(solution)/shard_map/part/pallas_call | solution.py:146
  (55 shorter events, 11.2 us)
Async XLA Ops:
  0.0 12.9 %copy-start.3 = (s32[1024]{0:T(1024)S(1)}, s32[1024]{0:T(1024)}, u32[]{:S(2)}) copy-start(s32[1024]{0:T(1024)} %param.8) | copy-start | bytes 12292
  0.0 12.9 %copy-start.4 = (f32[1,4,8]{2,1,0:T(4,128)S(1)}, f32[1,4,8]{2,1,0:T(4,128)}, u32[]{:S(2)}) copy-start(f32[1,4,8]{2,1,0:T(4,128)} %param.7) | copy-start | bytes 388
  1.8 4.0 %collective-permute-start.5 = (f32[512,512]{1,0:T(8,128)S(1)}, f32[512,512]{1,0:T(8,128)}, u32[]{:S(2)}, u32[]{:S(2)}) collective-permute-start(f32[512,512]{1,0:T(8,128)S(1)} %get-tuple-element.34.rest_0_), channel_id=1, source_target_pairs={{1,5},{3,7},{5,9},{7,11},{9,13},{11,15},{13,1},{15,3},{17,21},{19,... | collective-permute-start | bytes 3145736 | tf_op jit(solution)/shard_map/ppermute | solution.py:184
  3.4 5.7 %collective-permute-start.1 = (f32[512,512]{1,0:T(8,128)S(1)}, f32[512,512]{1,0:T(8,128)S(1)}, u32[]{:S(2)}, u32[]{:S(2)}) collective-permute-start(f32[512,512]{1,0:T(8,128)S(1)} %get-tuple-element.34.rest_0_), channel_id=1, source_target_pairs={{1,3},{3,1},{5,7},{7,5},{9,11},{11,9},{13,15},{15,13},{17,19},{19,... | collective-permute-start | bytes 3145736 | tf_op jit(solution)/shard_map/ppermute | solution.py:184
  4.1 6.0 %collective-permute-start = (f32[512,512]{1,0:T(8,128)S(1)}, f32[512,512]{1,0:T(8,128)}, u32[]{:S(2)}, u32[]{:S(2)}) collective-permute-start(f32[512,512]{1,0:T(8,128)S(1)} %get-tuple-element.34.rest_0_), channel_id=1, source_target_pairs={{1,13},{3,15},{5,1},{7,3},{9,5},{11,7},{13,9},{15,11},{17,29},{19,... | collective-permute-start | bytes 3145736 | tf_op jit(solution)/shard_map/ppermute | solution.py:184
  5.8 7.3 %collective-permute-start.6 = (f32[512,512]{1,0:T(8,128)S(1)}, f32[512,512]{1,0:T(8,128)}, u32[]{:S(2)}, u32[]{:S(2)}) collective-permute-start(f32[512,512]{1,0:T(8,128)S(1)} %get-tuple-element.34.rest_0_), channel_id=1, source_target_pairs={{1,9},{3,11},{5,13},{7,15},{9,1},{11,3},{13,5},{15,7},{17,25},{19,... | collective-permute-start | bytes 3145736 | tf_op jit(solution)/shard_map/ppermute | solution.py:184
  7.5 6.3 %collective-permute-start.7 = (f32[512,512]{1,0:T(8,128)}, f32[512,512]{1,0:T(8,128)}, u32[]{:S(2)}, u32[]{:S(2)}) collective-permute-start(f32[512,512]{1,0:T(8,128)} %collective-permute-done.5.rest_1_), channel_id=1, source_target_pairs={{1,3},{3,1},{5,7},{7,5},{9,11},{11,9},{13,15},{15,13},{17,19},{19,... | collective-permute-start | bytes 3145736 | tf_op jit(solution)/shard_map/ppermute | solution.py:184
  10.1 4.5 %collective-permute-start.2 = (f32[512,512]{1,0:T(8,128)}, f32[512,512]{1,0:T(8,128)}, u32[]{:S(2)}, u32[]{:S(2)}) collective-permute-start(f32[512,512]{1,0:T(8,128)} %collective-permute-done.rest_2_), channel_id=1, source_target_pairs={{1,3},{3,1},{5,7},{7,5},{9,11},{11,9},{13,15},{15,13},{17,19},{19,... | collective-permute-start | bytes 3145736 | tf_op jit(solution)/shard_map/ppermute | solution.py:184
  11.7 3.6 %collective-permute-start.4 = (f32[512,512]{1,0:T(8,128)S(1)}, f32[512,512]{1,0:T(8,128)S(1)}, u32[]{:S(2)}, u32[]{:S(2)}) collective-permute-start(f32[512,512]{1,0:T(8,128)S(1)} %get-tuple-element.39.rest_0_), channel_id=1, source_target_pairs={{1,5},{3,7},{5,9},{7,11},{9,13},{11,15},{13,1},{15,3},{17,21},{19,... | collective-permute-start | bytes 3145736 | tf_op jit(solution)/shard_map/ppermute | solution.py:184
  13.0 6.5 %collective-permute-start.10 = (f32[512,512]{1,0:T(8,128)S(1)}, f32[512,512]{1,0:T(8,128)S(1)}, u32[]{:S(2)}, u32[]{:S(2)}) collective-permute-start(f32[512,512]{1,0:T(8,128)S(1)} %get-tuple-element.39.rest_0_), channel_id=1, source_target_pairs={{1,13},{3,15},{5,1},{7,3},{9,5},{11,7},{13,9},{15,11},{17,29},{19,... | collective-permute-start | bytes 3145736 | tf_op jit(solution)/shard_map/ppermute | solution.py:184
  13.8 3.0 %collective-permute-start.8 = (f32[512,512]{1,0:T(8,128)}, f32[512,512]{1,0:T(8,128)S(1)}, u32[]{:S(2)}, u32[]{:S(2)}) collective-permute-start(f32[512,512]{1,0:T(8,128)} %collective-permute-done.6.rest_3_), channel_id=1, source_target_pairs={{1,3},{3,1},{5,7},{7,5},{9,11},{11,9},{13,15},{15,13},{17,19},{19,... | collective-permute-start | bytes 3145736 | tf_op jit(solution)/shard_map/ppermute | solution.py:184
  14.5 5.0 %collective-permute-start.3 = (f32[512,512]{1,0:T(8,128)S(1)}, f32[512,512]{1,0:T(8,128)S(1)}, u32[]{:S(2)}, u32[]{:S(2)}) collective-permute-start(f32[512,512]{1,0:T(8,128)S(1)} %get-tuple-element.39.rest_0_), channel_id=1, source_target_pairs={{1,3},{3,1},{5,7},{7,5},{9,11},{11,9},{13,15},{15,13},{17,19},{19,... | collective-permute-start | bytes 3145736 | tf_op jit(solution)/shard_map/ppermute | solution.py:184
  15.3 5.0 %collective-permute-start.12 = (f32[512,512]{1,0:T(8,128)S(1)}, f32[512,512]{1,0:T(8,128)S(1)}, u32[]{:S(2)}, u32[]{:S(2)}) collective-permute-start(f32[512,512]{1,0:T(8,128)S(1)} %get-tuple-element.39.rest_0_), channel_id=1, source_target_pairs={{1,9},{3,11},{5,13},{7,15},{9,1},{11,3},{13,5},{15,7},{17,25},{19,... | collective-permute-start | bytes 3145736 | tf_op jit(solution)/shard_map/ppermute | solution.py:184
  16.8 3.5 %collective-permute-start.9 = (f32[512,512]{1,0:T(8,128)S(1)}, f32[512,512]{1,0:T(8,128)S(1)}, u32[]{:S(2)}, u32[]{:S(2)}) collective-permute-start(f32[512,512]{1,0:T(8,128)S(1)} %collective-permute-done.4.rest_1_), channel_id=1, source_target_pairs={{1,3},{3,1},{5,7},{7,5},{9,11},{11,9},{13,15},{15,13},{17,19},{19,... | collective-permute-start | bytes 3145736 | tf_op jit(solution)/shard_map/ppermute | solution.py:184
  18.2 102.8 %collective-permute-start.15 = (f32[512,512]{1,0:T(8,128)S(1)}, f32[512,512]{1,0:T(8,128)S(1)}, u32[]{:S(2)}, u32[]{:S(2)}) collective-permute-start(f32[512,512]{1,0:T(8,128)S(1)} %get-tuple-element.43), channel_id=1, source_target_pairs={{1,0},{3,2},{5,4},{7,6},{9,8},{11,10},{13,12},{15,14},{17,16},{19,... | collective-permute-start | bytes 3145736 | tf_op jit(solution)/shard_map/ppermute | solution.py:228
  19.6 122.8 %collective-permute-start.11 = (f32[512,512]{1,0:T(8,128)S(1)}, f32[512,512]{1,0:T(8,128)S(1)}, u32[]{:S(2)}, u32[]{:S(2)}) collective-permute-start(f32[512,512]{1,0:T(8,128)S(1)} %collective-permute-done.10.rest_2_), channel_id=1, source_target_pairs={{1,3},{3,1},{5,7},{7,5},{9,11},{11,9},{13,15},{15,13},{17,19},{19,... | collective-permute-start | bytes 3145736 | tf_op jit(solution)/shard_map/ppermute | solution.py:184
  20.3 124.5 %collective-permute-start.13 = (f32[512,512]{1,0:T(8,128)S(1)}, f32[512,512]{1,0:T(8,128)S(1)}, u32[]{:S(2)}, u32[]{:S(2)}) collective-permute-start(f32[512,512]{1,0:T(8,128)S(1)} %collective-permute-done.12.rest_3_), channel_id=1, source_target_pairs={{1,3},{3,1},{5,7},{7,5},{9,11},{11,9},{13,15},{15,13},{17,19},{19,... | collective-permute-start | bytes 3145736 | tf_op jit(solution)/shard_map/ppermute | solution.py:184
  121.1 18.7 %collective-permute-start.21 = (f32[512,512]{1,0:T(8,128)S(1)}, f32[512,512]{1,0:T(8,128)}, u32[]{:S(2)}, u32[]{:S(2)}) collective-permute-start(f32[512,512]{1,0:T(8,128)S(1)} %collective-permute-done.15.rest_0_), channel_id=1, source_target_pairs={{0,4},{2,6},{4,8},{6,10},{8,12},{10,14},{12,0},{14,2},{16,20},{18,... | collective-permute-start | bytes 3145736 | tf_op jit(solution)/shard_map/ppermute | solution.py:184
  125.4 28.0 %collective-permute-start.17 = (f32[512,512]{1,0:T(8,128)S(1)}, f32[512,512]{1,0:T(8,128)S(1)}, u32[]{:S(2)}, u32[]{:S(2)}) collective-permute-start(f32[512,512]{1,0:T(8,128)S(1)} %collective-permute-done.15.rest_0_), channel_id=1, source_target_pairs={{0,2},{2,0},{4,6},{6,4},{8,10},{10,8},{12,14},{14,12},{16,18},{18,... | collective-permute-start | bytes 3145736 | tf_op jit(solution)/shard_map/ppermute | solution.py:184
  127.8 25.6 %collective-permute-start.16 = (f32[512,512]{1,0:T(8,128)S(1)}, f32[512,512]{1,0:T(8,128)}, u32[]{:S(2)}, u32[]{:S(2)}) collective-permute-start(f32[512,512]{1,0:T(8,128)S(1)} %collective-permute-done.15.rest_0_), channel_id=1, source_target_pairs={{0,12},{2,14},{4,0},{6,2},{8,4},{10,6},{12,8},{14,10},{16,28},{18,... | collective-permute-start | bytes 3145736 | tf_op jit(solution)/shard_map/ppermute | solution.py:184
  139.8 33.5 %collective-permute-start.22 = (f32[512,512]{1,0:T(8,128)S(1)}, f32[512,512]{1,0:T(8,128)}, u32[]{:S(2)}, u32[]{:S(2)}) collective-permute-start(f32[512,512]{1,0:T(8,128)S(1)} %collective-permute-done.15.rest_0_), channel_id=1, source_target_pairs={{0,8},{2,10},{4,12},{6,14},{8,0},{10,2},{12,4},{14,6},{16,24},{18,... | collective-permute-start | bytes 3145736 | tf_op jit(solution)/shard_map/ppermute | solution.py:184
  142.4 31.0 %collective-permute-start.23 = (f32[512,512]{1,0:T(8,128)}, f32[512,512]{1,0:T(8,128)}, u32[]{:S(2)}, u32[]{:S(2)}) collective-permute-start(f32[512,512]{1,0:T(8,128)} %collective-permute-done.21.rest_1_), channel_id=1, source_target_pairs={{0,2},{2,0},{4,6},{6,4},{8,10},{10,8},{12,14},{14,12},{16,18},{18,... | collective-permute-start | bytes 3145736 | tf_op jit(solution)/shard_map/ppermute | solution.py:184
  145.7 37.4 %collective-permute-start.14 = (f32[512,512]{1,0:T(8,128)}, f32[512,512]{1,0:T(8,128)}, u32[]{:S(2)}, u32[]{:S(2)}) collective-permute-start(f32[512,512]{1,0:T(8,128)} %get-tuple-element.42), channel_id=1, source_target_pairs={{1,0},{3,2},{5,4},{7,6},{9,8},{11,10},{13,12},{15,14},{17,16},{19,... | collective-permute-start | bytes 3145736 | tf_op jit(solution)/shard_map/ppermute | solution.py:228
  153.4 29.7 %collective-permute-start.18 = (f32[512,512]{1,0:T(8,128)}, f32[512,512]{1,0:T(8,128)}, u32[]{:S(2)}, u32[]{:S(2)}) collective-permute-start(f32[512,512]{1,0:T(8,128)} %collective-permute-done.16.rest_2_), channel_id=1, source_target_pairs={{0,2},{2,0},{4,6},{6,4},{8,10},{10,8},{12,14},{14,12},{16,18},{18,... | collective-permute-start | bytes 3145736 | tf_op jit(solution)/shard_map/ppermute | solution.py:184
  173.3 37.8 %collective-permute-start.24 = (f32[512,512]{1,0:T(8,128)}, f32[512,512]{1,0:T(8,128)S(1)}, u32[]{:S(2)}, u32[]{:S(2)}) collective-permute-start(f32[512,512]{1,0:T(8,128)} %collective-permute-done.22.rest_3_), channel_id=1, source_target_pairs={{0,2},{2,0},{4,6},{6,4},{8,10},{10,8},{12,14},{14,12},{16,18},{18,... | collective-permute-start | bytes 3145736 | tf_op jit(solution)/shard_map/ppermute | solution.py:184
  183.1 38.5 %collective-permute-start.19 = (f32[512,512]{1,0:T(8,128)}, f32[512,512]{1,0:T(8,128)S(1)}, u32[]{:S(2)}, u32[]{:S(2)}) collective-permute-start(f32[512,512]{1,0:T(8,128)} %collective-permute-done.14.rest_0_), channel_id=1, source_target_pairs={{0,2},{2,0},{4,6},{6,4},{8,10},{10,8},{12,14},{14,12},{16,18},{18,... | collective-permute-start | bytes 3145736 | tf_op jit(solution)/shard_map/ppermute | solution.py:184
  185.5 25.6 %collective-permute-start.20 = (f32[512,512]{1,0:T(8,128)}, f32[512,512]{1,0:T(8,128)S(1)}, u32[]{:S(2)}, u32[]{:S(2)}) collective-permute-start(f32[512,512]{1,0:T(8,128)} %collective-permute-done.14.rest_0_), channel_id=1, source_target_pairs={{0,4},{2,6},{4,8},{6,10},{8,12},{10,14},{12,0},{14,2},{16,20},{18,... | collective-permute-start | bytes 3145736 | tf_op jit(solution)/shard_map/ppermute | solution.py:184
  187.9 33.7 %collective-permute-start.26 = (f32[512,512]{1,0:T(8,128)}, f32[512,512]{1,0:T(8,128)S(1)}, u32[]{:S(2)}, u32[]{:S(2)}) collective-permute-start(f32[512,512]{1,0:T(8,128)} %collective-permute-done.14.rest_0_), channel_id=1, source_target_pairs={{0,12},{2,14},{4,0},{6,2},{8,4},{10,6},{12,8},{14,10},{16,28},{18,... | collective-permute-start | bytes 3145736 | tf_op jit(solution)/shard_map/ppermute | solution.py:184
  211.1 31.3 %collective-permute-start.25 = (f32[512,512]{1,0:T(8,128)S(1)}, f32[512,512]{1,0:T(8,128)S(1)}, u32[]{:S(2)}, u32[]{:S(2)}) collective-permute-start(f32[512,512]{1,0:T(8,128)S(1)} %collective-permute-done.20.rest_1_), channel_id=1, source_target_pairs={{0,2},{2,0},{4,6},{6,4},{8,10},{10,8},{12,14},{14,12},{16,18},{18,... | collective-permute-start | bytes 3145736 | tf_op jit(solution)/shard_map/ppermute | solution.py:184
  214.6 31.2 %collective-permute-start.28 = (f32[512,512]{1,0:T(8,128)}, f32[512,512]{1,0:T(8,128)S(1)}, u32[]{:S(2)}, u32[]{:S(2)}) collective-permute-start(f32[512,512]{1,0:T(8,128)} %collective-permute-done.14.rest_0_), channel_id=1, source_target_pairs={{0,8},{2,10},{4,12},{6,14},{8,0},{10,2},{12,4},{14,6},{16,24},{18,... | collective-permute-start | bytes 3145736 | tf_op jit(solution)/shard_map/ppermute | solution.py:184
  221.6 44.1 %collective-permute-start.27 = (f32[512,512]{1,0:T(8,128)S(1)}, f32[512,512]{1,0:T(8,128)S(1)}, u32[]{:S(2)}, u32[]{:S(2)}) collective-permute-start(f32[512,512]{1,0:T(8,128)S(1)} %collective-permute-done.26.rest_2_), channel_id=1, source_target_pairs={{0,2},{2,0},{4,6},{6,4},{8,10},{10,8},{12,14},{14,12},{16,18},{18,... | collective-permute-start | bytes 3145736 | tf_op jit(solution)/shard_map/ppermute | solution.py:184
  245.8 20.0 %collective-permute-start.29 = (f32[512,512]{1,0:T(8,128)S(1)}, f32[512,512]{1,0:T(8,128)S(1)}, u32[]{:S(2)}, u32[]{:S(2)}) collective-permute-start(f32[512,512]{1,0:T(8,128)S(1)} %collective-permute-done.28.rest_3_), channel_id=1, source_target_pairs={{0,2},{2,0},{4,6},{6,4},{8,10},{10,8},{12,14},{14,12},{16,18},{18,... | collective-permute-start | bytes 3145736 | tf_op jit(solution)/shard_map/ppermute | solution.py:184
  (3 other events, 15.0 us)

commit v2 on v0

v2 whole, which is shorter than its diff:
```python
import functools

import jax
import jax.numpy as jnp
from jax import lax
from jax.experimental import pallas as pl
from jax.experimental.pallas import tpu as pltpu
from jax.sharding import PartitionSpec as P

CHAINS = 2
EARLY = 3
GATES = {3: ((1, ("late", 0)),), 4: ((0, ("late", 1)), (1, ("step", 1)))}
COST = 12
VMEM_LIMIT = 34 * 1024 * 1024


def split(x):
    high = x.astype(jnp.bfloat16)
    return high, (x - high.astype(jnp.float32)).astype(jnp.bfloat16)


def step_kernel(section, steps, who, first, chain, tile, names, info, *refs):
    at = dict(zip(names, refs))
    kernels = [at["own"], at.get("other")]
    blocks = [ref for name, ref in zip(names, refs) if name == "block"]
    x_high, x_low, tiles, t_sem = refs[len(names) :]
    at["token"][...] = jnp.zeros_like(at["token"])
    final = chain is not None
    actions, rows, _ = at["own"].shape
    depth, chain_width = blocks[0].shape
    width = x_high.shape[1]
    per_step = width // chain_width
    count = len(steps)
    tile_count = rows // tile
    lanes = pl.ds(chain * width if final else 0, width)

    def copies(t, slot, source):
        here = pl.ds(pl.multiple_of(t * tile, tile), tile)
        return [
            pltpu.make_async_copy(
                source.at[:, here, pl.ds(pl.multiple_of(info[1 + step] * depth, depth), depth)],
                tiles.at[slot, :, :, pl.ds(i * depth, depth)],
                t_sem.at[slot, i],
            )
            for i, step in enumerate(steps)
        ]

    def fetch(t, slot):
        def start(source):
            for copy in copies(t, slot, source):
                copy.start()

        if who == "own" or who == "other":
            start(kernels[who == "other"])
        else:
            pl.when(info[0] == section)(lambda: start(kernels[0]))
            pl.when(info[0] != section)(lambda: start(kernels[1]))

    def work():
        fetch(0, 0)
        for j, block in enumerate(blocks):
            here = (
                pl.ds(j // per_step * depth, depth),
                pl.ds(j % per_step * chain_width, chain_width),
            )
            x_high[here], x_low[here] = split(block[...])

        @pl.loop(0, tile_count)
        def _(t):
            slot = lax.rem(t, 2)
            here = pl.ds(pl.multiple_of(t * tile, tile), tile)

            @pl.when(t + 1 < tile_count)
            def _():
                fetch(t + 1, 1 - slot)

            for copy in copies(t, slot, kernels[0]):
                copy.wait()
            high, low = split(tiles[slot].reshape(actions * tile, count * depth))
            dot = functools.partial(jnp.dot, preferred_element_type=jnp.float32)
            summed = dot(high, x_high[...]) + (dot(high, x_low[...]) + dot(low, x_high[...]))
            summed = summed.reshape(actions, tile, width)
            if not first:
                summed = summed + at["total"][:, here, lanes]
            if final:
                gains = at["gains"][here, :]
                best = None
                for a in range(actions):
                    value = summed[a] + gains[:, a : a + 1] - at["charge"][a : a + 1, :]
                    best = value if best is None else jnp.maximum(best, value)
                at["values"][here, :] = best
            else:
                at["sum"][:, here, :] = summed

    if who == "all":
        work()
    else:
        pl.when((info[0] == section) if who == "own" else (info[0] != section))(work)


def step(info, section, steps, who, own, other, blocks, total, first, held, chain=None, gains=None, charge=None):
    final = chain is not None
    actions, rows, _ = own.shape
    depth, chain_width = blocks[0].shape
    width = chain_width * len(blocks) // len(steps)
    tile = min(rows, 128)
    hbm = pl.BlockSpec(memory_space=pl.ANY)
    vmem = pl.BlockSpec(memory_space=pltpu.VMEM)
    named = [("own", own, hbm)]
    if other is not None:
        named.append(("other", other, hbm))
    named += [("block", block, vmem) for block in blocks]
    named += [("held", token, vmem) for token in held]
    if final:
        named += [("gains", gains, vmem), ("charge", charge, vmem)]
    aliases = {}
    if total is not None:
        if not final:
            aliases = {1 + len(named): 0}
        named.append(("total", total, vmem))
    if final:
        out = jax.ShapeDtypeStruct((rows, width), jnp.float32)
    else:
        out = jax.ShapeDtypeStruct((actions, rows, width), jnp.float32)
    names = [name for name, _, _ in named] + ["values" if final else "sum", "token"]
    return pl.pallas_call(
        functools.partial(step_kernel, section, steps, who, first, chain, tile, names),
        out_shape=(out, jax.ShapeDtypeStruct((8, 128), jnp.float32)),
        in_specs=[pl.BlockSpec(memory_space=pltpu.SMEM)] + [spec for _, _, spec in named],
        out_specs=(vmem, vmem),
        scratch_shapes=[
            pltpu.VMEM((len(steps) * depth, width), jnp.bfloat16),
            pltpu.VMEM((len(steps) * depth, width), jnp.bfloat16),
            pltpu.VMEM((2, actions, tile, len(steps) * depth), jnp.float32),
            pltpu.SemaphoreType.DMA((2, len(steps))),
        ],
        input_output_aliases=aliases,
        compiler_params=pltpu.CompilerParams(vmem_limit_bytes=VMEM_LIMIT),
        cost_estimate=pl.CostEstimate(
            flops=COST * actions * rows * len(steps) * depth * width,
            bytes_accessed=4 * actions * rows * len(steps) * depth,
            transcendentals=0,
        ),
        name="step",
    )(info, *[value for _, value, _ in named])


def assemble(info, mine, theirs):
    (rows, width), count = mine[0][0].shape, len(mine[0])
    refs = [*mine[0], *mine[1], *theirs[0], *theirs[1]]

    def body(info, *rest):
        ins, out, sem = rest[: 4 * count], rest[-2], rest[-1]

        def copies(core):
            here = ins[core * count : (core + 1) * count]
            there = ins[(2 + core) * count : (3 + core) * count]
            columns = (here + there) if core == 0 else (there + here)
            return [
                pltpu.make_async_copy(ref, out.at[0, :, pl.ds(j * width, width)], sem.at[j])
                for j, ref in enumerate(columns)
            ]

        for core in range(2):

            @pl.when(info[0] == core)
            def _():
                for copy in copies(core):
                    copy.start()
                for copy in copies(core):
                    copy.wait()

    return pl.pallas_call(
        body,
        out_shape=jax.ShapeDtypeStruct((1, rows, 2 * count * width), jnp.float32),
        in_specs=[pl.BlockSpec(memory_space=pltpu.SMEM)] + [pl.BlockSpec(memory_space=pltpu.VMEM)] * len(refs),
        out_specs=pl.BlockSpec(memory_space=pl.ANY),
        scratch_shapes=[pltpu.SemaphoreType.DMA((2 * count,))],
        name="assemble",
    )(info, *refs)


def shards(transitions, gain, cost, price_class, terminal):
    core = lax.axis_index("section")
    row_count = lax.axis_size("rows")
    minor = 2 if row_count == 8 else 1
    major = row_count // minor

    def row_at(place):
        if minor == 1:
            return place
        down = place // major
        return (down * (2 * major - 1) + place * (1 - 2 * down)) * minor + down

    ring = [row_at(i) for i in range(row_count)]
    after = {ring[i]: ring[(i + 1) % row_count] for i in range(row_count)}
    before = {b: a for a, b in after.items()}
    onward = [(r * 2 + 1, after[r] * 2 + 1) for r in range(row_count)]
    onward += [(r * 2, before[r] * 2) for r in range(row_count)]
    swap = [(r * 2 + s, r * 2 + 1 - s) for r in range(row_count) for s in range(2)]

    def send(value, pairs):
        return lax.ppermute(value, ("rows", "section"), pairs)

    own = transitions[0]
    scenarios = terminal.shape[1]
    width = scenarios // 2 // CHAINS
    small = jnp.concatenate([gain[0], cost[0]], axis=1)
    small_other = send(small, swap)
    other = send(lax.optimization_barrier((own, small_other))[0], swap)
    chains = [
        lax.dynamic_slice_in_dim(terminal, core * (scenarios // 2) + i * width, width, 1) for i in range(CHAINS)
    ]

    me = lax.axis_index("rows")
    down = me % minor
    place = down * (2 * major - 1) + (me // minor) * (1 - 2 * down)
    back = jnp.arange(row_count, dtype=jnp.int32) * (1 - 2 * core)
    info = jnp.concatenate([core[None].astype(jnp.int32), row_at((place + back) % row_count).astype(jnp.int32)])

    my_class = lax.dynamic_slice_in_dim(price_class, core * (scenarios // 2), scenarios // 2, 0)
    levels = jnp.arange(cost.shape[2], dtype=jnp.int32)
    onehot = my_class[None, :] == levels[:, None]

    last = row_count - 1
    early = min(EARLY, last // 2)
    groups = [tuple(range(i, min(i + 2, early))) for i in range(0, early, 2)]
    done = [None, None]
    for section in (1, 0):
        here = jnp.where(core == section, small, small_other)
        gains = here[:, : gain.shape[2]].T
        charge = jnp.sum(jnp.where(onehot[None], here[:, gain.shape[2] :, None], 0.0), axis=1)
        total, arrived, tokens, passed = None, [], {}, []

        def add(steps, who, total, first):
            blocks = [block for s in steps for block in arrived[s]]
            held = [passed.pop() for _ in range(len(passed))]
            return step(info, section, steps, who, own, None if who == "own" else other, blocks, total, first, held)

        for s in range(row_count):
            if s:
                gates = GATES.get(s - early, ()) if section == 1 else ()
                for i, gate in gates:
                    if gate in tokens:
                        chains[i], token = lax.optimization_barrier((chains[i], tokens[gate]))
                        passed.append(token)
                chains = [send(chain, onward) for chain in chains]
            arrived.append(list(chains))
            if s == last:
                break
            if section == 1 and s < early:
                total, _ = add((s,), "own", total, s == 0)
                continue
            if section == 1 and s < early + len(groups):
                total, tokens["late", s - early] = add(groups[s - early], "other", total, s == early)
            total, tokens["step", s - early] = add((s,), "all", total, s == 0)
        chains = [
            step(
                info, section, (last,), "all", own, other, [chain], total, False, [], i,
                gains, charge[:, i * width : (i + 1) * width],
            )[0]
            for i, chain in enumerate(chains)
        ]
        done[section] = chains

    across = [[(r * 2 + 1 - c, r * 2 + c) for r in range(row_count)] for c in range(2)]
    received = [[send(value, across[section]) for value in done[section]] for section in range(2)]
    return assemble(info, done, received)


def solution(mesh):
    return jax.shard_map(
        shards,
        mesh=mesh,
        in_specs=(
            P(("region", "section"), None, "rows", None),
            P(("region", "section"), None, "rows"),
            P(("region", "section"), None, None),
            P("region"),
            P(("region", "rows"), None),
        ),
        out_specs=P(("region", "section"), "rows", None),
        check_vma=False,
    )
```

time: 579 us -> 232 us (0.40)
  waiting for transfers between devices: 369 us -> 51.5 us
  matrix products: 163 us -> 0 us
  Pallas kernels: 0 us -> 113 us
  starting transfers between devices: 6.47 us -> 42.3 us
  between operations: 13.1 us -> 0.57 us
    all_gather x5 -> x0, waiting for transfers between devices: 369 us -> none  [advance(): summed = accumulate(lax.all_gather(current, 'rows', axis=0, tiled=True))]
    dot_general x6 -> x0, matrix products: 163 us -> none  [the longest x5 162 us: accumulate(): jnp.einsum('arn,nc->arc', kernel, panel, precision=lax.Precision.HIGHEST,...]
    pallas_call x0 -> x21, Pallas kernels: none -> 113 us  [the longest x20 110 us: step(): pl.pallas_call(functools.partial(step_kernel, section, steps, who, first,...]
    ppermute x5 -> x34, waiting for transfers between devices: 0.37 us -> 51.5 us  [send(): return lax.ppermute(value, ('rows', 'section'), pairs)]
    ppermute x5 -> x34, starting transfers between devices: 6.46 us -> 42.3 us  [send(): return lax.ppermute(value, ('rows', 'section'), pairs)]
    unnamed x4 -> x30, local copies, waits for them, and re-layouts: 0.68 us -> 15 us
    dynamic_slice x25 -> x2, local copies, waits for them, and re-layouts: 12.8 us -> 2.03 us  [the longest x1 1.27 us: shards(): lax.dynamic_slice_in_dim(terminal, core * (scenarios // 2) + i * width, w...]
  transfers between devices with their start and end apart: 10 -> 34, of which waited for: 10 -> 16; matrix products, arithmetic and copies ran while one was open for 2% -> 3% of each run, Pallas kernels for 0% -> 48%
where the time goes in v2:
time: 232 us; the launch traced here: 230 us
  Pallas kernels  113 us (49%)
  waiting for transfers between devices  51.5 us (22%)
  starting transfers between devices  42.3 us (18%)
  local copies, waits for them, and re-layouts  20 us (9%)
    pallas_call x20, Pallas kernels, step(): pl.pallas_call(functools.partial(step_kernel, section, steps, who, first,...  110 us
    ppermute x34, waiting for transfers between devices, send(): return lax.ppermute(value, ('rows', 'section'), pairs)  51.5 us
    ppermute x34, starting transfers between devices, send(): return lax.ppermute(value, ('rows', 'section'), pairs)  42.3 us
    unnamed x30, local copies, waits for them, and re-layouts  15 us
  transfers between devices with their start and end apart: 34, of which 16 were waited for; matrix products, arithmetic and copies ran while one was open for 3% of the time, Pallas kernels for 48%

profile of v2, /device:TPU:0, one launch (start us, length us, event | category | flops | bytes accessed | tf_op | source)
XLA Modules:
  0.0 230.0 jit_solution(16265415300576896289)
XLA Ops:
  4.9 2.7 %collective-permute-start.2 = (f32[512,256]{1,0:T(8,128)S(1)}, f32[512,256]{1,0:T(8,128)S(1)}, u32[]{:S(2)}, u32[]{:S(2)}) collective-permute-start(f32[512,256]{1,0:T(8,128)S(1)} %get-tuple-element.56.refs_1_.refs_2_), channel_id=1, source_target_pairs={{1,5},{3,1},{5,9},{7,3},{9,13},{11,7},{13,15},{15,11},{0,2},{2,6},... | collective-permute-start | bytes 1572872 | tf_op jit(solution)/shard_map/ppermute | solution.py:203
  10.1 4.8 %collective-permute-done.2.refs_1_.refs_4_ = f32[512,256]{1,0:T(8,128)S(1)} collective-permute-done((f32[512,256]{1,0:T(8,128)S(1)}, f32[512,256]{1,0:T(8,128)S(1)}, u32[]{:S(2)}, u32[]{:S(2)}) %collective-permute-start.2) | collective-permute-done | bytes 524320 | tf_op jit(solution)/shard_map/ppermute | solution.py:203
  20.0 6.0 %collective-permute-done.3.refs_1_.refs_2_ = f32[512,256]{1,0:T(8,128)S(1)} collective-permute-done((f32[512,256]{1,0:T(8,128)S(1)}, f32[512,256]{1,0:T(8,128)S(1)}, u32[]{:S(2)}, u32[]{:S(2)}) %collective-permute-start.3) | collective-permute-done | bytes 524320 | tf_op jit(solution)/shard_map/ppermute | solution.py:203
  32.6 2.6 %collective-permute-done.4.refs_2_ = f32[512,256]{1,0:T(8,128)S(1)} collective-permute-done((f32[512,256]{1,0:T(8,128)S(1)}, f32[512,256]{1,0:T(8,128)S(1)}, u32[]{:S(2)}, u32[]{:S(2)}) %collective-permute-start.4) | collective-permute-done | bytes 524320 | tf_op jit(solution)/shard_map/ppermute | solution.py:203
  42.8 3.7 %collective-permute-done.5.refs_2_ = f32[512,256]{1,0:T(8,128)S(1)} collective-permute-done((f32[512,256]{1,0:T(8,128)S(1)}, f32[512,256]{1,0:T(8,128)S(1)}, u32[]{:S(2)}, u32[]{:S(2)}) %collective-permute-start.5) | collective-permute-done | bytes 524320 | tf_op jit(solution)/shard_map/ppermute | solution.py:203
  54.1 3.7 %collective-permute-done.6.refs_2_ = f32[512,256]{1,0:T(8,128)S(1)} collective-permute-done((f32[512,256]{1,0:T(8,128)S(1)}, f32[512,256]{1,0:T(8,128)S(1)}, u32[]{:S(2)}, u32[]{:S(2)}) %collective-permute-start.6) | collective-permute-done | bytes 524320 | tf_op jit(solution)/shard_map/ppermute | solution.py:203
  65.3 3.7 %collective-permute-done.7.refs_2_ = f32[512,256]{1,0:T(8,128)S(1)} collective-permute-done((f32[512,256]{1,0:T(8,128)S(1)}, f32[512,256]{1,0:T(8,128)S(1)}, u32[]{:S(2)}, u32[]{:S(2)}) %collective-permute-start.7) | collective-permute-done | bytes 524320 | tf_op jit(solution)/shard_map/ppermute | solution.py:203
  70.9 2.2 copy-done.3
  73.1 9.5 %step.23 = (f32[4,512,512]{2,1,0:T(8,128)S(1)}, f32[8,128]{1,0:T(8,128)S(1)}) custom-call(s32[9]{0:T(128)S(1)} %pad_add_fusion.info, f32[4,512,4096]{2,1,0:T(8,128)} %bitcast.12, f32[4,512,4096]{2,1,0:T(8,128)} %collective-permute-done.1.refs_1_, f32[512,256]{1,0:T(8,128)S(1)} %get-tuple-element.56.refs_1_.refs_2_, ...), custom_call_target="tpu_custom_call", output_to_operand_aliasing={{0}: (7, {})} | custom-call | flops 12884901888 | bytes 8388608 | tf_op jit(solution)/shard_map/step/pallas_call | solution.py:126
  88.4 6.2 %step.24 = (f32[4,512,512]{2,1,0:T(8,128)S(1)}, f32[8,128]{1,0:T(8,128)}) custom-call(s32[9]{0:T(128)S(1)} %pad_add_fusion.info, f32[4,512,4096]{2,1,0:T(8,128)} %bitcast.13, f32[4,512,4096]{2,1,0:T(8,128)} %collective-permute-done.1.refs_1_, f32[512,256]{1,0:T(8,128)S(1)} %collective-permute-done.4.refs_2_, ...), custom_call_target="tpu_custom_call", output_to_operand_aliasing={{0}: (5, {})} | custom-call | flops 6442450944 | bytes 4194304 | tf_op jit(solution)/shard_map/step/pallas_call | solution.py:126
  94.7 6.8 %step.25 = (f32[4,512,512]{2,1,0:T(8,128)S(1)}, f32[8,128]{1,0:T(8,128)}) custom-call(s32[9]{0:T(128)S(1)} %pad_add_fusion.info, f32[4,512,4096]{2,1,0:T(8,128)} %bitcast.14, f32[4,512,4096]{2,1,0:T(8,128)} %collective-permute-done.1.refs_1_, f32[512,256]{1,0:T(8,128)S(1)} %collective-permute-done.3.refs_1_.refs_2_, ...), custom_call_target="tpu_custom_call", output_to_operand_aliasing={{0}: (5, {})} | custom-call | flops 6442450944 | bytes 4194304 | tf_op jit(solution)/shard_map/step/pallas_call | solution.py:126
  101.5 6.2 %step.26 = (f32[4,512,512]{2,1,0:T(8,128)S(1)}, f32[8,128]{1,0:T(8,128)}) custom-call(s32[9]{0:T(128)S(1)} %pad_add_fusion.info, f32[4,512,4096]{2,1,0:T(8,128)} %bitcast.15, f32[4,512,4096]{2,1,0:T(8,128)} %collective-permute-done.1.refs_1_, f32[512,256]{1,0:T(8,128)S(1)} %collective-permute-done.5.refs_2_, ...), custom_call_target="tpu_custom_call", output_to_operand_aliasing={{0}: (5, {})} | custom-call | flops 6442450944 | bytes 4194304 | tf_op jit(solution)/shard_map/step/pallas_call | solution.py:126
  107.7 6.2 %step.27 = (f32[4,512,512]{2,1,0:T(8,128)S(1)}, f32[8,128]{1,0:T(8,128)}) custom-call(s32[9]{0:T(128)S(1)} %pad_add_fusion.info, f32[4,512,4096]{2,1,0:T(8,128)} %bitcast.16, f32[4,512,4096]{2,1,0:T(8,128)} %collective-permute-done.1.refs_1_, f32[512,256]{1,0:T(8,128)S(1)} %collective-permute-done.6.refs_2_, ...), custom_call_target="tpu_custom_call", output_to_operand_aliasing={{0}: (5, {})} | custom-call | flops 6442450944 | bytes 4194304 | tf_op jit(solution)/shard_map/step/pallas_call | solution.py:126
  115.6 6.2 %step.28 = (f32[4,512,512]{2,1,0:T(8,128)S(1)}, f32[8,128]{1,0:T(8,128)}) custom-call(s32[9]{0:T(128)S(1)} %pad_add_fusion.info, f32[4,512,4096]{2,1,0:T(8,128)} %bitcast.17, f32[4,512,4096]{2,1,0:T(8,128)} %collective-permute-done.1.refs_1_, f32[512,256]{1,0:T(8,128)S(1)} %collective-permute-done.7.refs_2_, ...), custom_call_target="tpu_custom_call", output_to_operand_aliasing={{0}: (6, {})} | custom-call | flops 6442450944 | bytes 4194304 | tf_op jit(solution)/shard_map/step/pallas_call | solution.py:126
  121.8 5.7 %step.29 = (f32[512,256]{1,0:T(8,128)}, f32[8,128]{1,0:T(8,128)}) custom-call(s32[9]{0:T(128)S(1)} %pad_add_fusion.info, f32[4,512,4096]{2,1,0:T(8,128)} %bitcast.18, f32[4,512,4096]{2,1,0:T(8,128)} %collective-permute-done.1.refs_1_, f32[512,256]{1,0:T(8,128)S(1)} %collective-permute-done.8.refs_2_, f32[512,4]{1,0:T(8,128)S(1)} %slice_bitcast_fusion.1.refs_3_, ...), custom_call_target="tpu_custom_call" | custom-call | flops 3221225472 | bytes 4194304 | tf_op jit(solution)/shard_map/step/pallas_call | solution.py:126
  131.3 5.7 %step.30 = (f32[512,256]{1,0:T(8,128)}, f32[8,128]{1,0:T(8,128)}) custom-call(s32[9]{0:T(128)S(1)} %pad_add_fusion.info, f32[4,512,4096]{2,1,0:T(8,128)} %bitcast.19, f32[4,512,4096]{2,1,0:T(8,128)} %collective-permute-done.1.refs_1_, f32[512,256]{1,0:T(8,128)S(1)} %collective-permute-done.22.refs_2_, f32[512,4]{1,0:T(8,128)S(1)} %slice_bitcast_fusion.1.refs_3_, ...), custom_call_target="tpu_custom_call" | custom-call | flops 3221225472 | bytes 4194304 | tf_op jit(solution)/shard_map/step/pallas_call | solution.py:126
  140.1 6.8 %step.31 = (f32[4,512,512]{2,1,0:T(8,128)S(1)}, f32[8,128]{1,0:T(8,128)}) custom-call(s32[9]{0:T(128)S(1)} %pad_add_fusion.info, f32[4,512,4096]{2,1,0:T(8,128)} %bitcast.20, f32[4,512,4096]{2,1,0:T(8,128)} %collective-permute-done.1.refs_1_, f32[512,256]{1,0:T(8,128)} %get-tuple-element.42.refs_2_.rest_2_, f32[512,256]{1,0:T(8,128)} %get-tuple-element.43.refs_3_.rest_3_), custom_call_target="tpu_custom_call" | custom-call | flops 6442450944 | bytes 4194304 | tf_op jit(solution)/shard_map/step/pallas_call | solution.py:126
  147.4 4.7 %collective-permute-done.16.refs_2_ = f32[512,256]{1,0:T(8,128)S(1)} collective-permute-done((f32[512,256]{1,0:T(8,128)S(1)}, f32[512,256]{1,0:T(8,128)S(1)}, u32[]{:S(2)}, u32[]{:S(2)}) %collective-permute-start.16) | collective-permute-done | bytes 524320 | tf_op jit(solution)/shard_map/ppermute | solution.py:203
  152.6 6.2 %step.32 = (f32[4,512,512]{2,1,0:T(8,128)S(1)}, f32[8,128]{1,0:T(8,128)}) custom-call(s32[9]{0:T(128)S(1)} %pad_add_fusion.info, f32[4,512,4096]{2,1,0:T(8,128)} %bitcast.21, f32[4,512,4096]{2,1,0:T(8,128)} %collective-permute-done.1.refs_1_, f32[512,256]{1,0:T(8,128)S(1)} %collective-permute-done.15.refs_2_, ...), custom_call_target="tpu_custom_call", output_to_operand_aliasing={{0}: (5, {})} | custom-call | flops 6442450944 | bytes 4194304 | tf_op jit(solution)/shard_map/step/pallas_call | solution.py:126
  159.3 4.0 %collective-permute-done.17.refs_2_ = f32[512,256]{1,0:T(8,128)S(1)} collective-permute-done((f32[512,256]{1,0:T(8,128)S(1)}, f32[512,256]{1,0:T(8,128)S(1)}, u32[]{:S(2)}, u32[]{:S(2)}) %collective-permute-start.17) | collective-permute-done | bytes 524320 | tf_op jit(solution)/shard_map/ppermute | solution.py:203
  163.8 6.2 %step.33 = (f32[4,512,512]{2,1,0:T(8,128)S(1)}, f32[8,128]{1,0:T(8,128)}) custom-call(s32[9]{0:T(128)S(1)} %pad_add_fusion.info, f32[4,512,4096]{2,1,0:T(8,128)} %bitcast.22, f32[4,512,4096]{2,1,0:T(8,128)} %collective-permute-done.1.refs_1_, f32[512,256]{1,0:T(8,128)S(1)} %collective-permute-done.16.refs_2_, ...), custom_call_target="tpu_custom_call", output_to_operand_aliasing={{0}: (5, {})} | custom-call | flops 6442450944 | bytes 4194304 | tf_op jit(solution)/shard_map/step/pallas_call | solution.py:126
  170.6 4.0 %collective-permute-done.18.refs_2_ = f32[512,256]{1,0:T(8,128)S(1)} collective-permute-done((f32[512,256]{1,0:T(8,128)S(1)}, f32[512,256]{1,0:T(8,128)S(1)}, u32[]{:S(2)}, u32[]{:S(2)}) %collective-permute-start.18) | collective-permute-done | bytes 524320 | tf_op jit(solution)/shard_map/ppermute | solution.py:203
  175.1 6.2 %step.34 = (f32[4,512,512]{2,1,0:T(8,128)S(1)}, f32[8,128]{1,0:T(8,128)}) custom-call(s32[9]{0:T(128)S(1)} %pad_add_fusion.info, f32[4,512,4096]{2,1,0:T(8,128)} %bitcast.23, f32[4,512,4096]{2,1,0:T(8,128)} %collective-permute-done.1.refs_1_, f32[512,256]{1,0:T(8,128)S(1)} %collective-permute-done.17.refs_2_, ...), custom_call_target="tpu_custom_call", output_to_operand_aliasing={{0}: (5, {})} | custom-call | flops 6442450944 | bytes 4194304 | tf_op jit(solution)/shard_map/step/pallas_call | solution.py:126
  181.8 4.0 %collective-permute-done.19.refs_2_ = f32[512,256]{1,0:T(8,128)S(1)} collective-permute-done((f32[512,256]{1,0:T(8,128)S(1)}, f32[512,256]{1,0:T(8,128)S(1)}, u32[]{:S(2)}, u32[]{:S(2)}) %collective-permute-start.19) | collective-permute-done | bytes 524320 | tf_op jit(solution)/shard_map/ppermute | solution.py:203
  186.3 6.2 %step.35 = (f32[4,512,512]{2,1,0:T(8,128)S(1)}, f32[8,128]{1,0:T(8,128)}) custom-call(s32[9]{0:T(128)S(1)} %pad_add_fusion.info, f32[4,512,4096]{2,1,0:T(8,128)} %bitcast.24, f32[4,512,4096]{2,1,0:T(8,128)} %collective-permute-done.1.refs_1_, f32[512,256]{1,0:T(8,128)S(1)} %collective-permute-done.18.refs_2_, ...), custom_call_target="tpu_custom_call", output_to_operand_aliasing={{0}: (5, {})} | custom-call | flops 6442450944 | bytes 4194304 | tf_op jit(solution)/shard_map/step/pallas_call | solution.py:126
  193.0 4.0 %collective-permute-done.20.refs_2_ = f32[512,256]{1,0:T(8,128)S(1)} collective-permute-done((f32[512,256]{1,0:T(8,128)S(1)}, f32[512,256]{1,0:T(8,128)S(1)}, u32[]{:S(2)}, u32[]{:S(2)}) %collective-permute-start.20) | collective-permute-done | bytes 524320 | tf_op jit(solution)/shard_map/ppermute | solution.py:203
  197.5 6.2 %step.36 = (f32[4,512,512]{2,1,0:T(8,128)S(1)}, f32[8,128]{1,0:T(8,128)}) custom-call(s32[9]{0:T(128)S(1)} %pad_add_fusion.info, f32[4,512,4096]{2,1,0:T(8,128)} %bitcast.25, f32[4,512,4096]{2,1,0:T(8,128)} %collective-permute-done.1.refs_1_, f32[512,256]{1,0:T(8,128)S(1)} %collective-permute-done.19.refs_2_, ...), custom_call_target="tpu_custom_call", output_to_operand_aliasing={{0}: (5, {})} | custom-call | flops 6442450944 | bytes 4194304 | tf_op jit(solution)/shard_map/step/pallas_call | solution.py:126
  204.3 6.2 %step.37 = (f32[4,512,512]{2,1,0:T(8,128)S(1)}, f32[8,128]{1,0:T(8,128)}) custom-call(s32[9]{0:T(128)S(1)} %pad_add_fusion.info, f32[4,512,4096]{2,1,0:T(8,128)} %bitcast.26, f32[4,512,4096]{2,1,0:T(8,128)} %collective-permute-done.1.refs_1_, f32[512,256]{1,0:T(8,128)S(1)} %collective-permute-done.20.refs_2_, ...), custom_call_target="tpu_custom_call", output_to_operand_aliasing={{0}: (5, {})} | custom-call | flops 6442450944 | bytes 4194304 | tf_op jit(solution)/shard_map/step/pallas_call | solution.py:126
  210.5 4.9 %step.38 = (f32[512,256]{1,0:T(8,128)S(1)}, f32[8,128]{1,0:T(8,128)}) custom-call(s32[9]{0:T(128)S(1)} %pad_add_fusion.info, f32[4,512,4096]{2,1,0:T(8,128)} %bitcast.27, f32[4,512,4096]{2,1,0:T(8,128)} %collective-permute-done.1.refs_1_, f32[512,256]{1,0:T(8,128)S(1)} %collective-permute-done.21.refs_2_, f32[512,4]{1,0:T(8,128)S(1)} %slice_bitcast_fusion.refs_3_, ...), custom_call_target="tpu_custom_call" | custom-call | flops 3221225472 | bytes 4194304 | tf_op jit(solution)/shard_map/step/pallas_call | solution.py:126
  216.8 4.9 %step.39 = (f32[512,256]{1,0:T(8,128)S(1)}, f32[8,128]{1,0:T(8,128)}) custom-call(s32[9]{0:T(128)S(1)} %pad_add_fusion.info, f32[4,512,4096]{2,1,0:T(8,128)} %bitcast.28, f32[4,512,4096]{2,1,0:T(8,128)} %collective-permute-done.1.refs_1_, f32[512,256]{1,0:T(8,128)S(1)} %collective-permute-done.29.refs_2_, f32[512,4]{1,0:T(8,128)S(1)} %slice_bitcast_fusion.refs_3_, ...), custom_call_target="tpu_custom_call" | custom-call | flops 3221225472 | bytes 4194304 | tf_op jit(solution)/shard_map/step/pallas_call | solution.py:126
  223.0 2.5 %collective-permute-done.31.rest_5_ = f32[512,256]{1,0:T(8,128)S(1)} collective-permute-done((f32[512,256]{1,0:T(8,128)S(1)}, f32[512,256]{1,0:T(8,128)S(1)}, u32[]{:S(2)}, u32[]{:S(2)}) %collective-permute-start.31) | collective-permute-done | bytes 524320 | tf_op jit(solution)/shard_map/ppermute | solution.py:203
  226.4 3.5 %assemble.1 = f32[1,512,1024]{2,1,0:T(8,128)} custom-call(s32[9]{0:T(128)} %copy-done.8, f32[512,256]{1,0:T(8,128)} %copy-done.6, f32[512,256]{1,0:T(8,128)} %copy-done.7, f32[512,256]{1,0:T(8,128)} %get-tuple-element.42.refs_2_.rest_2_, f32[512,256]{1,0:T(8,128)} %get-tuple-element.43.refs_3_.rest_3_, f32[512,256]{1,0:T(8,128)} %copy-done.10, ...), custom_call_target="tpu_custom_call" | custom-call | tf_op jit(solution)/shard_map/assemble/pallas_call | solution.py:173
  (104 shorter events, 66.7 us)
Async XLA Ops:
  3.3 67.7 %collective-permute-start.1 = (f32[4,512,4096]{2,1,0:T(8,128)}, f32[4,512,4096]{2,1,0:T(8,128)}, u32[]{:S(2)}, u32[]{:S(2)}) collective-permute-start(f32[4,512,4096]{2,1,0:T(8,128)} %bitcast.8), channel_id=1, source_target_pairs={{0,1},{1,0},{2,3},{3,2},{4,5},{5,4},{6,7},{7,6},{8,9},{9,8},{10,11... | collective-permute-start | bytes 100663304 | tf_op jit(solution)/shard_map/ppermute | solution.py:203
  4.9 9.9 %collective-permute-start.2 = (f32[512,256]{1,0:T(8,128)S(1)}, f32[512,256]{1,0:T(8,128)S(1)}, u32[]{:S(2)}, u32[]{:S(2)}) collective-permute-start(f32[512,256]{1,0:T(8,128)S(1)} %get-tuple-element.56.refs_1_.refs_2_), channel_id=1, source_target_pairs={{1,5},{3,1},{5,9},{7,3},{9,13},{11,7},{13,15},{15,11},{0,2},{2,6},... | collective-permute-start | bytes 1572872 | tf_op jit(solution)/shard_map/ppermute | solution.py:203
  7.6 23.4 %collective-permute-start.9 = (f32[512,256]{1,0:T(8,128)S(1)}, f32[512,256]{1,0:T(8,128)S(1)}, u32[]{:S(2)}, u32[]{:S(2)}) collective-permute-start(f32[512,256]{1,0:T(8,128)S(1)} %get-tuple-element.55.refs_2_.refs_3_), channel_id=1, source_target_pairs={{1,5},{3,1},{5,9},{7,3},{9,13},{11,7},{13,15},{15,11},{0,2},{2,6},... | collective-permute-start | bytes 1572872 | tf_op jit(solution)/shard_map/ppermute | solution.py:203
  14.8 11.2 %collective-permute-start.3 = (f32[512,256]{1,0:T(8,128)S(1)}, f32[512,256]{1,0:T(8,128)S(1)}, u32[]{:S(2)}, u32[]{:S(2)}) collective-permute-start(f32[512,256]{1,0:T(8,128)S(1)} %collective-permute-done.2.refs_1_.refs_4_), channel_id=1, source_target_pairs={{1,5},{3,1},{5,9},{7,3},{9,13},{11,7},{13,15},{15,11},{0,2},{2,6},... | collective-permute-start | bytes 1572872 | tf_op jit(solution)/shard_map/ppermute | solution.py:203
  26.1 9.2 %collective-permute-start.4 = (f32[512,256]{1,0:T(8,128)S(1)}, f32[512,256]{1,0:T(8,128)S(1)}, u32[]{:S(2)}, u32[]{:S(2)}) collective-permute-start(f32[512,256]{1,0:T(8,128)S(1)} %collective-permute-done.3.refs_1_.refs_2_), channel_id=1, source_target_pairs={{1,5},{3,1},{5,9},{7,3},{9,13},{11,7},{13,15},{15,11},{0,2},{2,6},... | collective-permute-start | bytes 1572872 | tf_op jit(solution)/shard_map/ppermute | solution.py:203
  31.1 9.8 %collective-permute-start.10 = (f32[512,256]{1,0:T(8,128)S(1)}, f32[512,256]{1,0:T(8,128)S(1)}, u32[]{:S(2)}, u32[]{:S(2)}) collective-permute-start(f32[512,256]{1,0:T(8,128)S(1)} %collective-permute-done.9.refs_2_.refs_5_), channel_id=1, source_target_pairs={{1,5},{3,1},{5,9},{7,3},{9,13},{11,7},{13,15},{15,11},{0,2},{2,6},... | collective-permute-start | bytes 1572872 | tf_op jit(solution)/shard_map/ppermute | solution.py:203
  35.3 11.2 %collective-permute-start.5 = (f32[512,256]{1,0:T(8,128)S(1)}, f32[512,256]{1,0:T(8,128)S(1)}, u32[]{:S(2)}, u32[]{:S(2)}) collective-permute-start(f32[512,256]{1,0:T(8,128)S(1)} %collective-permute-done.4.refs_2_), channel_id=1, source_target_pairs={{1,5},{3,1},{5,9},{7,3},{9,13},{11,7},{13,15},{15,11},{0,2},{2,6},... | collective-permute-start | bytes 1572872 | tf_op jit(solution)/shard_map/ppermute | solution.py:203
  40.9 11.2 %collective-permute-start.11 = (f32[512,256]{1,0:T(8,128)S(1)}, f32[512,256]{1,0:T(8,128)S(1)}, u32[]{:S(2)}, u32[]{:S(2)}) collective-permute-start(f32[512,256]{1,0:T(8,128)S(1)} %collective-permute-done.10.refs_2_.refs_3_), channel_id=1, source_target_pairs={{1,5},{3,1},{5,9},{7,3},{9,13},{11,7},{13,15},{15,11},{0,2},{2,6},... | collective-permute-start | bytes 1572872 | tf_op jit(solution)/shard_map/ppermute | solution.py:203
  46.5 11.2 %collective-permute-start.6 = (f32[512,256]{1,0:T(8,128)S(1)}, f32[512,256]{1,0:T(8,128)S(1)}, u32[]{:S(2)}, u32[]{:S(2)}) collective-permute-start(f32[512,256]{1,0:T(8,128)S(1)} %collective-permute-done.5.refs_2_), channel_id=1, source_target_pairs={{1,5},{3,1},{5,9},{7,3},{9,13},{11,7},{13,15},{15,11},{0,2},{2,6},... | collective-permute-start | bytes 1572872 | tf_op jit(solution)/shard_map/ppermute | solution.py:203
  52.1 11.2 %collective-permute-start.12 = (f32[512,256]{1,0:T(8,128)S(1)}, f32[512,256]{1,0:T(8,128)S(1)}, u32[]{:S(2)}, u32[]{:S(2)}) collective-permute-start(f32[512,256]{1,0:T(8,128)S(1)} %collective-permute-done.11.refs_3_), channel_id=1, source_target_pairs={{1,5},{3,1},{5,9},{7,3},{9,13},{11,7},{13,15},{15,11},{0,2},{2,6},... | collective-permute-start | bytes 1572872 | tf_op jit(solution)/shard_map/ppermute | solution.py:203
  57.7 11.2 %collective-permute-start.7 = (f32[512,256]{1,0:T(8,128)S(1)}, f32[512,256]{1,0:T(8,128)S(1)}, u32[]{:S(2)}, u32[]{:S(2)}) collective-permute-start(f32[512,256]{1,0:T(8,128)S(1)} %collective-permute-done.6.refs_2_), channel_id=1, source_target_pairs={{1,5},{3,1},{5,9},{7,3},{9,13},{11,7},{13,15},{15,11},{0,2},{2,6},... | collective-permute-start | bytes 1572872 | tf_op jit(solution)/shard_map/ppermute | solution.py:203
  63.3 21.3 %collective-permute-start.13 = (f32[512,256]{1,0:T(8,128)S(1)}, f32[512,256]{1,0:T(8,128)S(1)}, u32[]{:S(2)}, u32[]{:S(2)}) collective-permute-start(f32[512,256]{1,0:T(8,128)S(1)} %collective-permute-done.12.refs_3_), channel_id=1, source_target_pairs={{1,5},{3,1},{5,9},{7,3},{9,13},{11,7},{13,15},{15,11},{0,2},{2,6},... | collective-permute-start | bytes 1572872 | tf_op jit(solution)/shard_map/ppermute | solution.py:203
  69.0 52.9 %collective-permute-start.8 = (f32[512,256]{1,0:T(8,128)S(1)}, f32[512,256]{1,0:T(8,128)S(1)}, u32[]{:S(2)}, u32[]{:S(2)}) collective-permute-start(f32[512,256]{1,0:T(8,128)S(1)} %collective-permute-done.7.refs_2_), channel_id=1, source_target_pairs={{1,5},{3,1},{5,9},{7,3},{9,13},{11,7},{13,15},{15,11},{0,2},{2,6},... | collective-permute-start | bytes 1572872 | tf_op jit(solution)/shard_map/ppermute | solution.py:203
  84.7 29.3 %collective-permute-start.14 = (f32[512,256]{1,0:T(8,128)S(1)}, f32[512,256]{1,0:T(8,128)S(1)}, u32[]{:S(2)}, u32[]{:S(2)}) collective-permute-start(f32[512,256]{1,0:T(8,128)S(1)} %collective-permute-done.13.refs_3_), channel_id=1, source_target_pairs={{1,5},{3,1},{5,9},{7,3},{9,13},{11,7},{13,15},{15,11},{0,2},{2,6},... | collective-permute-start | bytes 1572872 | tf_op jit(solution)/shard_map/ppermute | solution.py:203
  114.0 17.4 %collective-permute-start.22 = (f32[512,256]{1,0:T(8,128)S(1)}, f32[512,256]{1,0:T(8,128)S(1)}, u32[]{:S(2)}, u32[]{:S(2)}) collective-permute-start(f32[512,256]{1,0:T(8,128)S(1)} %collective-permute-done.14.refs_3_), channel_id=1, source_target_pairs={{1,5},{3,1},{5,9},{7,3},{9,13},{11,7},{13,15},{15,11},{0,2},{2,6},... | collective-permute-start | bytes 1572872 | tf_op jit(solution)/shard_map/ppermute | solution.py:203
  127.6 12.1 %collective-permute-start.15 = (f32[512,256]{1,0:T(8,128)}, f32[512,256]{1,0:T(8,128)S(1)}, u32[]{:S(2)}, u32[]{:S(2)}) collective-permute-start(f32[512,256]{1,0:T(8,128)} %get-tuple-element.42.refs_2_.rest_2_), channel_id=1, source_target_pairs={{1,5},{3,1},{5,9},{7,3},{9,13},{11,7},{13,15},{15,11},{0,2},{2,6},... | collective-permute-start | bytes 1572872 | tf_op jit(solution)/shard_map/ppermute | solution.py:203
  129.3 93.7 %collective-permute-start.32 = (f32[512,256]{1,0:T(8,128)}, f32[512,256]{1,0:T(8,128)}, u32[]{:S(2)}, u32[]{:S(2)}) collective-permute-start(f32[512,256]{1,0:T(8,128)} %get-tuple-element.42.refs_2_.rest_2_), channel_id=1, source_target_pairs={{0,1},{2,3},{4,5},{6,7},{8,9},{10,11},{12,13},{14,15},{16,17},{18,... | collective-permute-start | bytes 1572872 | tf_op jit(solution)/shard_map/ppermute | solution.py:203
  137.1 9.8 %collective-permute-start.23 = (f32[512,256]{1,0:T(8,128)}, f32[512,256]{1,0:T(8,128)S(1)}, u32[]{:S(2)}, u32[]{:S(2)}) collective-permute-start(f32[512,256]{1,0:T(8,128)} %get-tuple-element.43.refs_3_.rest_3_), channel_id=1, source_target_pairs={{1,5},{3,1},{5,9},{7,3},{9,13},{11,7},{13,15},{15,11},{0,2},{2,6},... | collective-permute-start | bytes 1572872 | tf_op jit(solution)/shard_map/ppermute | solution.py:203
  137.6 85.4 %collective-permute-start.33 = (f32[512,256]{1,0:T(8,128)}, f32[512,256]{1,0:T(8,128)}, u32[]{:S(2)}, u32[]{:S(2)}) collective-permute-start(f32[512,256]{1,0:T(8,128)} %get-tuple-element.43.refs_3_.rest_3_), channel_id=1, source_target_pairs={{0,1},{2,3},{4,5},{6,7},{8,9},{10,11},{12,13},{14,15},{16,17},{18,... | collective-permute-start | bytes 1572872 | tf_op jit(solution)/shard_map/ppermute | solution.py:203
  139.7 12.5 %collective-permute-start.16 = (f32[512,256]{1,0:T(8,128)S(1)}, f32[512,256]{1,0:T(8,128)S(1)}, u32[]{:S(2)}, u32[]{:S(2)}) collective-permute-start(f32[512,256]{1,0:T(8,128)S(1)} %collective-permute-done.15.refs_2_), channel_id=1, source_target_pairs={{1,5},{3,1},{5,9},{7,3},{9,13},{11,7},{13,15},{15,11},{0,2},{2,6},... | collective-permute-start | bytes 1572872 | tf_op jit(solution)/shard_map/ppermute | solution.py:203
  146.9 11.9 %collective-permute-start.24 = (f32[512,256]{1,0:T(8,128)S(1)}, f32[512,256]{1,0:T(8,128)S(1)}, u32[]{:S(2)}, u32[]{:S(2)}) collective-permute-start(f32[512,256]{1,0:T(8,128)S(1)} %collective-permute-done.23.refs_3_), channel_id=1, source_target_pairs={{1,5},{3,1},{5,9},{7,3},{9,13},{11,7},{13,15},{15,11},{0,2},{2,6},... | collective-permute-start | bytes 1572872 | tf_op jit(solution)/shard_map/ppermute | solution.py:203
  152.1 11.2 %collective-permute-start.17 = (f32[512,256]{1,0:T(8,128)S(1)}, f32[512,256]{1,0:T(8,128)S(1)}, u32[]{:S(2)}, u32[]{:S(2)}) collective-permute-start(f32[512,256]{1,0:T(8,128)S(1)} %collective-permute-done.16.refs_2_), channel_id=1, source_target_pairs={{1,5},{3,1},{5,9},{7,3},{9,13},{11,7},{13,15},{15,11},{0,2},{2,6},... | collective-permute-start | bytes 1572872 | tf_op jit(solution)/shard_map/ppermute | solution.py:203
  158.8 11.2 %collective-permute-start.25 = (f32[512,256]{1,0:T(8,128)S(1)}, f32[512,256]{1,0:T(8,128)S(1)}, u32[]{:S(2)}, u32[]{:S(2)}) collective-permute-start(f32[512,256]{1,0:T(8,128)S(1)} %collective-permute-done.24.refs_3_), channel_id=1, source_target_pairs={{1,5},{3,1},{5,9},{7,3},{9,13},{11,7},{13,15},{15,11},{0,2},{2,6},... | collective-permute-start | bytes 1572872 | tf_op jit(solution)/shard_map/ppermute | solution.py:203
  163.4 11.2 %collective-permute-start.18 = (f32[512,256]{1,0:T(8,128)S(1)}, f32[512,256]{1,0:T(8,128)S(1)}, u32[]{:S(2)}, u32[]{:S(2)}) collective-permute-start(f32[512,256]{1,0:T(8,128)S(1)} %collective-permute-done.17.refs_2_), channel_id=1, source_target_pairs={{1,5},{3,1},{5,9},{7,3},{9,13},{11,7},{13,15},{15,11},{0,2},{2,6},... | collective-permute-start | bytes 1572872 | tf_op jit(solution)/shard_map/ppermute | solution.py:203
  170.1 11.2 %collective-permute-start.26 = (f32[512,256]{1,0:T(8,128)S(1)}, f32[512,256]{1,0:T(8,128)S(1)}, u32[]{:S(2)}, u32[]{:S(2)}) collective-permute-start(f32[512,256]{1,0:T(8,128)S(1)} %collective-permute-done.25.refs_3_), channel_id=1, source_target_pairs={{1,5},{3,1},{5,9},{7,3},{9,13},{11,7},{13,15},{15,11},{0,2},{2,6},... | collective-permute-start | bytes 1572872 | tf_op jit(solution)/shard_map/ppermute | solution.py:203
  174.6 11.2 %collective-permute-start.19 = (f32[512,256]{1,0:T(8,128)S(1)}, f32[512,256]{1,0:T(8,128)S(1)}, u32[]{:S(2)}, u32[]{:S(2)}) collective-permute-start(f32[512,256]{1,0:T(8,128)S(1)} %collective-permute-done.18.refs_2_), channel_id=1, source_target_pairs={{1,5},{3,1},{5,9},{7,3},{9,13},{11,7},{13,15},{15,11},{0,2},{2,6},... | collective-permute-start | bytes 1572872 | tf_op jit(solution)/shard_map/ppermute | solution.py:203
  181.3 11.2 %collective-permute-start.27 = (f32[512,256]{1,0:T(8,128)S(1)}, f32[512,256]{1,0:T(8,128)S(1)}, u32[]{:S(2)}, u32[]{:S(2)}) collective-permute-start(f32[512,256]{1,0:T(8,128)S(1)} %collective-permute-done.26.refs_3_), channel_id=1, source_target_pairs={{1,5},{3,1},{5,9},{7,3},{9,13},{11,7},{13,15},{15,11},{0,2},{2,6},... | collective-permute-start | bytes 1572872 | tf_op jit(solution)/shard_map/ppermute | solution.py:203
  185.8 11.2 %collective-permute-start.20 = (f32[512,256]{1,0:T(8,128)S(1)}, f32[512,256]{1,0:T(8,128)S(1)}, u32[]{:S(2)}, u32[]{:S(2)}) collective-permute-start(f32[512,256]{1,0:T(8,128)S(1)} %collective-permute-done.19.refs_2_), channel_id=1, source_target_pairs={{1,5},{3,1},{5,9},{7,3},{9,13},{11,7},{13,15},{15,11},{0,2},{2,6},... | collective-permute-start | bytes 1572872 | tf_op jit(solution)/shard_map/ppermute | solution.py:203
  192.5 11.2 %collective-permute-start.28 = (f32[512,256]{1,0:T(8,128)S(1)}, f32[512,256]{1,0:T(8,128)S(1)}, u32[]{:S(2)}, u32[]{:S(2)}) collective-permute-start(f32[512,256]{1,0:T(8,128)S(1)} %collective-permute-done.27.refs_3_), channel_id=1, source_target_pairs={{1,5},{3,1},{5,9},{7,3},{9,13},{11,7},{13,15},{15,11},{0,2},{2,6},... | collective-permute-start | bytes 1572872 | tf_op jit(solution)/shard_map/ppermute | solution.py:203
  197.1 13.4 %collective-permute-start.21 = (f32[512,256]{1,0:T(8,128)S(1)}, f32[512,256]{1,0:T(8,128)S(1)}, u32[]{:S(2)}, u32[]{:S(2)}) collective-permute-start(f32[512,256]{1,0:T(8,128)S(1)} %collective-permute-done.20.refs_2_), channel_id=1, source_target_pairs={{1,5},{3,1},{5,9},{7,3},{9,13},{11,7},{13,15},{15,11},{0,2},{2,6},... | collective-permute-start | bytes 1572872 | tf_op jit(solution)/shard_map/ppermute | solution.py:203
  203.8 13.0 %collective-permute-start.29 = (f32[512,256]{1,0:T(8,128)S(1)}, f32[512,256]{1,0:T(8,128)S(1)}, u32[]{:S(2)}, u32[]{:S(2)}) collective-permute-start(f32[512,256]{1,0:T(8,128)S(1)} %collective-permute-done.28.refs_3_), channel_id=1, source_target_pairs={{1,5},{3,1},{5,9},{7,3},{9,13},{11,7},{13,15},{15,11},{0,2},{2,6},... | collective-permute-start | bytes 1572872 | tf_op jit(solution)/shard_map/ppermute | solution.py:203
  215.4 7.6 %collective-permute-start.30 = (f32[512,256]{1,0:T(8,128)S(1)}, f32[512,256]{1,0:T(8,128)S(1)}, u32[]{:S(2)}, u32[]{:S(2)}) collective-permute-start(f32[512,256]{1,0:T(8,128)S(1)} %get-tuple-element.51.rest_0_), channel_id=1, source_target_pairs={{1,0},{3,2},{5,4},{7,6},{9,8},{11,10},{13,12},{15,14},{17,16},{19,... | collective-permute-start | bytes 1572872 | tf_op jit(solution)/shard_map/ppermute | solution.py:203
  (17 other events, 265.3 us)

commit v3 on v2

v3 whole, which is shorter than its diff:
```python
import functools

import jax
import jax.numpy as jnp
from jax import lax
from jax.experimental import pallas as pl
from jax.experimental.pallas import tpu as pltpu
from jax.sharding import PartitionSpec as P

CHAINS = 2
EARLY = 3
PAIR = 2
COST = 12
VMEM_LIMIT = 26 * 1024 * 1024


def split(x):
    high = x.astype(jnp.bfloat16)
    return high, (x - high.astype(jnp.float32)).astype(jnp.bfloat16)


def step_kernel(section, steps, who, first, finish, tile, names, info, *refs):
    at = dict(zip(names, refs))
    kernels = [at["own"], at.get("other")]
    blocks = [ref for name, ref in zip(names, refs) if name == "block"]
    x_high, x_low, tiles, t_sem = refs[len(names) :]
    at["token"][...] = jnp.zeros_like(at["token"])
    final = bool(finish)
    half = CHAINS * blocks[0].shape[1]
    actions, rows, _ = at["own"].shape
    depth, chain_width = blocks[0].shape
    width = x_high.shape[1]
    per_step = width // chain_width
    count = len(steps)
    tile_count = rows // tile
    lanes = pl.ds(finish[0] * width if final else 0, width)

    def copies(t, slot, source):
        here = pl.ds(pl.multiple_of(t * tile, tile), tile)
        return [
            pltpu.make_async_copy(
                source.at[:, here, pl.ds(pl.multiple_of(info[1 + step] * depth, depth), depth)],
                tiles.at[slot, :, :, pl.ds(i * depth, depth)],
                t_sem.at[slot, i],
            )
            for i, step in enumerate(steps)
        ]

    def fetch(t, slot):
        def start(source):
            for copy in copies(t, slot, source):
                copy.start()

        if who == "own" or who == "other":
            start(kernels[who == "other"])
        else:
            pl.when(info[0] == section)(lambda: start(kernels[0]))
            pl.when(info[0] != section)(lambda: start(kernels[1]))

    def work():
        fetch(0, 0)
        for j, block in enumerate(blocks):
            here = (
                pl.ds(j // per_step * depth, depth),
                pl.ds(j % per_step * chain_width, chain_width),
            )
            x_high[here], x_low[here] = split(block[...])

        @pl.loop(0, tile_count)
        def _(t):
            slot = lax.rem(t, 2)
            here = pl.ds(pl.multiple_of(t * tile, tile), tile)

            @pl.when(t + 1 < tile_count)
            def _():
                fetch(t + 1, 1 - slot)

            for copy in copies(t, slot, kernels[0]):
                copy.wait()
            high, low = split(tiles[slot].reshape(actions * tile, count * depth))
            dot = functools.partial(jnp.dot, preferred_element_type=jnp.float32)
            summed = dot(high, x_high[...]) + (dot(high, x_low[...]) + dot(low, x_high[...]))
            summed = summed.reshape(actions, tile, width)
            if not first:
                summed = summed + at["total"][:, here, lanes]
            if final:
                mine = info[0] == section
                gains = jnp.where(mine, at["gains", 0][here, :], at["gains", 1][here, :])
                columns = pl.ds(pl.multiple_of(info[0] * half + finish[0] * chain_width, chain_width), width)
                charge = jnp.where(mine, at["charge", 0][:, columns], at["charge", 1][:, columns])
                best = None
                for a in range(actions):
                    value = summed[a] + gains[:, a : a + 1] - charge[a : a + 1, :]
                    best = value if best is None else jnp.maximum(best, value)
                for i, chain in enumerate(finish):
                    at["values", chain][here, :] = best[:, i * chain_width : (i + 1) * chain_width]
            else:
                at["sum"][:, here, :] = summed

    if who == "all":
        work()
    else:
        pl.when((info[0] == section) if who == "own" else (info[0] != section))(work)


def step(info, section, steps, who, own, other, blocks, total, first, held, finish=(), terms=()):
    final = bool(finish)
    actions, rows, _ = own.shape
    depth, chain_width = blocks[0].shape
    width = chain_width * len(blocks) // len(steps)
    tile = min(rows, 128)
    hbm = pl.BlockSpec(memory_space=pl.ANY)
    vmem = pl.BlockSpec(memory_space=pltpu.VMEM)
    named = [("own", own, pl.BlockSpec(memory_space=pltpu.HBM))]
    if other is not None:
        named.append(("other", other, pl.BlockSpec(memory_space=pltpu.HBM)))
    named += [("block", block, vmem) for block in blocks]
    named += [("held", token, vmem) for token in held]
    if final:
        names = (("gains", 0), ("charge", 0), ("gains", 1), ("charge", 1))
        named += [(name, term, vmem) for name, term in zip(names, terms)]
    aliases = {}
    if total is not None:
        if not final:
            aliases = {1 + len(named): 0}
        named.append(("total", total, vmem))
    if final:
        outs = [jax.ShapeDtypeStruct((rows, chain_width), jnp.float32) for _ in finish]
        out_names = [("values", chain) for chain in finish]
    else:
        outs, out_names = [jax.ShapeDtypeStruct((actions, rows, width), jnp.float32)], ["sum"]
    names = [name for name, _, _ in named] + out_names + ["token"]
    return pl.pallas_call(
        functools.partial(step_kernel, section, steps, who, first, tuple(finish), tile, names),
        out_shape=(*outs, jax.ShapeDtypeStruct((8, 128), jnp.float32)),
        in_specs=[pl.BlockSpec(memory_space=pltpu.SMEM)] + [spec for _, _, spec in named],
        out_specs=tuple([vmem] * (len(outs) + 1)),
        scratch_shapes=[
            pltpu.VMEM((len(steps) * depth, width), jnp.bfloat16),
            pltpu.VMEM((len(steps) * depth, width), jnp.bfloat16),
            pltpu.VMEM((2, actions, tile, len(steps) * depth), jnp.float32),
            pltpu.SemaphoreType.DMA((2, len(steps))),
        ],
        input_output_aliases=aliases,
        compiler_params=pltpu.CompilerParams(vmem_limit_bytes=VMEM_LIMIT),
        cost_estimate=pl.CostEstimate(
            flops=COST * actions * rows * len(steps) * depth * width,
            bytes_accessed=4 * actions * rows * len(steps) * depth,
            transcendentals=0,
        ),
        name="step",
    )(info, *[value for _, value, _ in named])


def assemble(info, mine, theirs, ready, result):
    rows, width = mine[0][0].shape
    chosen = [
        (core, (core * CHAINS + i if there == 0 else (1 - core) * CHAINS + i), (theirs if there else mine)[core][i])
        for core in range(2)
        for i in ready[core]
        for there in range(2)
    ]
    refs = [value for _, _, value in chosen]
    aliases = {} if result is None else {1 + len(refs): 0}

    def body(info, *rest):
        ins, out, sem = rest[: len(refs)], rest[-2], rest[-1]
        for core in range(2):

            @pl.when(info[0] == core)
            def _():
                copies = [
                    pltpu.make_async_copy(ref, out.at[0, :, pl.ds(place * width, width)], sem.at[j])
                    for j, (ref, (owner, place, _)) in enumerate(zip(ins, chosen))
                    if owner == core
                ]
                for copy in copies:
                    copy.start()
                for copy in copies:
                    copy.wait()

    hbm = pl.BlockSpec(memory_space=pl.ANY)
    return pl.pallas_call(
        body,
        out_shape=jax.ShapeDtypeStruct((1, rows, 2 * CHAINS * width), jnp.float32),
        in_specs=[pl.BlockSpec(memory_space=pltpu.SMEM)]
        + [pl.BlockSpec(memory_space=pltpu.VMEM)] * len(refs)
        + [hbm] * len(aliases),
        out_specs=hbm,
        scratch_shapes=[pltpu.SemaphoreType.DMA((len(refs),))],
        input_output_aliases=aliases,
        name="assemble",
    )(info, *refs, *([] if result is None else [result]))


def shards(transitions, gain, cost, price_class, terminal):
    core = lax.axis_index("section")
    row_count = lax.axis_size("rows")
    minor = 2 if row_count == 8 else 1
    major = row_count // minor

    def row_at(place):
        if minor == 1:
            return place
        down = place // major
        return (down * (2 * major - 1) + place * (1 - 2 * down)) * minor + down

    ring = [row_at(i) for i in range(row_count)]
    after = {ring[i]: ring[(i + 1) % row_count] for i in range(row_count)}
    before = {b: a for a, b in after.items()}
    onward = [(r * 2 + 1, after[r] * 2 + 1) for r in range(row_count)]
    onward += [(r * 2, before[r] * 2) for r in range(row_count)]
    swap = [(r * 2 + s, r * 2 + 1 - s) for r in range(row_count) for s in range(2)]

    def send(value, pairs):
        return lax.ppermute(value, ("rows", "section"), pairs)

    own = transitions[0]
    scenarios = terminal.shape[1]
    width = scenarios // 2 // CHAINS
    chains = [
        lax.dynamic_slice_in_dim(terminal, core * (scenarios // 2) + i * width, width, 1) for i in range(CHAINS)
    ]

    me = lax.axis_index("rows")
    down = me % minor
    place = down * (2 * major - 1) + (me // minor) * (1 - 2 * down)
    back = jnp.arange(row_count, dtype=jnp.int32) * (1 - 2 * core)
    info = jnp.concatenate([core[None].astype(jnp.int32), row_at((place + back) % row_count).astype(jnp.int32)])

    levels = jnp.arange(cost.shape[2], dtype=jnp.int32)
    onehot = price_class[None, :] == levels[:, None]
    other = send(own, swap)
    terms = [gain[0].T, jnp.sum(jnp.where(onehot[None], cost[0][:, :, None], 0.0), axis=1)]

    last = row_count - 1
    groups = [tuple(range(i, min(i + PAIR, last - 1))) for i in range(0, last - 1, PAIR)]
    when = {max(EARLY + i, group[-1]): [group] for i, group in enumerate(groups)}
    when[last - 2] = [(step,) for group in when[last - 2] for step in group]
    done = [None, None]
    for section in (1, 0):
        total, arrived, tokens, passed = None, [], {}, []

        def add(steps, who, total, first):
            blocks = [block for s in steps for block in arrived[s]]
            held = [passed.pop() for _ in range(len(passed))]
            return step(info, section, steps, who, own, None if who == "own" else other, blocks, total, first, held)

        for s in range(row_count):
            if s:
                for i, gate in ((0, s - 3), (-1, s - 2)):
                    if gate in tokens:
                        chains[i], tokens[gate] = lax.optimization_barrier((chains[i], tokens[gate]))
                        if i == 0 or s == last:
                            passed.append(tokens[gate])
                chains = [send(chain, onward) for chain in chains]
            arrived.append(list(chains))
            if section == 1 and s == 1:
                chains[0], *terms = lax.optimization_barrier((chains[0], *terms))
                terms += [send(term, swap) for term in terms]
            if section == 0 and s < last:
                total, _ = add((s,), "all", total, s == 0)
            if section == 1 and s < last - 1:
                total, _ = add((s,), "own", total, s == 0)
                for group in when.get(s, ()):
                    total, token = add(group, "other", total, group[0] == 0)
                    tokens.setdefault(s, token)
        if section == 1:
            steps = (last - 1, last)
            blocks = arrived[-2] + arrived[-1]
            chains = step(info, section, steps, "all", own, other, blocks, total, False, passed, range(CHAINS), terms)[:CHAINS]
        else:
            chains = [
                step(
                    info, section, (last,), "all", own, other, [chain], total, False, [], (i,), terms
                )[0]
                for i, chain in enumerate(chains)
            ]
        chains = list(chains)
        done[section] = chains

    across = [[(r * 2 + 1 - c, r * 2 + c) for r in range(row_count)] for c in range(2)]
    received = [[send(value, across[section]) for value in done[section]] for section in range(2)]
    result = assemble(info, done, received, (range(CHAINS - 1), range(CHAINS)), None)
    return assemble(info, done, received, ((CHAINS - 1,), ()), result)


def solution(mesh):
    return jax.shard_map(
        shards,
        mesh=mesh,
        in_specs=(
            P(("region", "section"), None, "rows", None),
            P(("region", "section"), None, "rows"),
            P(("region", "section"), None, None),
            P("region"),
            P(("region", "rows"), None),
        ),
        out_specs=P(("region", "section"), "rows", None),
        check_vma=False,
    )
```

time: 232 us -> 211 us (0.909)
  local copies, waits for them, and re-layouts: 20 us -> 3.74 us
  starting transfers between devices: 42.3 us -> 58.4 us
  waiting for transfers between devices: 51.5 us -> 36.5 us
  Pallas kernels: 113 us -> 108 us
    ppermute x34 -> x35, starting transfers between devices: 42.3 us -> 58.4 us  [send(): return lax.ppermute(value, ('rows', 'section'), pairs)]
    ppermute x34 -> x35, waiting for transfers between devices: 51.5 us -> 36.5 us  [send(): return lax.ppermute(value, ('rows', 'section'), pairs)]
    unnamed x30 -> x11, local copies, waits for them, and re-layouts: 15 us -> 2.47 us
    pallas_call x20, Pallas kernels: 110 us -> 103 us  [step(): pl.pallas_call(functools.partial(step_kernel, section, steps, who, first,...]
    pallas_call x1 -> x2, Pallas kernels: 3.5 us -> 5.05 us  [assemble(): pl.pallas_call(body, out_shape=jax.ShapeDtypeStruct((1, rows, 2 * CHAINS...]
  transfers between devices with their start and end apart: 34 -> 35, of which waited for: 16 -> 16; matrix products, arithmetic and copies ran while one was open for 3% -> 2% of each run, Pallas kernels for 48% -> 46%
where the time goes in v3:
time: 211 us; the launch traced here: 209 us
  Pallas kernels  108 us (51%)
  starting transfers between devices  58.4 us (28%)
  waiting for transfers between devices  36.5 us (17%)
  local copies, waits for them, and re-layouts  3.74 us (2%)
    pallas_call x20, Pallas kernels, step(): pl.pallas_call(functools.partial(step_kernel, section, steps, who, first,...  103 us
    ppermute x35, starting transfers between devices, send(): return lax.ppermute(value, ('rows', 'section'), pairs)  58.4 us
    ppermute x35, waiting for transfers between devices, send(): return lax.ppermute(value, ('rows', 'section'), pairs)  36.5 us
    pallas_call x2, Pallas kernels, assemble(): pl.pallas_call(body, out_shape=jax.ShapeDtypeStruct((1, rows, 2 * CHAINS...  5.05 us
  transfers between devices with their start and end apart: 35, of which 16 were waited for; matrix products, arithmetic and copies ran while one was open for 2% of the time, Pallas kernels for 46%

profile of v3, /device:TPU:0, one launch (start us, length us, event | category | flops | bytes accessed | tf_op | source)
XLA Modules:
  0.0 209.2 jit_solution(16916048799289834410)
XLA Ops:
  1.7 2.6 %collective-permute-start.1 = (f32[512,256]{1,0:T(8,128)S(1)}, f32[512,256]{1,0:T(8,128)S(1)}, u32[]{:S(2)}, u32[]{:S(2)}) collective-permute-start(f32[512,256]{1,0:T(8,128)S(1)} %get-tuple-element.80.refs_1_.refs_2_), channel_id=1, source_target_pairs={{1,5},{3,1},{5,9},{7,3},{9,13},{11,7},{13,15},{15,11},{0,2},{2,6},... | collective-permute-start | bytes 1572872 | tf_op jit(solution)/shard_map/ppermute | solution.py:216
  9.5 2.0 collective-permute-done.1.refs_1_.refs_4_
  11.5 2.0 collective-permute-start.2
  13.5 2.9 %collective-permute-start.15 = (f32[512,4]{1,0:T(8,128)S(1)}, f32[512,4]{1,0:T(8,128)S(1)}, u32[]{:S(2)}, u32[]{:S(2)}) collective-permute-start(f32[512,4]{1,0:T(8,128)S(1)} %bitcast.6), channel_id=1, source_target_pairs={{0,1},{1,0},{2,3},{3,2},{4,5},{5,4},{6,7},{7,6},{8,9},{9,8},{10,11... | collective-permute-start | bytes 24584 | tf_op jit(solution)/shard_map/ppermute | solution.py:216
  20.3 2.5 %collective-permute-done.2.refs_1_.refs_2_ = f32[512,256]{1,0:T(8,128)S(1)} collective-permute-done((f32[512,256]{1,0:T(8,128)S(1)}, f32[512,256]{1,0:T(8,128)S(1)}, u32[]{:S(2)}, u32[]{:S(2)}) %collective-permute-start.2) | collective-permute-done | bytes 524320 | tf_op jit(solution)/shard_map/ppermute | solution.py:216
  24.7 3.7 %collective-permute-done.7.refs_2_.refs_3_ = f32[512,256]{1,0:T(8,128)S(1)} collective-permute-done((f32[512,256]{1,0:T(8,128)S(1)}, f32[512,256]{1,0:T(8,128)S(1)}, u32[]{:S(2)}, u32[]{:S(2)}) %collective-permute-start.7) | collective-permute-done | bytes 524320 | tf_op jit(solution)/shard_map/ppermute | solution.py:216
  31.5 2.5 %collective-permute-done.3.refs_1_.refs_4_ = f32[512,256]{1,0:T(8,128)S(1)} collective-permute-done((f32[512,256]{1,0:T(8,128)S(1)}, f32[512,256]{1,0:T(8,128)S(1)}, u32[]{:S(2)}, u32[]{:S(2)}) %collective-permute-start.3) | collective-permute-done | bytes 524320 | tf_op jit(solution)/shard_map/ppermute | solution.py:216
  36.0 3.7 %collective-permute-done.8.refs_2_.refs_5_ = f32[512,256]{1,0:T(8,128)S(1)} collective-permute-done((f32[512,256]{1,0:T(8,128)S(1)}, f32[512,256]{1,0:T(8,128)S(1)}, u32[]{:S(2)}, u32[]{:S(2)}) %collective-permute-start.8) | collective-permute-done | bytes 524320 | tf_op jit(solution)/shard_map/ppermute | solution.py:216
  42.7 2.5 %collective-permute-done.4.refs_1_.refs_2_ = f32[512,256]{1,0:T(8,128)S(1)} collective-permute-done((f32[512,256]{1,0:T(8,128)S(1)}, f32[512,256]{1,0:T(8,128)S(1)}, u32[]{:S(2)}, u32[]{:S(2)}) %collective-permute-start.4) | collective-permute-done | bytes 524320 | tf_op jit(solution)/shard_map/ppermute | solution.py:216
  47.2 2.4 %collective-permute-done.refs_1_ = f32[4,512,4096]{2,1,0:T(8,128)} collective-permute-done((f32[4,512,4096]{2,1,0:T(8,128)}, f32[4,512,4096]{2,1,0:T(8,128)}, u32[]{:S(2)}, u32[]{:S(2)}) %collective-permute-start) | collective-permute-done | bytes 33554464 | tf_op jit(solution)/shard_map/ppermute | solution.py:216
  49.6 9.3 %step.24 = (f32[4,512,512]{2,1,0:T(8,128)S(1)}, f32[8,128]{1,0:T(8,128)S(1)}) custom-call(s32[9]{0:T(128)S(1)} %pad_add_fusion.info, f32[4,512,4096]{2,1,0:T(8,128)} %bitcast.15, f32[4,512,4096]{2,1,0:T(8,128)} %collective-permute-done.refs_1_, f32[512,256]{1,0:T(8,128)S(1)} %get-tuple-element.80.refs_1_.refs_2_, ...), custom_call_target="tpu_custom_call", output_to_operand_aliasing={{0}: (7, {})} | custom-call | flops 12884901888 | bytes 8388608 | tf_op jit(solution)/shard_map/step/pallas_call | solution.py:133
  58.9 2.9 %collective-permute-start.11 = (f32[512,256]{1,0:T(8,128)S(1)}, f32[512,256]{1,0:T(8,128)S(1)}, u32[]{:S(2)}, u32[]{:S(2)}) collective-permute-start(f32[512,256]{1,0:T(8,128)S(1)} %collective-permute-done.9.refs_2_.refs_3_), channel_id=1, source_target_pairs={{1,5},{3,1},{5,9},{7,3},{9,13},{11,7},{13,15},{15,11},{0,2},{2,6},... | collective-permute-start | bytes 1572872 | tf_op jit(solution)/shard_map/ppermute | solution.py:216
  64.6 9.5 %step.26 = (f32[4,512,512]{2,1,0:T(8,128)S(1)}, f32[8,128]{1,0:T(8,128)S(1)}) custom-call(s32[9]{0:T(128)S(1)} %pad_add_fusion.info, f32[4,512,4096]{2,1,0:T(8,128)} %bitcast.17, f32[4,512,4096]{2,1,0:T(8,128)} %collective-permute-done.refs_1_, f32[512,256]{1,0:T(8,128)S(1)} %collective-permute-done.2.refs_1_.refs_2_, ...), custom_call_target="tpu_custom_call", output_to_operand_aliasing={{0}: (7, {})} | custom-call | flops 12884901888 | bytes 8388608 | tf_op jit(solution)/shard_map/step/pallas_call | solution.py:133
  78.5 6.2 %step.28 = (f32[4,512,512]{2,1,0:T(8,128)S(1)}, f32[8,128]{1,0:T(8,128)S(1)}) custom-call(s32[9]{0:T(128)S(1)} %pad_add_fusion.info, f32[4,512,4096]{2,1,0:T(8,128)} %bitcast.19, f32[4,512,4096]{2,1,0:T(8,128)} %collective-permute-done.refs_1_, f32[512,256]{1,0:T(8,128)S(1)} %collective-permute-done.4.refs_1_.refs_2_, ...), custom_call_target="tpu_custom_call", output_to_operand_aliasing={{0}: (5, {})} | custom-call | flops 6442450944 | bytes 4194304 | tf_op jit(solution)/shard_map/step/pallas_call | solution.py:133
  85.7 6.9 %step.29 = (f32[4,512,512]{2,1,0:T(8,128)S(1)}, f32[8,128]{1,0:T(8,128)}) custom-call(s32[9]{0:T(128)S(1)} %pad_add_fusion.info, f32[4,512,4096]{2,1,0:T(8,128)} %bitcast.20, f32[4,512,4096]{2,1,0:T(8,128)} %collective-permute-done.refs_1_, f32[512,256]{1,0:T(8,128)S(1)} %collective-permute-done.5.refs_1_.refs_2_, ...), custom_call_target="tpu_custom_call", output_to_operand_aliasing={{0}: (5, {})} | custom-call | flops 6442450944 | bytes 4194304 | tf_op jit(solution)/shard_map/step/pallas_call | solution.py:133
  92.6 2.0 collective-permute-done.14.refs_5_
  94.6 10.5 %step.30 = (f32[512,256]{1,0:T(8,128)}, f32[512,256]{1,0:T(8,128)}, f32[8,128]{1,0:T(8,128)}) custom-call(s32[9]{0:T(128)S(1)} %pad_add_fusion.info, f32[4,512,4096]{2,1,0:T(8,128)} %bitcast.21, f32[4,512,4096]{2,1,0:T(8,128)} %collective-permute-done.refs_1_, f32[512,256]{1,0:T(8,128)S(1)} %collective-permute-done.10.refs_2_, ...), custom_call_target="tpu_custom_call" | custom-call | flops 12884901888 | bytes 8388608 | tf_op jit(solution)/shard_map/step/pallas_call | solution.py:133
  106.8 2.1 %collective-permute-start.33 = (f32[512,256]{1,0:T(8,128)}, f32[512,256]{1,0:T(8,128)}, u32[]{:S(2)}, u32[]{:S(2)}) collective-permute-start(f32[512,256]{1,0:T(8,128)} %get-tuple-element.69.refs_2_.rest_2_), channel_id=1, source_target_pairs={{0,1},{2,3},{4,5},{6,7},{8,9},{10,11},{12,13},{14,15},{16,17},{18,... | collective-permute-start | bytes 1572872 | tf_op jit(solution)/shard_map/ppermute | solution.py:216
  110.5 2.1 collective-permute-start.34
  112.6 6.7 %step.31 = (f32[4,512,512]{2,1,0:T(8,128)S(1)}, f32[8,128]{1,0:T(8,128)}) custom-call(s32[9]{0:T(128)S(1)} %pad_add_fusion.info, f32[4,512,4096]{2,1,0:T(8,128)} %bitcast.22, f32[4,512,4096]{2,1,0:T(8,128)} %collective-permute-done.refs_1_, f32[512,256]{1,0:T(8,128)} %get-tuple-element.69.refs_2_.rest_2_, f32[512,256]{1,0:T(8,128)} %get-tuple-element.68.refs_3_.rest_4_), custom_call_target="tpu_custom_call" | custom-call | flops 6442450944 | bytes 4194304 | tf_op jit(solution)/shard_map/step/pallas_call | solution.py:133
  123.4 6.2 %step.32 = (f32[4,512,512]{2,1,0:T(8,128)S(1)}, f32[8,128]{1,0:T(8,128)}) custom-call(s32[9]{0:T(128)S(1)} %pad_add_fusion.info, f32[4,512,4096]{2,1,0:T(8,128)} %bitcast.23, f32[4,512,4096]{2,1,0:T(8,128)} %collective-permute-done.refs_1_, f32[512,256]{1,0:T(8,128)S(1)} %collective-permute-done.24.refs_2_, ...), custom_call_target="tpu_custom_call", output_to_operand_aliasing={{0}: (5, {})} | custom-call | flops 6442450944 | bytes 4194304 | tf_op jit(solution)/shard_map/step/pallas_call | solution.py:133
  131.0 4.0 %collective-permute-done.25.refs_2_ = f32[512,256]{1,0:T(8,128)S(1)} collective-permute-done((f32[512,256]{1,0:T(8,128)S(1)}, f32[512,256]{1,0:T(8,128)S(1)}, u32[]{:S(2)}, u32[]{:S(2)}) %collective-permute-start.25) | collective-permute-done | bytes 524320 | tf_op jit(solution)/shard_map/ppermute | solution.py:216
  136.6 6.2 %step.33 = (f32[4,512,512]{2,1,0:T(8,128)S(1)}, f32[8,128]{1,0:T(8,128)}) custom-call(s32[9]{0:T(128)S(1)} %pad_add_fusion.info, f32[4,512,4096]{2,1,0:T(8,128)} %bitcast.24, f32[4,512,4096]{2,1,0:T(8,128)} %collective-permute-done.refs_1_, f32[512,256]{1,0:T(8,128)S(1)} %collective-permute-done.25.refs_2_, ...), custom_call_target="tpu_custom_call", output_to_operand_aliasing={{0}: (5, {})} | custom-call | flops 6442450944 | bytes 4194304 | tf_op jit(solution)/shard_map/step/pallas_call | solution.py:133
  147.8 6.2 %step.34 = (f32[4,512,512]{2,1,0:T(8,128)S(1)}, f32[8,128]{1,0:T(8,128)}) custom-call(s32[9]{0:T(128)S(1)} %pad_add_fusion.info, f32[4,512,4096]{2,1,0:T(8,128)} %bitcast.25, f32[4,512,4096]{2,1,0:T(8,128)} %collective-permute-done.refs_1_, f32[512,256]{1,0:T(8,128)S(1)} %collective-permute-done.26.refs_2_, ...), custom_call_target="tpu_custom_call", output_to_operand_aliasing={{0}: (5, {})} | custom-call | flops 6442450944 | bytes 4194304 | tf_op jit(solution)/shard_map/step/pallas_call | solution.py:133
  159.2 6.2 %step.35 = (f32[4,512,512]{2,1,0:T(8,128)S(1)}, f32[8,128]{1,0:T(8,128)}) custom-call(s32[9]{0:T(128)S(1)} %pad_add_fusion.info, f32[4,512,4096]{2,1,0:T(8,128)} %bitcast.26, f32[4,512,4096]{2,1,0:T(8,128)} %collective-permute-done.refs_1_, f32[512,256]{1,0:T(8,128)S(1)} %collective-permute-done.27.refs_2_, ...), custom_call_target="tpu_custom_call", output_to_operand_aliasing={{0}: (5, {})} | custom-call | flops 6442450944 | bytes 4194304 | tf_op jit(solution)/shard_map/step/pallas_call | solution.py:133
  170.5 6.2 %step.36 = (f32[4,512,512]{2,1,0:T(8,128)S(1)}, f32[8,128]{1,0:T(8,128)}) custom-call(s32[9]{0:T(128)S(1)} %pad_add_fusion.info, f32[4,512,4096]{2,1,0:T(8,128)} %bitcast.27, f32[4,512,4096]{2,1,0:T(8,128)} %collective-permute-done.refs_1_, f32[512,256]{1,0:T(8,128)S(1)} %collective-permute-done.28.refs_2_, ...), custom_call_target="tpu_custom_call", output_to_operand_aliasing={{0}: (5, {})} | custom-call | flops 6442450944 | bytes 4194304 | tf_op jit(solution)/shard_map/step/pallas_call | solution.py:133
  176.7 3.6 %collective-permute-done.29.refs_2_ = f32[512,256]{1,0:T(8,128)S(1)} collective-permute-done((f32[512,256]{1,0:T(8,128)S(1)}, f32[512,256]{1,0:T(8,128)S(1)}, u32[]{:S(2)}, u32[]{:S(2)}) %collective-permute-start.29) | collective-permute-done | bytes 524320 | tf_op jit(solution)/shard_map/ppermute | solution.py:216
  183.1 6.2 %step.37 = (f32[4,512,512]{2,1,0:T(8,128)S(1)}, f32[8,128]{1,0:T(8,128)}) custom-call(s32[9]{0:T(128)S(1)} %pad_add_fusion.info, f32[4,512,4096]{2,1,0:T(8,128)} %bitcast.28, f32[4,512,4096]{2,1,0:T(8,128)} %collective-permute-done.refs_1_, f32[512,256]{1,0:T(8,128)S(1)} %collective-permute-done.29.refs_2_, ...), custom_call_target="tpu_custom_call", output_to_operand_aliasing={{0}: (5, {})} | custom-call | flops 6442450944 | bytes 4194304 | tf_op jit(solution)/shard_map/step/pallas_call | solution.py:133
  189.5 4.9 %step.39 = (f32[512,256]{1,0:T(8,128)S(1)}, f32[8,128]{1,0:T(8,128)}) custom-call(s32[9]{0:T(128)S(1)} %pad_add_fusion.info, f32[4,512,4096]{2,1,0:T(8,128)} %bitcast.29, f32[4,512,4096]{2,1,0:T(8,128)} %collective-permute-done.refs_1_, f32[512,256]{1,0:T(8,128)S(1)} %collective-permute-done.31.refs_2_, f32[512,4]{1,0:T(8,128)S(1)} %bitcast.8, ...), custom_call_target="tpu_custom_call" | custom-call | flops 3221225472 | bytes 4194304 | tf_op jit(solution)/shard_map/step/pallas_call | solution.py:133
  195.7 5.2 %step.38 = (f32[512,256]{1,0:T(8,128)S(1)}, f32[8,128]{1,0:T(8,128)}) custom-call(s32[9]{0:T(128)S(1)} %pad_add_fusion.info, f32[4,512,4096]{2,1,0:T(8,128)} %bitcast.30, f32[4,512,4096]{2,1,0:T(8,128)} %collective-permute-done.refs_1_, f32[512,256]{1,0:T(8,128)S(1)} %collective-permute-done.23.refs_2_, f32[512,4]{1,0:T(8,128)S(1)} %bitcast.9, ...), custom_call_target="tpu_custom_call" | custom-call | flops 3221225472 | bytes 4194304 | tf_op jit(solution)/shard_map/step/pallas_call | solution.py:133
  203.2 2.9 %assemble.2.rest_2_ = f32[1,512,1024]{2,1,0:T(8,128)} custom-call(s32[9]{0:T(128)} %copy-done.2, f32[512,256]{1,0:T(8,128)} %copy-done, f32[512,256]{1,0:T(8,128)} %copy-done.3, f32[512,256]{1,0:T(8,128)} %get-tuple-element.69.refs_2_.rest_2_, f32[512,256]{1,0:T(8,128)} %collective-permute-done.33.rest_3_, f32[512,256]{1,0:T(8,128)} %get-tuple-element.68.refs_3_.rest_4_, ...), custom_call_target="tpu_custom_call" | custom-call | tf_op jit(solution)/shard_map/assemble/pallas_call | solution.py:183
  206.9 2.2 %assemble.3 = f32[1,512,1024]{2,1,0:T(8,128)} custom-call(s32[9]{0:T(128)} %copy-done.2, f32[512,256]{1,0:T(8,128)} %copy-done.1, f32[512,256]{1,0:T(8,128)} %copy-done.4, f32[1,512,1024]{2,1,0:T(8,128)} %assemble.2.rest_2_), custom_call_target="tpu_custom_call", output_to_operand_aliasing={{}: (3, {})} | custom-call | tf_op jit(solution)/shard_map/assemble/pallas_call | solution.py:183
  (76 shorter events, 63.8 us)
Async XLA Ops:
  0.0 49.6 %collective-permute-start = (f32[4,512,4096]{2,1,0:T(8,128)}, f32[4,512,4096]{2,1,0:T(8,128)}, u32[]{:S(2)}, u32[]{:S(2)}) collective-permute-start(f32[4,512,4096]{2,1,0:T(8,128)} %bitcast.10), channel_id=1, source_target_pairs={{0,1},{1,0},{2,3},{3,2},{4,5},{5,4},{6,7},{7,6},{8,9},{9,8},{10,11... | collective-permute-start | bytes 100663304 | tf_op jit(solution)/shard_map/ppermute | solution.py:216
  1.7 9.8 %collective-permute-start.1 = (f32[512,256]{1,0:T(8,128)S(1)}, f32[512,256]{1,0:T(8,128)S(1)}, u32[]{:S(2)}, u32[]{:S(2)}) collective-permute-start(f32[512,256]{1,0:T(8,128)S(1)} %get-tuple-element.80.refs_1_.refs_2_), channel_id=1, source_target_pairs={{1,5},{3,1},{5,9},{7,3},{9,13},{11,7},{13,15},{15,11},{0,2},{2,6},... | collective-permute-start | bytes 1572872 | tf_op jit(solution)/shard_map/ppermute | solution.py:216
  4.3 12.8 %collective-permute-start.6 = (f32[512,256]{1,0:T(8,128)S(1)}, f32[512,256]{1,0:T(8,128)S(1)}, u32[]{:S(2)}, u32[]{:S(2)}) collective-permute-start(f32[512,256]{1,0:T(8,128)S(1)} %get-tuple-element.79.refs_2_.refs_3_), channel_id=1, source_target_pairs={{1,5},{3,1},{5,9},{7,3},{9,13},{11,7},{13,15},{15,11},{0,2},{2,6},... | collective-permute-start | bytes 1572872 | tf_op jit(solution)/shard_map/ppermute | solution.py:216
  11.5 11.2 %collective-permute-start.2 = (f32[512,256]{1,0:T(8,128)S(1)}, f32[512,256]{1,0:T(8,128)S(1)}, u32[]{:S(2)}, u32[]{:S(2)}) collective-permute-start(f32[512,256]{1,0:T(8,128)S(1)} %collective-permute-done.1.refs_1_.refs_4_), channel_id=1, source_target_pairs={{1,5},{3,1},{5,9},{7,3},{9,13},{11,7},{13,15},{15,11},{0,2},{2,6},... | collective-permute-start | bytes 1572872 | tf_op jit(solution)/shard_map/ppermute | solution.py:216
  13.5 79.1 %collective-permute-start.15 = (f32[512,4]{1,0:T(8,128)S(1)}, f32[512,4]{1,0:T(8,128)S(1)}, u32[]{:S(2)}, u32[]{:S(2)}) collective-permute-start(f32[512,4]{1,0:T(8,128)S(1)} %bitcast.6), channel_id=1, source_target_pairs={{0,1},{1,0},{2,3},{3,2},{4,5},{5,4},{6,7},{7,6},{8,9},{9,8},{10,11... | collective-permute-start | bytes 24584 | tf_op jit(solution)/shard_map/ppermute | solution.py:216
  16.3 76.3 %collective-permute-start.16 = (f32[4,1024]{1,0:T(4,128)S(1)}, f32[4,1024]{1,0:T(4,128)S(1)}, u32[]{:S(2)}, u32[]{:S(2)}) collective-permute-start(f32[4,1024]{1,0:T(4,128)S(1)} %select_reduce_fusion.refs_10_.refs_4_), channel_id=1, source_target_pairs={{0,1},{1,0},{2,3},{3,2},{4,5},{5,4},{6,7},{7,6},{8,9},{9,8},{10,11... | collective-permute-start | bytes 49160 | tf_op jit(solution)/shard_map/ppermute | solution.py:216
  17.1 11.2 %collective-permute-start.7 = (f32[512,256]{1,0:T(8,128)S(1)}, f32[512,256]{1,0:T(8,128)S(1)}, u32[]{:S(2)}, u32[]{:S(2)}) collective-permute-start(f32[512,256]{1,0:T(8,128)S(1)} %collective-permute-done.6.refs_2_.refs_5_), channel_id=1, source_target_pairs={{1,5},{3,1},{5,9},{7,3},{9,13},{11,7},{13,15},{15,11},{0,2},{2,6},... | collective-permute-start | bytes 1572872 | tf_op jit(solution)/shard_map/ppermute | solution.py:216
  22.8 11.2 %collective-permute-start.3 = (f32[512,256]{1,0:T(8,128)S(1)}, f32[512,256]{1,0:T(8,128)S(1)}, u32[]{:S(2)}, u32[]{:S(2)}) collective-permute-start(f32[512,256]{1,0:T(8,128)S(1)} %collective-permute-done.2.refs_1_.refs_2_), channel_id=1, source_target_pairs={{1,5},{3,1},{5,9},{7,3},{9,13},{11,7},{13,15},{15,11},{0,2},{2,6},... | collective-permute-start | bytes 1572872 | tf_op jit(solution)/shard_map/ppermute | solution.py:216
  28.4 11.2 %collective-permute-start.8 = (f32[512,256]{1,0:T(8,128)S(1)}, f32[512,256]{1,0:T(8,128)S(1)}, u32[]{:S(2)}, u32[]{:S(2)}) collective-permute-start(f32[512,256]{1,0:T(8,128)S(1)} %collective-permute-done.7.refs_2_.refs_3_), channel_id=1, source_target_pairs={{1,5},{3,1},{5,9},{7,3},{9,13},{11,7},{13,15},{15,11},{0,2},{2,6},... | collective-permute-start | bytes 1572872 | tf_op jit(solution)/shard_map/ppermute | solution.py:216
  34.0 11.2 %collective-permute-start.4 = (f32[512,256]{1,0:T(8,128)S(1)}, f32[512,256]{1,0:T(8,128)S(1)}, u32[]{:S(2)}, u32[]{:S(2)}) collective-permute-start(f32[512,256]{1,0:T(8,128)S(1)} %collective-permute-done.3.refs_1_.refs_4_), channel_id=1, source_target_pairs={{1,5},{3,1},{5,9},{7,3},{9,13},{11,7},{13,15},{15,11},{0,2},{2,6},... | collective-permute-start | bytes 1572872 | tf_op jit(solution)/shard_map/ppermute | solution.py:216
  39.6 19.3 %collective-permute-start.9 = (f32[512,256]{1,0:T(8,128)S(1)}, f32[512,256]{1,0:T(8,128)S(1)}, u32[]{:S(2)}, u32[]{:S(2)}) collective-permute-start(f32[512,256]{1,0:T(8,128)S(1)} %collective-permute-done.8.refs_2_.refs_5_), channel_id=1, source_target_pairs={{1,5},{3,1},{5,9},{7,3},{9,13},{11,7},{13,15},{15,11},{0,2},{2,6},... | collective-permute-start | bytes 1572872 | tf_op jit(solution)/shard_map/ppermute | solution.py:216
  45.2 16.7 %collective-permute-start.5 = (f32[512,256]{1,0:T(8,128)S(1)}, f32[512,256]{1,0:T(8,128)S(1)}, u32[]{:S(2)}, u32[]{:S(2)}) collective-permute-start(f32[512,256]{1,0:T(8,128)S(1)} %collective-permute-done.4.refs_1_.refs_2_), channel_id=1, source_target_pairs={{1,5},{3,1},{5,9},{7,3},{9,13},{11,7},{13,15},{15,11},{0,2},{2,6},... | collective-permute-start | bytes 1572872 | tf_op jit(solution)/shard_map/ppermute | solution.py:216
  58.9 15.2 %collective-permute-start.11 = (f32[512,256]{1,0:T(8,128)S(1)}, f32[512,256]{1,0:T(8,128)S(1)}, u32[]{:S(2)}, u32[]{:S(2)}) collective-permute-start(f32[512,256]{1,0:T(8,128)S(1)} %collective-permute-done.9.refs_2_.refs_3_), channel_id=1, source_target_pairs={{1,5},{3,1},{5,9},{7,3},{9,13},{11,7},{13,15},{15,11},{0,2},{2,6},... | collective-permute-start | bytes 1572872 | tf_op jit(solution)/shard_map/ppermute | solution.py:216
  61.9 13.9 %collective-permute-start.10 = (f32[512,256]{1,0:T(8,128)S(1)}, f32[512,256]{1,0:T(8,128)S(1)}, u32[]{:S(2)}, u32[]{:S(2)}) collective-permute-start(f32[512,256]{1,0:T(8,128)S(1)} %collective-permute-done.5.refs_1_.refs_2_), channel_id=1, source_target_pairs={{1,5},{3,1},{5,9},{7,3},{9,13},{11,7},{13,15},{15,11},{0,2},{2,6},... | collective-permute-start | bytes 1572872 | tf_op jit(solution)/shard_map/ppermute | solution.py:216
  74.2 10.6 %collective-permute-start.12 = (f32[512,256]{1,0:T(8,128)S(1)}, f32[512,256]{1,0:T(8,128)S(1)}, u32[]{:S(2)}, u32[]{:S(2)}) collective-permute-start(f32[512,256]{1,0:T(8,128)S(1)} %collective-permute-done.11.refs_2_.refs_3_), channel_id=1, source_target_pairs={{1,5},{3,1},{5,9},{7,3},{9,13},{11,7},{13,15},{15,11},{0,2},{2,6},... | collective-permute-start | bytes 1572872 | tf_op jit(solution)/shard_map/ppermute | solution.py:216
  75.8 16.8 %collective-permute-start.13 = (f32[512,256]{1,0:T(8,128)S(1)}, f32[512,256]{1,0:T(8,128)S(1)}, u32[]{:S(2)}, u32[]{:S(2)}) collective-permute-start(f32[512,256]{1,0:T(8,128)S(1)} %collective-permute-done.10.refs_2_), channel_id=1, source_target_pairs={{1,5},{3,1},{5,9},{7,3},{9,13},{11,7},{13,15},{15,11},{0,2},{2,6},... | collective-permute-start | bytes 1572872 | tf_op jit(solution)/shard_map/ppermute | solution.py:216
  84.7 9.9 %collective-permute-start.14 = (f32[512,256]{1,0:T(8,128)S(1)}, f32[512,256]{1,0:T(8,128)S(1)}, u32[]{:S(2)}, u32[]{:S(2)}) collective-permute-start(f32[512,256]{1,0:T(8,128)S(1)} %collective-permute-done.12.refs_3_), channel_id=1, source_target_pairs={{1,5},{3,1},{5,9},{7,3},{9,13},{11,7},{13,15},{15,11},{0,2},{2,6},... | collective-permute-start | bytes 1572872 | tf_op jit(solution)/shard_map/ppermute | solution.py:216
  105.2 16.6 %collective-permute-start.24 = (f32[512,256]{1,0:T(8,128)}, f32[512,256]{1,0:T(8,128)S(1)}, u32[]{:S(2)}, u32[]{:S(2)}) collective-permute-start(f32[512,256]{1,0:T(8,128)} %get-tuple-element.69.refs_2_.rest_2_), channel_id=1, source_target_pairs={{1,5},{3,1},{5,9},{7,3},{9,13},{11,7},{13,15},{15,11},{0,2},{2,6},... | collective-permute-start | bytes 1572872 | tf_op jit(solution)/shard_map/ppermute | solution.py:216
  106.8 95.5 %collective-permute-start.33 = (f32[512,256]{1,0:T(8,128)}, f32[512,256]{1,0:T(8,128)}, u32[]{:S(2)}, u32[]{:S(2)}) collective-permute-start(f32[512,256]{1,0:T(8,128)} %get-tuple-element.69.refs_2_.rest_2_), channel_id=1, source_target_pairs={{0,1},{2,3},{4,5},{6,7},{8,9},{10,11},{12,13},{14,15},{16,17},{18,... | collective-permute-start | bytes 1572872 | tf_op jit(solution)/shard_map/ppermute | solution.py:216
  108.9 11.3 %collective-permute-start.17 = (f32[512,256]{1,0:T(8,128)}, f32[512,256]{1,0:T(8,128)S(1)}, u32[]{:S(2)}, u32[]{:S(2)}) collective-permute-start(f32[512,256]{1,0:T(8,128)} %get-tuple-element.68.refs_3_.rest_4_), channel_id=1, source_target_pairs={{1,5},{3,1},{5,9},{7,3},{9,13},{11,7},{13,15},{15,11},{0,2},{2,6},... | collective-permute-start | bytes 1572872 | tf_op jit(solution)/shard_map/ppermute | solution.py:216
  110.5 91.8 %collective-permute-start.34 = (f32[512,256]{1,0:T(8,128)}, f32[512,256]{1,0:T(8,128)}, u32[]{:S(2)}, u32[]{:S(2)}) collective-permute-start(f32[512,256]{1,0:T(8,128)} %get-tuple-element.68.refs_3_.rest_4_), channel_id=1, source_target_pairs={{0,1},{2,3},{4,5},{6,7},{8,9},{10,11},{12,13},{14,15},{16,17},{18,... | collective-permute-start | bytes 1572872 | tf_op jit(solution)/shard_map/ppermute | solution.py:216
  120.2 9.4 %collective-permute-start.18 = (f32[512,256]{1,0:T(8,128)S(1)}, f32[512,256]{1,0:T(8,128)S(1)}, u32[]{:S(2)}, u32[]{:S(2)}) collective-permute-start(f32[512,256]{1,0:T(8,128)S(1)} %collective-permute-done.17.refs_3_), channel_id=1, source_target_pairs={{1,5},{3,1},{5,9},{7,3},{9,13},{11,7},{13,15},{15,11},{0,2},{2,6},... | collective-permute-start | bytes 1572872 | tf_op jit(solution)/shard_map/ppermute | solution.py:216
  121.8 13.2 %collective-permute-start.25 = (f32[512,256]{1,0:T(8,128)S(1)}, f32[512,256]{1,0:T(8,128)S(1)}, u32[]{:S(2)}, u32[]{:S(2)}) collective-permute-start(f32[512,256]{1,0:T(8,128)S(1)} %collective-permute-done.24.refs_2_), channel_id=1, source_target_pairs={{1,5},{3,1},{5,9},{7,3},{9,13},{11,7},{13,15},{15,11},{0,2},{2,6},... | collective-permute-start | bytes 1572872 | tf_op jit(solution)/shard_map/ppermute | solution.py:216
  129.6 13.2 %collective-permute-start.19 = (f32[512,256]{1,0:T(8,128)S(1)}, f32[512,256]{1,0:T(8,128)S(1)}, u32[]{:S(2)}, u32[]{:S(2)}) collective-permute-start(f32[512,256]{1,0:T(8,128)S(1)} %collective-permute-done.18.refs_3_), channel_id=1, source_target_pairs={{1,5},{3,1},{5,9},{7,3},{9,13},{11,7},{13,15},{15,11},{0,2},{2,6},... | collective-permute-start | bytes 1572872 | tf_op jit(solution)/shard_map/ppermute | solution.py:216
  135.0 11.2 %collective-permute-start.26 = (f32[512,256]{1,0:T(8,128)S(1)}, f32[512,256]{1,0:T(8,128)S(1)}, u32[]{:S(2)}, u32[]{:S(2)}) collective-permute-start(f32[512,256]{1,0:T(8,128)S(1)} %collective-permute-done.25.refs_2_), channel_id=1, source_target_pairs={{1,5},{3,1},{5,9},{7,3},{9,13},{11,7},{13,15},{15,11},{0,2},{2,6},... | collective-permute-start | bytes 1572872 | tf_op jit(solution)/shard_map/ppermute | solution.py:216
  142.8 11.2 %collective-permute-start.20 = (f32[512,256]{1,0:T(8,128)S(1)}, f32[512,256]{1,0:T(8,128)S(1)}, u32[]{:S(2)}, u32[]{:S(2)}) collective-permute-start(f32[512,256]{1,0:T(8,128)S(1)} %collective-permute-done.19.refs_3_), channel_id=1, source_target_pairs={{1,5},{3,1},{5,9},{7,3},{9,13},{11,7},{13,15},{15,11},{0,2},{2,6},... | collective-permute-start | bytes 1572872 | tf_op jit(solution)/shard_map/ppermute | solution.py:216
  146.3 11.4 %collective-permute-start.27 = (f32[512,256]{1,0:T(8,128)S(1)}, f32[512,256]{1,0:T(8,128)S(1)}, u32[]{:S(2)}, u32[]{:S(2)}) collective-permute-start(f32[512,256]{1,0:T(8,128)S(1)} %collective-permute-done.26.refs_2_), channel_id=1, source_target_pairs={{1,5},{3,1},{5,9},{7,3},{9,13},{11,7},{13,15},{15,11},{0,2},{2,6},... | collective-permute-start | bytes 1572872 | tf_op jit(solution)/shard_map/ppermute | solution.py:216
  154.0 11.4 %collective-permute-start.21 = (f32[512,256]{1,0:T(8,128)S(1)}, f32[512,256]{1,0:T(8,128)S(1)}, u32[]{:S(2)}, u32[]{:S(2)}) collective-permute-start(f32[512,256]{1,0:T(8,128)S(1)} %collective-permute-done.20.refs_3_), channel_id=1, source_target_pairs={{1,5},{3,1},{5,9},{7,3},{9,13},{11,7},{13,15},{15,11},{0,2},{2,6},... | collective-permute-start | bytes 1572872 | tf_op jit(solution)/shard_map/ppermute | solution.py:216
  157.6 11.2 %collective-permute-start.28 = (f32[512,256]{1,0:T(8,128)S(1)}, f32[512,256]{1,0:T(8,128)S(1)}, u32[]{:S(2)}, u32[]{:S(2)}) collective-permute-start(f32[512,256]{1,0:T(8,128)S(1)} %collective-permute-done.27.refs_2_), channel_id=1, source_target_pairs={{1,5},{3,1},{5,9},{7,3},{9,13},{11,7},{13,15},{15,11},{0,2},{2,6},... | collective-permute-start | bytes 1572872 | tf_op jit(solution)/shard_map/ppermute | solution.py:216
  165.4 16.3 %collective-permute-start.22 = (f32[512,256]{1,0:T(8,128)S(1)}, f32[512,256]{1,0:T(8,128)S(1)}, u32[]{:S(2)}, u32[]{:S(2)}) collective-permute-start(f32[512,256]{1,0:T(8,128)S(1)} %collective-permute-done.21.refs_3_), channel_id=1, source_target_pairs={{1,5},{3,1},{5,9},{7,3},{9,13},{11,7},{13,15},{15,11},{0,2},{2,6},... | collective-permute-start | bytes 1572872 | tf_op jit(solution)/shard_map/ppermute | solution.py:216
  168.9 11.4 %collective-permute-start.29 = (f32[512,256]{1,0:T(8,128)S(1)}, f32[512,256]{1,0:T(8,128)S(1)}, u32[]{:S(2)}, u32[]{:S(2)}) collective-permute-start(f32[512,256]{1,0:T(8,128)S(1)} %collective-permute-done.28.refs_2_), channel_id=1, source_target_pairs={{1,5},{3,1},{5,9},{7,3},{9,13},{11,7},{13,15},{15,11},{0,2},{2,6},... | collective-permute-start | bytes 1572872 | tf_op jit(solution)/shard_map/ppermute | solution.py:216
  181.7 14.0 %collective-permute-start.23 = (f32[512,256]{1,0:T(8,128)S(1)}, f32[512,256]{1,0:T(8,128)S(1)}, u32[]{:S(2)}, u32[]{:S(2)}) collective-permute-start(f32[512,256]{1,0:T(8,128)S(1)} %collective-permute-done.22.refs_3_), channel_id=1, source_target_pairs={{1,5},{3,1},{5,9},{7,3},{9,13},{11,7},{13,15},{15,11},{0,2},{2,6},... | collective-permute-start | bytes 1572872 | tf_op jit(solution)/shard_map/ppermute | solution.py:216
  (8 other events, 224.3 us)

commit v4 on v3

--- a/solution.py
+++ b/solution.py
@@ -156,9 +156,7 @@
     rows, width = mine[0][0].shape
     chosen = [
         (core, (core * CHAINS + i if there == 0 else (1 - core) * CHAINS + i), (theirs if there else mine)[core][i])
-        for core in range(2)
-        for i in ready[core]
-        for there in range(2)
+        for core, there, i in ready
     ]
     refs = [value for _, _, value in chosen]
     aliases = {} if result is None else {1 + len(refs): 0}
@@ -189,6 +187,7 @@
         out_specs=hbm,
         scratch_shapes=[pltpu.SemaphoreType.DMA((len(refs),))],
         input_output_aliases=aliases,
+        compiler_params=pltpu.CompilerParams(vmem_limit_bytes=8 * 1024 * 1024),
         name="assemble",
     )(info, *refs, *([] if result is None else [result]))
 
@@ -237,6 +236,8 @@
     groups = [tuple(range(i, min(i + PAIR, last - 1))) for i in range(0, last - 1, PAIR)]
     when = {max(EARLY + i, group[-1]): [group] for i, group in enumerate(groups)}
     when[last - 2] = [(step,) for group in when[last - 2] for step in group]
+    across = [[(r * 2 + 1 - c, r * 2 + c) for r in range(row_count)] for c in range(2)]
+    received = [[], []]
     done = [None, None]
     for section in (1, 0):
         total, arrived, tokens, passed = None, [], {}, []
@@ -259,7 +260,11 @@
                 chains[0], *terms = lax.optimization_barrier((chains[0], *terms))
                 terms += [send(term, swap) for term in terms]
             if section == 0 and s < last:
-                total, _ = add((s,), "all", total, s == 0)
+                total, token = add((s,), "all", total, s == 0)
+                if 0 < s <= CHAINS:
+                    value, token = lax.optimization_barrier((done[1][s - 1], token))
+                    passed.append(token)
+                    received[1].append(send(value, across[1]))
             if section == 1 and s < last - 1:
                 total, _ = add((s,), "own", total, s == 0)
                 for group in when.get(s, ()):
@@ -279,10 +284,11 @@
         chains = list(chains)
         done[section] = chains
 
-    across = [[(r * 2 + 1 - c, r * 2 + c) for r in range(row_count)] for c in range(2)]
-    received = [[send(value, across[section]) for value in done[section]] for section in range(2)]
-    result = assemble(info, done, received, (range(CHAINS - 1), range(CHAINS)), None)
-    return assemble(info, done, received, ((CHAINS - 1,), ()), result)
+    received[0] = [send(value, across[0]) for value in done[0]]
+    ready = [(c, there, i) for c in range(2) for there in range(2) for i in range(CHAINS)]
+    late = (0, 1, CHAINS - 1)
+    result = assemble(info, done, received, [chunk for chunk in ready if chunk != late], None)
+    return assemble(info, done, received, [late], result)
 
 
 def solution(mesh):

time: 211 us -> 204 us (0.967)
  starting transfers between devices: 58.4 us -> 53.8 us
  waiting for transfers between devices: 36.5 us -> 40 us
  Pallas kernels: 108 us -> 105 us
    ppermute x35, starting transfers between devices: 58.4 us -> 53.8 us  [send(): return lax.ppermute(value, ('rows', 'section'), pairs)]
    ppermute x35, waiting for transfers between devices: 36.5 us -> 40 us  [send(): return lax.ppermute(value, ('rows', 'section'), pairs)]
  transfers between devices with their start and end apart: 35 -> 35, of which waited for: 16 -> 17; matrix products, arithmetic and copies ran while one was open for 2% -> 2% of each run, Pallas kernels for 46% -> 46%
where the time goes in v4:
time: 204 us; the launch traced here: 203 us
  Pallas kernels  105 us (51%)
  starting transfers between devices  53.8 us (26%)
  waiting for transfers between devices  40 us (20%)
  local copies, waits for them, and re-layouts  2.11 us (1%)
    pallas_call x20, Pallas kernels, step(): pl.pallas_call(functools.partial(step_kernel, section, steps, who, first,...  102 us
    ppermute x35, starting transfers between devices, send(): return lax.ppermute(value, ('rows', 'section'), pairs)  53.8 us
    ppermute x35, waiting for transfers between devices, send(): return lax.ppermute(value, ('rows', 'section'), pairs)  40 us
  transfers between devices with their start and end apart: 35, of which 17 were waited for; matrix products, arithmetic and copies ran while one was open for 2% of the time, Pallas kernels for 46%

profile of v4, /device:TPU:0, one launch (start us, length us, event | category | flops | bytes accessed | tf_op | source)
XLA Modules:
  0.0 203.1 jit_solution(831035566719910617)
XLA Ops:
  1.7 2.6 %collective-permute-start.1 = (f32[512,256]{1,0:T(8,128)S(1)}, f32[512,256]{1,0:T(8,128)S(1)}, u32[]{:S(2)}, u32[]{:S(2)}) collective-permute-start(f32[512,256]{1,0:T(8,128)S(1)} %get-tuple-element.92.refs_1_.refs_2_), channel_id=1, source_target_pairs={{1,5},{3,1},{5,9},{7,3},{9,13},{11,7},{13,15},{15,11},{0,2},{2,6},... | collective-permute-start | bytes 1572872 | tf_op jit(solution)/shard_map/ppermute | solution.py:215
  9.5 2.0 collective-permute-done.1.refs_1_.refs_4_
  11.5 2.0 collective-permute-start.2
  13.5 2.9 %collective-permute-start.15 = (f32[512,4]{1,0:T(8,128)S(1)}, f32[512,4]{1,0:T(8,128)S(1)}, u32[]{:S(2)}, u32[]{:S(2)}) collective-permute-start(f32[512,4]{1,0:T(8,128)S(1)} %bitcast.6), channel_id=1, source_target_pairs={{0,1},{1,0},{2,3},{3,2},{4,5},{5,4},{6,7},{7,6},{8,9},{9,8},{10,11... | collective-permute-start | bytes 24584 | tf_op jit(solution)/shard_map/ppermute | solution.py:215
  17.1 2.0 collective-permute-start.7
  20.3 2.5 %collective-permute-done.2.refs_1_.refs_2_ = f32[512,256]{1,0:T(8,128)S(1)} collective-permute-done((f32[512,256]{1,0:T(8,128)S(1)}, f32[512,256]{1,0:T(8,128)S(1)}, u32[]{:S(2)}, u32[]{:S(2)}) %collective-permute-start.2) | collective-permute-done | bytes 524320 | tf_op jit(solution)/shard_map/ppermute | solution.py:215
  24.7 3.7 %collective-permute-done.7.refs_2_.refs_3_ = f32[512,256]{1,0:T(8,128)S(1)} collective-permute-done((f32[512,256]{1,0:T(8,128)S(1)}, f32[512,256]{1,0:T(8,128)S(1)}, u32[]{:S(2)}, u32[]{:S(2)}) %collective-permute-start.7) | collective-permute-done | bytes 524320 | tf_op jit(solution)/shard_map/ppermute | solution.py:215
  31.5 2.5 %collective-permute-done.3.refs_1_.refs_4_ = f32[512,256]{1,0:T(8,128)S(1)} collective-permute-done((f32[512,256]{1,0:T(8,128)S(1)}, f32[512,256]{1,0:T(8,128)S(1)}, u32[]{:S(2)}, u32[]{:S(2)}) %collective-permute-start.3) | collective-permute-done | bytes 524320 | tf_op jit(solution)/shard_map/ppermute | solution.py:215
  36.0 3.7 %collective-permute-done.8.refs_2_.refs_5_ = f32[512,256]{1,0:T(8,128)S(1)} collective-permute-done((f32[512,256]{1,0:T(8,128)S(1)}, f32[512,256]{1,0:T(8,128)S(1)}, u32[]{:S(2)}, u32[]{:S(2)}) %collective-permute-start.8) | collective-permute-done | bytes 524320 | tf_op jit(solution)/shard_map/ppermute | solution.py:215
  42.7 2.5 %collective-permute-done.4.refs_1_.refs_2_ = f32[512,256]{1,0:T(8,128)S(1)} collective-permute-done((f32[512,256]{1,0:T(8,128)S(1)}, f32[512,256]{1,0:T(8,128)S(1)}, u32[]{:S(2)}, u32[]{:S(2)}) %collective-permute-start.4) | collective-permute-done | bytes 524320 | tf_op jit(solution)/shard_map/ppermute | solution.py:215
  47.2 2.4 %collective-permute-done.refs_1_ = f32[4,512,4096]{2,1,0:T(8,128)} collective-permute-done((f32[4,512,4096]{2,1,0:T(8,128)}, f32[4,512,4096]{2,1,0:T(8,128)}, u32[]{:S(2)}, u32[]{:S(2)}) %collective-permute-start) | collective-permute-done | bytes 33554464 | tf_op jit(solution)/shard_map/ppermute | solution.py:215
  49.6 9.3 %step.24 = (f32[4,512,512]{2,1,0:T(8,128)S(1)}, f32[8,128]{1,0:T(8,128)S(1)}) custom-call(s32[9]{0:T(128)S(1)} %pad_add_fusion.info, f32[4,512,4096]{2,1,0:T(8,128)} %bitcast.15, f32[4,512,4096]{2,1,0:T(8,128)} %collective-permute-done.refs_1_, f32[512,256]{1,0:T(8,128)S(1)} %get-tuple-element.92.refs_1_.refs_2_, ...), custom_call_target="tpu_custom_call", output_to_operand_aliasing={{0}: (7, {})} | custom-call | flops 12884901888 | bytes 8388608 | tf_op jit(solution)/shard_map/step/pallas_call | solution.py:133
  58.9 2.9 %collective-permute-start.11 = (f32[512,256]{1,0:T(8,128)S(1)}, f32[512,256]{1,0:T(8,128)S(1)}, u32[]{:S(2)}, u32[]{:S(2)}) collective-permute-start(f32[512,256]{1,0:T(8,128)S(1)} %collective-permute-done.9.refs_2_.refs_3_), channel_id=1, source_target_pairs={{1,5},{3,1},{5,9},{7,3},{9,13},{11,7},{13,15},{15,11},{0,2},{2,6},... | collective-permute-start | bytes 1572872 | tf_op jit(solution)/shard_map/ppermute | solution.py:215
  64.6 9.5 %step.26 = (f32[4,512,512]{2,1,0:T(8,128)S(1)}, f32[8,128]{1,0:T(8,128)S(1)}) custom-call(s32[9]{0:T(128)S(1)} %pad_add_fusion.info, f32[4,512,4096]{2,1,0:T(8,128)} %bitcast.17, f32[4,512,4096]{2,1,0:T(8,128)} %collective-permute-done.refs_1_, f32[512,256]{1,0:T(8,128)S(1)} %collective-permute-done.2.refs_1_.refs_2_, ...), custom_call_target="tpu_custom_call", output_to_operand_aliasing={{0}: (7, {})} | custom-call | flops 12884901888 | bytes 8388608 | tf_op jit(solution)/shard_map/step/pallas_call | solution.py:133
  78.5 6.2 %step.28 = (f32[4,512,512]{2,1,0:T(8,128)S(1)}, f32[8,128]{1,0:T(8,128)S(1)}) custom-call(s32[9]{0:T(128)S(1)} %pad_add_fusion.info, f32[4,512,4096]{2,1,0:T(8,128)} %bitcast.19, f32[4,512,4096]{2,1,0:T(8,128)} %collective-permute-done.refs_1_, f32[512,256]{1,0:T(8,128)S(1)} %collective-permute-done.4.refs_1_.refs_2_, ...), custom_call_target="tpu_custom_call", output_to_operand_aliasing={{0}: (5, {})} | custom-call | flops 6442450944 | bytes 4194304 | tf_op jit(solution)/shard_map/step/pallas_call | solution.py:133
  85.7 6.9 %step.29 = (f32[4,512,512]{2,1,0:T(8,128)S(1)}, f32[8,128]{1,0:T(8,128)}) custom-call(s32[9]{0:T(128)S(1)} %pad_add_fusion.info, f32[4,512,4096]{2,1,0:T(8,128)} %bitcast.20, f32[4,512,4096]{2,1,0:T(8,128)} %collective-permute-done.refs_1_, f32[512,256]{1,0:T(8,128)S(1)} %collective-permute-done.5.refs_1_.refs_2_, ...), custom_call_target="tpu_custom_call", output_to_operand_aliasing={{0}: (5, {})} | custom-call | flops 6442450944 | bytes 4194304 | tf_op jit(solution)/shard_map/step/pallas_call | solution.py:133
  92.6 2.0 collective-permute-done.14.refs_5_
  94.6 9.8 %step.30 = (f32[512,256]{1,0:T(8,128)S(1)}, f32[512,256]{1,0:T(8,128)S(1)}, f32[8,128]{1,0:T(8,128)}) custom-call(s32[9]{0:T(128)S(1)} %pad_add_fusion.info, f32[4,512,4096]{2,1,0:T(8,128)} %bitcast.21, f32[4,512,4096]{2,1,0:T(8,128)} %collective-permute-done.refs_1_, f32[512,256]{1,0:T(8,128)S(1)} %collective-permute-done.10.refs_2_, ...), custom_call_target="tpu_custom_call" | custom-call | flops 12884901888 | bytes 8388608 | tf_op jit(solution)/shard_map/step/pallas_call | solution.py:133
  107.6 6.1 %step.31 = (f32[4,512,512]{2,1,0:T(8,128)S(1)}, f32[8,128]{1,0:T(8,128)}) custom-call(s32[9]{0:T(128)S(1)} %pad_add_fusion.info, f32[4,512,4096]{2,1,0:T(8,128)} %bitcast.22, f32[4,512,4096]{2,1,0:T(8,128)} %collective-permute-done.refs_1_, f32[512,256]{1,0:T(8,128)S(1)} %get-tuple-element.89.refs_2_.rest_3_, f32[512,256]{1,0:T(8,128)S(1)} %get-tuple-element.90.refs_3_.rest_4_), custom_call_target="tpu_custom_call" | custom-call | flops 6442450944 | bytes 4194304 | tf_op jit(solution)/shard_map/step/pallas_call | solution.py:133
  115.2 4.1 %collective-permute-done.24.refs_2_ = f32[512,256]{1,0:T(8,128)S(1)} collective-permute-done((f32[512,256]{1,0:T(8,128)S(1)}, f32[512,256]{1,0:T(8,128)S(1)}, u32[]{:S(2)}, u32[]{:S(2)}) %collective-permute-start.24) | collective-permute-done | bytes 524320 | tf_op jit(solution)/shard_map/ppermute | solution.py:215
  120.9 6.2 %step.32 = (f32[4,512,512]{2,1,0:T(8,128)S(1)}, f32[8,128]{1,0:T(8,128)S(1)}) custom-call(s32[9]{0:T(128)S(1)} %pad_add_fusion.info, f32[4,512,4096]{2,1,0:T(8,128)} %bitcast.23, f32[4,512,4096]{2,1,0:T(8,128)} %collective-permute-done.refs_1_, f32[512,256]{1,0:T(8,128)S(1)} %collective-permute-done.24.refs_2_, ...), custom_call_target="tpu_custom_call", output_to_operand_aliasing={{0}: (5, {})} | custom-call | flops 6442450944 | bytes 4194304 | tf_op jit(solution)/shard_map/step/pallas_call | solution.py:133
  132.1 6.2 %step.33 = (f32[4,512,512]{2,1,0:T(8,128)S(1)}, f32[8,128]{1,0:T(8,128)S(1)}) custom-call(s32[9]{0:T(128)S(1)} %pad_add_fusion.info, f32[4,512,4096]{2,1,0:T(8,128)} %bitcast.24, f32[4,512,4096]{2,1,0:T(8,128)} %collective-permute-done.refs_1_, f32[512,256]{1,0:T(8,128)S(1)} %collective-permute-done.25.refs_2_, ...), custom_call_target="tpu_custom_call", output_to_operand_aliasing={{0}: (6, {})} | custom-call | flops 6442450944 | bytes 4194304 | tf_op jit(solution)/shard_map/step/pallas_call | solution.py:133
  141.2 2.0 collective-permute-done.26.refs_2_
  144.8 6.2 %step.34 = (f32[4,512,512]{2,1,0:T(8,128)S(1)}, f32[8,128]{1,0:T(8,128)}) custom-call(s32[9]{0:T(128)S(1)} %pad_add_fusion.info, f32[4,512,4096]{2,1,0:T(8,128)} %bitcast.25, f32[4,512,4096]{2,1,0:T(8,128)} %collective-permute-done.refs_1_, f32[512,256]{1,0:T(8,128)S(1)} %collective-permute-done.26.refs_2_, ...), custom_call_target="tpu_custom_call", output_to_operand_aliasing={{0}: (6, {})} | custom-call | flops 6442450944 | bytes 4194304 | tf_op jit(solution)/shard_map/step/pallas_call | solution.py:133
  151.6 2.9 %collective-permute-done.27.refs_2_ = f32[512,256]{1,0:T(8,128)S(1)} collective-permute-done((f32[512,256]{1,0:T(8,128)S(1)}, f32[512,256]{1,0:T(8,128)S(1)}, u32[]{:S(2)}, u32[]{:S(2)}) %collective-permute-start.27) | collective-permute-done | bytes 524320 | tf_op jit(solution)/shard_map/ppermute | solution.py:215
  156.0 6.2 %step.35 = (f32[4,512,512]{2,1,0:T(8,128)S(1)}, f32[8,128]{1,0:T(8,128)}) custom-call(s32[9]{0:T(128)S(1)} %pad_add_fusion.info, f32[4,512,4096]{2,1,0:T(8,128)} %bitcast.26, f32[4,512,4096]{2,1,0:T(8,128)} %collective-permute-done.refs_1_, f32[512,256]{1,0:T(8,128)S(1)} %collective-permute-done.27.refs_2_, ...), custom_call_target="tpu_custom_call", output_to_operand_aliasing={{0}: (5, {})} | custom-call | flops 6442450944 | bytes 4194304 | tf_op jit(solution)/shard_map/step/pallas_call | solution.py:133
  162.8 3.1 %collective-permute-done.28.refs_2_ = f32[512,256]{1,0:T(8,128)S(1)} collective-permute-done((f32[512,256]{1,0:T(8,128)S(1)}, f32[512,256]{1,0:T(8,128)S(1)}, u32[]{:S(2)}, u32[]{:S(2)}) %collective-permute-start.28) | collective-permute-done | bytes 524320 | tf_op jit(solution)/shard_map/ppermute | solution.py:215
  167.3 6.2 %step.36 = (f32[4,512,512]{2,1,0:T(8,128)S(1)}, f32[8,128]{1,0:T(8,128)}) custom-call(s32[9]{0:T(128)S(1)} %pad_add_fusion.info, f32[4,512,4096]{2,1,0:T(8,128)} %bitcast.27, f32[4,512,4096]{2,1,0:T(8,128)} %collective-permute-done.refs_1_, f32[512,256]{1,0:T(8,128)S(1)} %collective-permute-done.28.refs_2_, ...), custom_call_target="tpu_custom_call", output_to_operand_aliasing={{0}: (5, {})} | custom-call | flops 6442450944 | bytes 4194304 | tf_op jit(solution)/shard_map/step/pallas_call | solution.py:133
  173.5 3.6 %collective-permute-done.29.refs_2_ = f32[512,256]{1,0:T(8,128)S(1)} collective-permute-done((f32[512,256]{1,0:T(8,128)S(1)}, f32[512,256]{1,0:T(8,128)S(1)}, u32[]{:S(2)}, u32[]{:S(2)}) %collective-permute-start.29) | collective-permute-done | bytes 524320 | tf_op jit(solution)/shard_map/ppermute | solution.py:215
  179.0 6.2 %step.37 = (f32[4,512,512]{2,1,0:T(8,128)S(1)}, f32[8,128]{1,0:T(8,128)}) custom-call(s32[9]{0:T(128)S(1)} %pad_add_fusion.info, f32[4,512,4096]{2,1,0:T(8,128)} %bitcast.28, f32[4,512,4096]{2,1,0:T(8,128)} %collective-permute-done.refs_1_, f32[512,256]{1,0:T(8,128)S(1)} %collective-permute-done.29.refs_2_, ...), custom_call_target="tpu_custom_call", output_to_operand_aliasing={{0}: (5, {})} | custom-call | flops 6442450944 | bytes 4194304 | tf_op jit(solution)/shard_map/step/pallas_call | solution.py:133
  186.3 4.9 %step.39 = (f32[512,256]{1,0:T(8,128)S(1)}, f32[8,128]{1,0:T(8,128)}) custom-call(s32[9]{0:T(128)S(1)} %pad_add_fusion.info, f32[4,512,4096]{2,1,0:T(8,128)} %bitcast.29, f32[4,512,4096]{2,1,0:T(8,128)} %collective-permute-done.refs_1_, f32[512,256]{1,0:T(8,128)S(1)} %collective-permute-done.31.refs_2_, f32[512,4]{1,0:T(8,128)S(1)} %bitcast.8, ...), custom_call_target="tpu_custom_call" | custom-call | flops 3221225472 | bytes 4194304 | tf_op jit(solution)/shard_map/step/pallas_call | solution.py:133
  192.5 5.2 %step.38 = (f32[512,256]{1,0:T(8,128)S(1)}, f32[8,128]{1,0:T(8,128)}) custom-call(s32[9]{0:T(128)S(1)} %pad_add_fusion.info, f32[4,512,4096]{2,1,0:T(8,128)} %bitcast.30, f32[4,512,4096]{2,1,0:T(8,128)} %collective-permute-done.refs_1_, f32[512,256]{1,0:T(8,128)S(1)} %collective-permute-done.23.refs_2_, f32[512,4]{1,0:T(8,128)S(1)} %bitcast.9, ...), custom_call_target="tpu_custom_call" | custom-call | flops 3221225472 | bytes 4194304 | tf_op jit(solution)/shard_map/step/pallas_call | solution.py:133
  (66 shorter events, 58.5 us)
Async XLA Ops:
  0.0 49.6 %collective-permute-start = (f32[4,512,4096]{2,1,0:T(8,128)}, f32[4,512,4096]{2,1,0:T(8,128)}, u32[]{:S(2)}, u32[]{:S(2)}) collective-permute-start(f32[4,512,4096]{2,1,0:T(8,128)} %bitcast.10), channel_id=1, source_target_pairs={{0,1},{1,0},{2,3},{3,2},{4,5},{5,4},{6,7},{7,6},{8,9},{9,8},{10,11... | collective-permute-start | bytes 100663304 | tf_op jit(solution)/shard_map/ppermute | solution.py:215
  1.7 9.8 %collective-permute-start.1 = (f32[512,256]{1,0:T(8,128)S(1)}, f32[512,256]{1,0:T(8,128)S(1)}, u32[]{:S(2)}, u32[]{:S(2)}) collective-permute-start(f32[512,256]{1,0:T(8,128)S(1)} %get-tuple-element.92.refs_1_.refs_2_), channel_id=1, source_target_pairs={{1,5},{3,1},{5,9},{7,3},{9,13},{11,7},{13,15},{15,11},{0,2},{2,6},... | collective-permute-start | bytes 1572872 | tf_op jit(solution)/shard_map/ppermute | solution.py:215
  4.3 12.8 %collective-permute-start.6 = (f32[512,256]{1,0:T(8,128)S(1)}, f32[512,256]{1,0:T(8,128)S(1)}, u32[]{:S(2)}, u32[]{:S(2)}) collective-permute-start(f32[512,256]{1,0:T(8,128)S(1)} %get-tuple-element.91.refs_2_.refs_3_), channel_id=1, source_target_pairs={{1,5},{3,1},{5,9},{7,3},{9,13},{11,7},{13,15},{15,11},{0,2},{2,6},... | collective-permute-start | bytes 1572872 | tf_op jit(solution)/shard_map/ppermute | solution.py:215
  11.5 11.2 %collective-permute-start.2 = (f32[512,256]{1,0:T(8,128)S(1)}, f32[512,256]{1,0:T(8,128)S(1)}, u32[]{:S(2)}, u32[]{:S(2)}) collective-permute-start(f32[512,256]{1,0:T(8,128)S(1)} %collective-permute-done.1.refs_1_.refs_4_), channel_id=1, source_target_pairs={{1,5},{3,1},{5,9},{7,3},{9,13},{11,7},{13,15},{15,11},{0,2},{2,6},... | collective-permute-start | bytes 1572872 | tf_op jit(solution)/shard_map/ppermute | solution.py:215
  13.5 79.1 %collective-permute-start.15 = (f32[512,4]{1,0:T(8,128)S(1)}, f32[512,4]{1,0:T(8,128)S(1)}, u32[]{:S(2)}, u32[]{:S(2)}) collective-permute-start(f32[512,4]{1,0:T(8,128)S(1)} %bitcast.6), channel_id=1, source_target_pairs={{0,1},{1,0},{2,3},{3,2},{4,5},{5,4},{6,7},{7,6},{8,9},{9,8},{10,11... | collective-permute-start | bytes 24584 | tf_op jit(solution)/shard_map/ppermute | solution.py:215
  16.3 76.3 %collective-permute-start.16 = (f32[4,1024]{1,0:T(4,128)S(1)}, f32[4,1024]{1,0:T(4,128)S(1)}, u32[]{:S(2)}, u32[]{:S(2)}) collective-permute-start(f32[4,1024]{1,0:T(4,128)S(1)} %select_reduce_fusion.refs_10_.refs_4_), channel_id=1, source_target_pairs={{0,1},{1,0},{2,3},{3,2},{4,5},{5,4},{6,7},{7,6},{8,9},{9,8},{10,11... | collective-permute-start | bytes 49160 | tf_op jit(solution)/shard_map/ppermute | solution.py:215
  17.1 11.2 %collective-permute-start.7 = (f32[512,256]{1,0:T(8,128)S(1)}, f32[512,256]{1,0:T(8,128)S(1)}, u32[]{:S(2)}, u32[]{:S(2)}) collective-permute-start(f32[512,256]{1,0:T(8,128)S(1)} %collective-permute-done.6.refs_2_.refs_5_), channel_id=1, source_target_pairs={{1,5},{3,1},{5,9},{7,3},{9,13},{11,7},{13,15},{15,11},{0,2},{2,6},... | collective-permute-start | bytes 1572872 | tf_op jit(solution)/shard_map/ppermute | solution.py:215
  22.8 11.2 %collective-permute-start.3 = (f32[512,256]{1,0:T(8,128)S(1)}, f32[512,256]{1,0:T(8,128)S(1)}, u32[]{:S(2)}, u32[]{:S(2)}) collective-permute-start(f32[512,256]{1,0:T(8,128)S(1)} %collective-permute-done.2.refs_1_.refs_2_), channel_id=1, source_target_pairs={{1,5},{3,1},{5,9},{7,3},{9,13},{11,7},{13,15},{15,11},{0,2},{2,6},... | collective-permute-start | bytes 1572872 | tf_op jit(solution)/shard_map/ppermute | solution.py:215
  28.4 11.2 %collective-permute-start.8 = (f32[512,256]{1,0:T(8,128)S(1)}, f32[512,256]{1,0:T(8,128)S(1)}, u32[]{:S(2)}, u32[]{:S(2)}) collective-permute-start(f32[512,256]{1,0:T(8,128)S(1)} %collective-permute-done.7.refs_2_.refs_3_), channel_id=1, source_target_pairs={{1,5},{3,1},{5,9},{7,3},{9,13},{11,7},{13,15},{15,11},{0,2},{2,6},... | collective-permute-start | bytes 1572872 | tf_op jit(solution)/shard_map/ppermute | solution.py:215
  34.0 11.2 %collective-permute-start.4 = (f32[512,256]{1,0:T(8,128)S(1)}, f32[512,256]{1,0:T(8,128)S(1)}, u32[]{:S(2)}, u32[]{:S(2)}) collective-permute-start(f32[512,256]{1,0:T(8,128)S(1)} %collective-permute-done.3.refs_1_.refs_4_), channel_id=1, source_target_pairs={{1,5},{3,1},{5,9},{7,3},{9,13},{11,7},{13,15},{15,11},{0,2},{2,6},... | collective-permute-start | bytes 1572872 | tf_op jit(solution)/shard_map/ppermute | solution.py:215
  39.6 19.3 %collective-permute-start.9 = (f32[512,256]{1,0:T(8,128)S(1)}, f32[512,256]{1,0:T(8,128)S(1)}, u32[]{:S(2)}, u32[]{:S(2)}) collective-permute-start(f32[512,256]{1,0:T(8,128)S(1)} %collective-permute-done.8.refs_2_.refs_5_), channel_id=1, source_target_pairs={{1,5},{3,1},{5,9},{7,3},{9,13},{11,7},{13,15},{15,11},{0,2},{2,6},... | collective-permute-start | bytes 1572872 | tf_op jit(solution)/shard_map/ppermute | solution.py:215
  45.2 16.7 %collective-permute-start.5 = (f32[512,256]{1,0:T(8,128)S(1)}, f32[512,256]{1,0:T(8,128)S(1)}, u32[]{:S(2)}, u32[]{:S(2)}) collective-permute-start(f32[512,256]{1,0:T(8,128)S(1)} %collective-permute-done.4.refs_1_.refs_2_), channel_id=1, source_target_pairs={{1,5},{3,1},{5,9},{7,3},{9,13},{11,7},{13,15},{15,11},{0,2},{2,6},... | collective-permute-start | bytes 1572872 | tf_op jit(solution)/shard_map/ppermute | solution.py:215
  58.9 15.2 %collective-permute-start.11 = (f32[512,256]{1,0:T(8,128)S(1)}, f32[512,256]{1,0:T(8,128)S(1)}, u32[]{:S(2)}, u32[]{:S(2)}) collective-permute-start(f32[512,256]{1,0:T(8,128)S(1)} %collective-permute-done.9.refs_2_.refs_3_), channel_id=1, source_target_pairs={{1,5},{3,1},{5,9},{7,3},{9,13},{11,7},{13,15},{15,11},{0,2},{2,6},... | collective-permute-start | bytes 1572872 | tf_op jit(solution)/shard_map/ppermute | solution.py:215
  61.9 13.9 %collective-permute-start.10 = (f32[512,256]{1,0:T(8,128)S(1)}, f32[512,256]{1,0:T(8,128)S(1)}, u32[]{:S(2)}, u32[]{:S(2)}) collective-permute-start(f32[512,256]{1,0:T(8,128)S(1)} %collective-permute-done.5.refs_1_.refs_2_), channel_id=1, source_target_pairs={{1,5},{3,1},{5,9},{7,3},{9,13},{11,7},{13,15},{15,11},{0,2},{2,6},... | collective-permute-start | bytes 1572872 | tf_op jit(solution)/shard_map/ppermute | solution.py:215
  74.2 10.5 %collective-permute-start.12 = (f32[512,256]{1,0:T(8,128)S(1)}, f32[512,256]{1,0:T(8,128)S(1)}, u32[]{:S(2)}, u32[]{:S(2)}) collective-permute-start(f32[512,256]{1,0:T(8,128)S(1)} %collective-permute-done.11.refs_2_.refs_3_), channel_id=1, source_target_pairs={{1,5},{3,1},{5,9},{7,3},{9,13},{11,7},{13,15},{15,11},{0,2},{2,6},... | collective-permute-start | bytes 1572872 | tf_op jit(solution)/shard_map/ppermute | solution.py:215
  75.8 16.8 %collective-permute-start.13 = (f32[512,256]{1,0:T(8,128)S(1)}, f32[512,256]{1,0:T(8,128)S(1)}, u32[]{:S(2)}, u32[]{:S(2)}) collective-permute-start(f32[512,256]{1,0:T(8,128)S(1)} %collective-permute-done.10.refs_2_), channel_id=1, source_target_pairs={{1,5},{3,1},{5,9},{7,3},{9,13},{11,7},{13,15},{15,11},{0,2},{2,6},... | collective-permute-start | bytes 1572872 | tf_op jit(solution)/shard_map/ppermute | solution.py:215
  84.7 9.9 %collective-permute-start.14 = (f32[512,256]{1,0:T(8,128)S(1)}, f32[512,256]{1,0:T(8,128)S(1)}, u32[]{:S(2)}, u32[]{:S(2)}) collective-permute-start(f32[512,256]{1,0:T(8,128)S(1)} %collective-permute-done.12.refs_3_), channel_id=1, source_target_pairs={{1,5},{3,1},{5,9},{7,3},{9,13},{11,7},{13,15},{15,11},{0,2},{2,6},... | collective-permute-start | bytes 1572872 | tf_op jit(solution)/shard_map/ppermute | solution.py:215
  104.4 9.3 %collective-permute-start.17 = (f32[512,256]{1,0:T(8,128)S(1)}, f32[512,256]{1,0:T(8,128)S(1)}, u32[]{:S(2)}, u32[]{:S(2)}) collective-permute-start(f32[512,256]{1,0:T(8,128)S(1)} %get-tuple-element.90.refs_3_.rest_4_), channel_id=1, source_target_pairs={{1,5},{3,1},{5,9},{7,3},{9,13},{11,7},{13,15},{15,11},{0,2},{2,6},... | collective-permute-start | bytes 1572872 | tf_op jit(solution)/shard_map/ppermute | solution.py:215
  106.1 13.2 %collective-permute-start.24 = (f32[512,256]{1,0:T(8,128)S(1)}, f32[512,256]{1,0:T(8,128)S(1)}, u32[]{:S(2)}, u32[]{:S(2)}) collective-permute-start(f32[512,256]{1,0:T(8,128)S(1)} %get-tuple-element.89.refs_2_.rest_3_), channel_id=1, source_target_pairs={{1,5},{3,1},{5,9},{7,3},{9,13},{11,7},{13,15},{15,11},{0,2},{2,6},... | collective-permute-start | bytes 1572872 | tf_op jit(solution)/shard_map/ppermute | solution.py:215
  113.7 14.7 %collective-permute-start.18 = (f32[512,256]{1,0:T(8,128)S(1)}, f32[512,256]{1,0:T(8,128)S(1)}, u32[]{:S(2)}, u32[]{:S(2)}) collective-permute-start(f32[512,256]{1,0:T(8,128)S(1)} %collective-permute-done.17.refs_3_), channel_id=1, source_target_pairs={{1,5},{3,1},{5,9},{7,3},{9,13},{11,7},{13,15},{15,11},{0,2},{2,6},... | collective-permute-start | bytes 1572872 | tf_op jit(solution)/shard_map/ppermute | solution.py:215
  119.3 11.2 %collective-permute-start.25 = (f32[512,256]{1,0:T(8,128)S(1)}, f32[512,256]{1,0:T(8,128)S(1)}, u32[]{:S(2)}, u32[]{:S(2)}) collective-permute-start(f32[512,256]{1,0:T(8,128)S(1)} %collective-permute-done.24.refs_2_), channel_id=1, source_target_pairs={{1,5},{3,1},{5,9},{7,3},{9,13},{11,7},{13,15},{15,11},{0,2},{2,6},... | collective-permute-start | bytes 1572872 | tf_op jit(solution)/shard_map/ppermute | solution.py:215
  127.0 72.0 %collective-permute-start.33 = (f32[512,256]{1,0:T(8,128)S(1)}, f32[512,256]{1,0:T(8,128)S(1)}, u32[]{:S(2)}, u32[]{:S(2)}) collective-permute-start(f32[512,256]{1,0:T(8,128)S(1)} %get-tuple-element.89.refs_2_.rest_3_), channel_id=1, source_target_pairs={{0,1},{2,3},{4,5},{6,7},{8,9},{10,11},{12,13},{14,15},{16,17},{18,... | collective-permute-start | bytes 1572872 | tf_op jit(solution)/shard_map/ppermute | solution.py:215
  128.4 11.2 %collective-permute-start.19 = (f32[512,256]{1,0:T(8,128)S(1)}, f32[512,256]{1,0:T(8,128)S(1)}, u32[]{:S(2)}, u32[]{:S(2)}) collective-permute-start(f32[512,256]{1,0:T(8,128)S(1)} %collective-permute-done.18.refs_3_), channel_id=1, source_target_pairs={{1,5},{3,1},{5,9},{7,3},{9,13},{11,7},{13,15},{15,11},{0,2},{2,6},... | collective-permute-start | bytes 1572872 | tf_op jit(solution)/shard_map/ppermute | solution.py:215
  130.5 12.7 %collective-permute-start.26 = (f32[512,256]{1,0:T(8,128)S(1)}, f32[512,256]{1,0:T(8,128)S(1)}, u32[]{:S(2)}, u32[]{:S(2)}) collective-permute-start(f32[512,256]{1,0:T(8,128)S(1)} %collective-permute-done.25.refs_2_), channel_id=1, source_target_pairs={{1,5},{3,1},{5,9},{7,3},{9,13},{11,7},{13,15},{15,11},{0,2},{2,6},... | collective-permute-start | bytes 1572872 | tf_op jit(solution)/shard_map/ppermute | solution.py:215
  138.3 60.8 %collective-permute-start.34 = (f32[512,256]{1,0:T(8,128)S(1)}, f32[512,256]{1,0:T(8,128)S(1)}, u32[]{:S(2)}, u32[]{:S(2)}) collective-permute-start(f32[512,256]{1,0:T(8,128)S(1)} %get-tuple-element.90.refs_3_.rest_4_), channel_id=1, source_target_pairs={{0,1},{2,3},{4,5},{6,7},{8,9},{10,11},{12,13},{14,15},{16,17},{18,... | collective-permute-start | bytes 1572872 | tf_op jit(solution)/shard_map/ppermute | solution.py:215
  139.6 11.4 %collective-permute-start.20 = (f32[512,256]{1,0:T(8,128)S(1)}, f32[512,256]{1,0:T(8,128)S(1)}, u32[]{:S(2)}, u32[]{:S(2)}) collective-permute-start(f32[512,256]{1,0:T(8,128)S(1)} %collective-permute-done.19.refs_3_), channel_id=1, source_target_pairs={{1,5},{3,1},{5,9},{7,3},{9,13},{11,7},{13,15},{15,11},{0,2},{2,6},... | collective-permute-start | bytes 1572872 | tf_op jit(solution)/shard_map/ppermute | solution.py:215
  143.2 11.2 %collective-permute-start.27 = (f32[512,256]{1,0:T(8,128)S(1)}, f32[512,256]{1,0:T(8,128)S(1)}, u32[]{:S(2)}, u32[]{:S(2)}) collective-permute-start(f32[512,256]{1,0:T(8,128)S(1)} %collective-permute-done.26.refs_2_), channel_id=1, source_target_pairs={{1,5},{3,1},{5,9},{7,3},{9,13},{11,7},{13,15},{15,11},{0,2},{2,6},... | collective-permute-start | bytes 1572872 | tf_op jit(solution)/shard_map/ppermute | solution.py:215
  151.0 11.2 %collective-permute-start.21 = (f32[512,256]{1,0:T(8,128)S(1)}, f32[512,256]{1,0:T(8,128)S(1)}, u32[]{:S(2)}, u32[]{:S(2)}) collective-permute-start(f32[512,256]{1,0:T(8,128)S(1)} %collective-permute-done.20.refs_3_), channel_id=1, source_target_pairs={{1,5},{3,1},{5,9},{7,3},{9,13},{11,7},{13,15},{15,11},{0,2},{2,6},... | collective-permute-start | bytes 1572872 | tf_op jit(solution)/shard_map/ppermute | solution.py:215
  154.5 11.4 %collective-permute-start.28 = (f32[512,256]{1,0:T(8,128)S(1)}, f32[512,256]{1,0:T(8,128)S(1)}, u32[]{:S(2)}, u32[]{:S(2)}) collective-permute-start(f32[512,256]{1,0:T(8,128)S(1)} %collective-permute-done.27.refs_2_), channel_id=1, source_target_pairs={{1,5},{3,1},{5,9},{7,3},{9,13},{11,7},{13,15},{15,11},{0,2},{2,6},... | collective-permute-start | bytes 1572872 | tf_op jit(solution)/shard_map/ppermute | solution.py:215
  162.2 16.3 %collective-permute-start.22 = (f32[512,256]{1,0:T(8,128)S(1)}, f32[512,256]{1,0:T(8,128)S(1)}, u32[]{:S(2)}, u32[]{:S(2)}) collective-permute-start(f32[512,256]{1,0:T(8,128)S(1)} %collective-permute-done.21.refs_3_), channel_id=1, source_target_pairs={{1,5},{3,1},{5,9},{7,3},{9,13},{11,7},{13,15},{15,11},{0,2},{2,6},... | collective-permute-start | bytes 1572872 | tf_op jit(solution)/shard_map/ppermute | solution.py:215
  165.9 11.2 %collective-permute-start.29 = (f32[512,256]{1,0:T(8,128)S(1)}, f32[512,256]{1,0:T(8,128)S(1)}, u32[]{:S(2)}, u32[]{:S(2)}) collective-permute-start(f32[512,256]{1,0:T(8,128)S(1)} %collective-permute-done.28.refs_2_), channel_id=1, source_target_pairs={{1,5},{3,1},{5,9},{7,3},{9,13},{11,7},{13,15},{15,11},{0,2},{2,6},... | collective-permute-start | bytes 1572872 | tf_op jit(solution)/shard_map/ppermute | solution.py:215
  178.5 14.0 %collective-permute-start.23 = (f32[512,256]{1,0:T(8,128)S(1)}, f32[512,256]{1,0:T(8,128)S(1)}, u32[]{:S(2)}, u32[]{:S(2)}) collective-permute-start(f32[512,256]{1,0:T(8,128)S(1)} %collective-permute-done.22.refs_3_), channel_id=1, source_target_pairs={{1,5},{3,1},{5,9},{7,3},{9,13},{11,7},{13,15},{15,11},{0,2},{2,6},... | collective-permute-start | bytes 1572872 | tf_op jit(solution)/shard_map/ppermute | solution.py:215
  (3 other events, 20.9 us)

commit v5 on v4

--- a/solution.py
+++ b/solution.py
@@ -9,6 +9,7 @@
 
 CHAINS = 2
 EARLY = 3
+SLOTS = 3
 PAIR = 2
 COST = 12
 VMEM_LIMIT = 26 * 1024 * 1024
@@ -32,18 +33,23 @@
     width = x_high.shape[1]
     per_step = width // chain_width
     count = len(steps)
-    tile_count = rows // tile
+    tile_count, slots = rows // tile, tiles.shape[0]
     lanes = pl.ds(finish[0] * width if final else 0, width)
 
     def copies(t, slot, source):
         here = pl.ds(pl.multiple_of(t * tile, tile), tile)
+        parts = 1 if count > 1 else actions
+        share = actions // parts
         return [
             pltpu.make_async_copy(
-                source.at[:, here, pl.ds(pl.multiple_of(info[1 + step] * depth, depth), depth)],
-                tiles.at[slot, :, :, pl.ds(i * depth, depth)],
-                t_sem.at[slot, i],
+                source.at[
+                    pl.ds(a * share, share), here, pl.ds(pl.multiple_of(info[1 + step] * depth, depth), depth)
+                ],
+                tiles.at[slot, pl.ds(a * share, share), :, pl.ds(i * depth, depth)],
+                t_sem.at[slot, i, a],
             )
             for i, step in enumerate(steps)
+            for a in range(parts)
         ]
 
     def fetch(t, slot):
@@ -58,7 +64,8 @@
             pl.when(info[0] != section)(lambda: start(kernels[1]))
 
     def work():
-        fetch(0, 0)
+        for t in range(min(slots - 1, tile_count)):
+            fetch(t, t)
         for j, block in enumerate(blocks):
             here = (
                 pl.ds(j // per_step * depth, depth),
@@ -68,12 +75,12 @@
 
         @pl.loop(0, tile_count)
         def _(t):
-            slot = lax.rem(t, 2)
+            slot = lax.rem(t, slots)
             here = pl.ds(pl.multiple_of(t * tile, tile), tile)
 
-            @pl.when(t + 1 < tile_count)
+            @pl.when(t + slots - 1 < tile_count)
             def _():
-                fetch(t + 1, 1 - slot)
+                fetch(t + slots - 1, lax.rem(t + slots - 1, slots))
 
             for copy in copies(t, slot, kernels[0]):
                 copy.wait()
@@ -109,6 +116,7 @@
     depth, chain_width = blocks[0].shape
     width = chain_width * len(blocks) // len(steps)
     tile = min(rows, 128)
+    slots = SLOTS if len(steps) == 1 else 2
     hbm = pl.BlockSpec(memory_space=pl.ANY)
     vmem = pl.BlockSpec(memory_space=pltpu.VMEM)
     named = [("own", own, pl.BlockSpec(memory_space=pltpu.HBM))]
@@ -138,8 +146,8 @@
         scratch_shapes=[
             pltpu.VMEM((len(steps) * depth, width), jnp.bfloat16),
             pltpu.VMEM((len(steps) * depth, width), jnp.bfloat16),
-            pltpu.VMEM((2, actions, tile, len(steps) * depth), jnp.float32),
-            pltpu.SemaphoreType.DMA((2, len(steps))),
+            pltpu.VMEM((slots, actions, tile, len(steps) * depth), jnp.float32),
+            pltpu.SemaphoreType.DMA((slots, len(steps), actions)),
         ],
         input_output_aliases=aliases,
         compiler_params=pltpu.CompilerParams(vmem_limit_bytes=VMEM_LIMIT),

time: 204 us -> 203 us (level)
  transfers between devices with their start and end apart: 35 -> 35, of which waited for: 17 -> 18; matrix products, arithmetic and copies ran while one was open for 2% -> 2% of each run, Pallas kernels for 46% -> 45%
where the time goes in v5:
time: 203 us; the launch traced here: 202 us
  Pallas kernels  103 us (51%)
  starting transfers between devices  53.7 us (26%)
  waiting for transfers between devices  41.1 us (20%)
  local copies, waits for them, and re-layouts  2.11 us (1%)
    pallas_call x20, Pallas kernels, step(): pl.pallas_call(functools.partial(step_kernel, section, steps, who, first,...  100 us
    ppermute x35, starting transfers between devices, send(): return lax.ppermute(value, ('rows', 'section'), pairs)  53.7 us
    ppermute x35, waiting for transfers between devices, send(): return lax.ppermute(value, ('rows', 'section'), pairs)  41.1 us
  transfers between devices with their start and end apart: 35, of which 18 were waited for; matrix products, arithmetic and copies ran while one was open for 2% of the time, Pallas kernels for 45%

profile of v5, /device:TPU:0, one launch (start us, length us, event | category | flops | bytes accessed | tf_op | source)
XLA Modules:
  0.0 202.2 jit_solution(11582524733099744417)
XLA Ops:
  1.7 2.6 %collective-permute-start.1 = (f32[512,256]{1,0:T(8,128)S(1)}, f32[512,256]{1,0:T(8,128)S(1)}, u32[]{:S(2)}, u32[]{:S(2)}) collective-permute-start(f32[512,256]{1,0:T(8,128)S(1)} %get-tuple-element.92.refs_1_.refs_2_), channel_id=1, source_target_pairs={{1,5},{3,1},{5,9},{7,3},{9,13},{11,7},{13,15},{15,11},{0,2},{2,6},... | collective-permute-start | bytes 1572872 | tf_op jit(solution)/shard_map/ppermute | solution.py:223
  11.5 2.0 collective-permute-start.2
  13.5 2.6 %collective-permute-start.15 = (f32[512,4]{1,0:T(8,128)S(1)}, f32[512,4]{1,0:T(8,128)S(1)}, u32[]{:S(2)}, u32[]{:S(2)}) collective-permute-start(f32[512,4]{1,0:T(8,128)S(1)} %bitcast.6), channel_id=1, source_target_pairs={{0,1},{1,0},{2,3},{3,2},{4,5},{5,4},{6,7},{7,6},{8,9},{9,8},{10,11... | collective-permute-start | bytes 24584 | tf_op jit(solution)/shard_map/ppermute | solution.py:223
  20.4 2.4 %collective-permute-done.2.refs_1_.refs_2_ = f32[512,256]{1,0:T(8,128)S(1)} collective-permute-done((f32[512,256]{1,0:T(8,128)S(1)}, f32[512,256]{1,0:T(8,128)S(1)}, u32[]{:S(2)}, u32[]{:S(2)}) %collective-permute-start.2) | collective-permute-done | bytes 524320 | tf_op jit(solution)/shard_map/ppermute | solution.py:223
  22.8 2.0 collective-permute-start.3
  24.7 3.7 %collective-permute-done.7.refs_2_.refs_3_ = f32[512,256]{1,0:T(8,128)S(1)} collective-permute-done((f32[512,256]{1,0:T(8,128)S(1)}, f32[512,256]{1,0:T(8,128)S(1)}, u32[]{:S(2)}, u32[]{:S(2)}) %collective-permute-start.7) | collective-permute-done | bytes 524320 | tf_op jit(solution)/shard_map/ppermute | solution.py:223
  28.4 2.0 collective-permute-start.8
  31.6 2.4 %collective-permute-done.3.refs_1_.refs_4_ = f32[512,256]{1,0:T(8,128)S(1)} collective-permute-done((f32[512,256]{1,0:T(8,128)S(1)}, f32[512,256]{1,0:T(8,128)S(1)}, u32[]{:S(2)}, u32[]{:S(2)}) %collective-permute-start.3) | collective-permute-done | bytes 524320 | tf_op jit(solution)/shard_map/ppermute | solution.py:223
  36.0 3.7 %collective-permute-done.8.refs_2_.refs_5_ = f32[512,256]{1,0:T(8,128)S(1)} collective-permute-done((f32[512,256]{1,0:T(8,128)S(1)}, f32[512,256]{1,0:T(8,128)S(1)}, u32[]{:S(2)}, u32[]{:S(2)}) %collective-permute-start.8) | collective-permute-done | bytes 524320 | tf_op jit(solution)/shard_map/ppermute | solution.py:223
  42.8 2.4 %collective-permute-done.4.refs_1_.refs_2_ = f32[512,256]{1,0:T(8,128)S(1)} collective-permute-done((f32[512,256]{1,0:T(8,128)S(1)}, f32[512,256]{1,0:T(8,128)S(1)}, u32[]{:S(2)}, u32[]{:S(2)}) %collective-permute-start.4) | collective-permute-done | bytes 524320 | tf_op jit(solution)/shard_map/ppermute | solution.py:223
  47.2 2.4 %collective-permute-done.refs_1_ = f32[4,512,4096]{2,1,0:T(8,128)} collective-permute-done((f32[4,512,4096]{2,1,0:T(8,128)}, f32[4,512,4096]{2,1,0:T(8,128)}, u32[]{:S(2)}, u32[]{:S(2)}) %collective-permute-start) | collective-permute-done | bytes 33554464 | tf_op jit(solution)/shard_map/ppermute | solution.py:223
  49.6 9.5 %step.24 = (f32[4,512,512]{2,1,0:T(8,128)S(1)}, f32[8,128]{1,0:T(8,128)S(1)}) custom-call(s32[9]{0:T(128)S(1)} %pad_add_fusion.info, f32[4,512,4096]{2,1,0:T(8,128)} %bitcast.15, f32[4,512,4096]{2,1,0:T(8,128)} %collective-permute-done.refs_1_, f32[512,256]{1,0:T(8,128)S(1)} %get-tuple-element.92.refs_1_.refs_2_, ...), custom_call_target="tpu_custom_call", output_to_operand_aliasing={{0}: (7, {})} | custom-call | flops 12884901888 | bytes 8388608 | tf_op jit(solution)/shard_map/step/pallas_call | solution.py:141
  59.0 2.9 %collective-permute-start.11 = (f32[512,256]{1,0:T(8,128)S(1)}, f32[512,256]{1,0:T(8,128)S(1)}, u32[]{:S(2)}, u32[]{:S(2)}) collective-permute-start(f32[512,256]{1,0:T(8,128)S(1)} %collective-permute-done.9.refs_2_.refs_3_), channel_id=1, source_target_pairs={{1,5},{3,1},{5,9},{7,3},{9,13},{11,7},{13,15},{15,11},{0,2},{2,6},... | collective-permute-start | bytes 1572872 | tf_op jit(solution)/shard_map/ppermute | solution.py:223
  64.8 9.6 %step.26 = (f32[4,512,512]{2,1,0:T(8,128)S(1)}, f32[8,128]{1,0:T(8,128)S(1)}) custom-call(s32[9]{0:T(128)S(1)} %pad_add_fusion.info, f32[4,512,4096]{2,1,0:T(8,128)} %bitcast.17, f32[4,512,4096]{2,1,0:T(8,128)} %collective-permute-done.refs_1_, f32[512,256]{1,0:T(8,128)S(1)} %collective-permute-done.2.refs_1_.refs_2_, ...), custom_call_target="tpu_custom_call", output_to_operand_aliasing={{0}: (7, {})} | custom-call | flops 12884901888 | bytes 8388608 | tf_op jit(solution)/shard_map/step/pallas_call | solution.py:141
  78.9 6.0 %step.28 = (f32[4,512,512]{2,1,0:T(8,128)S(1)}, f32[8,128]{1,0:T(8,128)S(1)}) custom-call(s32[9]{0:T(128)S(1)} %pad_add_fusion.info, f32[4,512,4096]{2,1,0:T(8,128)} %bitcast.19, f32[4,512,4096]{2,1,0:T(8,128)} %collective-permute-done.refs_1_, f32[512,256]{1,0:T(8,128)S(1)} %collective-permute-done.4.refs_1_.refs_2_, ...), custom_call_target="tpu_custom_call", output_to_operand_aliasing={{0}: (5, {})} | custom-call | flops 6442450944 | bytes 4194304 | tf_op jit(solution)/shard_map/step/pallas_call | solution.py:141
  85.7 6.7 %step.29 = (f32[4,512,512]{2,1,0:T(8,128)S(1)}, f32[8,128]{1,0:T(8,128)}) custom-call(s32[9]{0:T(128)S(1)} %pad_add_fusion.info, f32[4,512,4096]{2,1,0:T(8,128)} %bitcast.20, f32[4,512,4096]{2,1,0:T(8,128)} %collective-permute-done.refs_1_, f32[512,256]{1,0:T(8,128)S(1)} %collective-permute-done.5.refs_1_.refs_2_, ...), custom_call_target="tpu_custom_call", output_to_operand_aliasing={{0}: (5, {})} | custom-call | flops 6442450944 | bytes 4194304 | tf_op jit(solution)/shard_map/step/pallas_call | solution.py:141
  92.4 2.5 %collective-permute-done.14.refs_5_ = f32[512,256]{1,0:T(8,128)S(1)} collective-permute-done((f32[512,256]{1,0:T(8,128)S(1)}, f32[512,256]{1,0:T(8,128)S(1)}, u32[]{:S(2)}, u32[]{:S(2)}) %collective-permute-start.14) | collective-permute-done | bytes 524320 | tf_op jit(solution)/shard_map/ppermute | solution.py:223
  94.9 9.9 %step.30 = (f32[512,256]{1,0:T(8,128)S(1)}, f32[512,256]{1,0:T(8,128)S(1)}, f32[8,128]{1,0:T(8,128)}) custom-call(s32[9]{0:T(128)S(1)} %pad_add_fusion.info, f32[4,512,4096]{2,1,0:T(8,128)} %bitcast.21, f32[4,512,4096]{2,1,0:T(8,128)} %collective-permute-done.refs_1_, f32[512,256]{1,0:T(8,128)S(1)} %collective-permute-done.10.refs_2_, ...), custom_call_target="tpu_custom_call" | custom-call | flops 12884901888 | bytes 8388608 | tf_op jit(solution)/shard_map/step/pallas_call | solution.py:141
  108.1 5.8 %step.31 = (f32[4,512,512]{2,1,0:T(8,128)S(1)}, f32[8,128]{1,0:T(8,128)}) custom-call(s32[9]{0:T(128)S(1)} %pad_add_fusion.info, f32[4,512,4096]{2,1,0:T(8,128)} %bitcast.22, f32[4,512,4096]{2,1,0:T(8,128)} %collective-permute-done.refs_1_, f32[512,256]{1,0:T(8,128)S(1)} %get-tuple-element.89.refs_2_.rest_3_, f32[512,256]{1,0:T(8,128)S(1)} %get-tuple-element.90.refs_3_.rest_4_), custom_call_target="tpu_custom_call" | custom-call | flops 6442450944 | bytes 4194304 | tf_op jit(solution)/shard_map/step/pallas_call | solution.py:141
  115.7 4.0 %collective-permute-done.24.refs_2_ = f32[512,256]{1,0:T(8,128)S(1)} collective-permute-done((f32[512,256]{1,0:T(8,128)S(1)}, f32[512,256]{1,0:T(8,128)S(1)}, u32[]{:S(2)}, u32[]{:S(2)}) %collective-permute-start.24) | collective-permute-done | bytes 524320 | tf_op jit(solution)/shard_map/ppermute | solution.py:223
  121.3 6.0 %step.32 = (f32[4,512,512]{2,1,0:T(8,128)S(1)}, f32[8,128]{1,0:T(8,128)S(1)}) custom-call(s32[9]{0:T(128)S(1)} %pad_add_fusion.info, f32[4,512,4096]{2,1,0:T(8,128)} %bitcast.23, f32[4,512,4096]{2,1,0:T(8,128)} %collective-permute-done.refs_1_, f32[512,256]{1,0:T(8,128)S(1)} %collective-permute-done.24.refs_2_, ...), custom_call_target="tpu_custom_call", output_to_operand_aliasing={{0}: (5, {})} | custom-call | flops 6442450944 | bytes 4194304 | tf_op jit(solution)/shard_map/step/pallas_call | solution.py:141
  132.5 6.0 %step.33 = (f32[4,512,512]{2,1,0:T(8,128)S(1)}, f32[8,128]{1,0:T(8,128)S(1)}) custom-call(s32[9]{0:T(128)S(1)} %pad_add_fusion.info, f32[4,512,4096]{2,1,0:T(8,128)} %bitcast.24, f32[4,512,4096]{2,1,0:T(8,128)} %collective-permute-done.refs_1_, f32[512,256]{1,0:T(8,128)S(1)} %collective-permute-done.25.refs_2_, ...), custom_call_target="tpu_custom_call", output_to_operand_aliasing={{0}: (6, {})} | custom-call | flops 6442450944 | bytes 4194304 | tf_op jit(solution)/shard_map/step/pallas_call | solution.py:141
  141.5 2.0 collective-permute-done.26.refs_2_
  145.0 6.0 %step.34 = (f32[4,512,512]{2,1,0:T(8,128)S(1)}, f32[8,128]{1,0:T(8,128)}) custom-call(s32[9]{0:T(128)S(1)} %pad_add_fusion.info, f32[4,512,4096]{2,1,0:T(8,128)} %bitcast.25, f32[4,512,4096]{2,1,0:T(8,128)} %collective-permute-done.refs_1_, f32[512,256]{1,0:T(8,128)S(1)} %collective-permute-done.26.refs_2_, ...), custom_call_target="tpu_custom_call", output_to_operand_aliasing={{0}: (6, {})} | custom-call | flops 6442450944 | bytes 4194304 | tf_op jit(solution)/shard_map/step/pallas_call | solution.py:141
  151.6 3.1 %collective-permute-done.27.refs_2_ = f32[512,256]{1,0:T(8,128)S(1)} collective-permute-done((f32[512,256]{1,0:T(8,128)S(1)}, f32[512,256]{1,0:T(8,128)S(1)}, u32[]{:S(2)}, u32[]{:S(2)}) %collective-permute-start.27) | collective-permute-done | bytes 524320 | tf_op jit(solution)/shard_map/ppermute | solution.py:223
  156.3 6.0 %step.35 = (f32[4,512,512]{2,1,0:T(8,128)S(1)}, f32[8,128]{1,0:T(8,128)}) custom-call(s32[9]{0:T(128)S(1)} %pad_add_fusion.info, f32[4,512,4096]{2,1,0:T(8,128)} %bitcast.26, f32[4,512,4096]{2,1,0:T(8,128)} %collective-permute-done.refs_1_, f32[512,256]{1,0:T(8,128)S(1)} %collective-permute-done.27.refs_2_, ...), custom_call_target="tpu_custom_call", output_to_operand_aliasing={{0}: (5, {})} | custom-call | flops 6442450944 | bytes 4194304 | tf_op jit(solution)/shard_map/step/pallas_call | solution.py:141
  162.8 3.1 %collective-permute-done.28.refs_2_ = f32[512,256]{1,0:T(8,128)S(1)} collective-permute-done((f32[512,256]{1,0:T(8,128)S(1)}, f32[512,256]{1,0:T(8,128)S(1)}, u32[]{:S(2)}, u32[]{:S(2)}) %collective-permute-start.28) | collective-permute-done | bytes 524320 | tf_op jit(solution)/shard_map/ppermute | solution.py:223
  167.5 6.0 %step.36 = (f32[4,512,512]{2,1,0:T(8,128)S(1)}, f32[8,128]{1,0:T(8,128)}) custom-call(s32[9]{0:T(128)S(1)} %pad_add_fusion.info, f32[4,512,4096]{2,1,0:T(8,128)} %bitcast.27, f32[4,512,4096]{2,1,0:T(8,128)} %collective-permute-done.refs_1_, f32[512,256]{1,0:T(8,128)S(1)} %collective-permute-done.28.refs_2_, ...), custom_call_target="tpu_custom_call", output_to_operand_aliasing={{0}: (5, {})} | custom-call | flops 6442450944 | bytes 4194304 | tf_op jit(solution)/shard_map/step/pallas_call | solution.py:141
  173.5 3.7 %collective-permute-done.29.refs_2_ = f32[512,256]{1,0:T(8,128)S(1)} collective-permute-done((f32[512,256]{1,0:T(8,128)S(1)}, f32[512,256]{1,0:T(8,128)S(1)}, u32[]{:S(2)}, u32[]{:S(2)}) %collective-permute-start.29) | collective-permute-done | bytes 524320 | tf_op jit(solution)/shard_map/ppermute | solution.py:223
  179.3 6.0 %step.37 = (f32[4,512,512]{2,1,0:T(8,128)S(1)}, f32[8,128]{1,0:T(8,128)}) custom-call(s32[9]{0:T(128)S(1)} %pad_add_fusion.info, f32[4,512,4096]{2,1,0:T(8,128)} %bitcast.28, f32[4,512,4096]{2,1,0:T(8,128)} %collective-permute-done.refs_1_, f32[512,256]{1,0:T(8,128)S(1)} %collective-permute-done.29.refs_2_, ...), custom_call_target="tpu_custom_call", output_to_operand_aliasing={{0}: (5, {})} | custom-call | flops 6442450944 | bytes 4194304 | tf_op jit(solution)/shard_map/step/pallas_call | solution.py:141
  186.4 4.6 %step.39 = (f32[512,256]{1,0:T(8,128)S(1)}, f32[8,128]{1,0:T(8,128)}) custom-call(s32[9]{0:T(128)S(1)} %pad_add_fusion.info, f32[4,512,4096]{2,1,0:T(8,128)} %bitcast.29, f32[4,512,4096]{2,1,0:T(8,128)} %collective-permute-done.refs_1_, f32[512,256]{1,0:T(8,128)S(1)} %collective-permute-done.31.refs_2_, f32[512,4]{1,0:T(8,128)S(1)} %bitcast.8, ...), custom_call_target="tpu_custom_call" | custom-call | flops 3221225472 | bytes 4194304 | tf_op jit(solution)/shard_map/step/pallas_call | solution.py:141
  192.3 4.6 %step.38 = (f32[512,256]{1,0:T(8,128)S(1)}, f32[8,128]{1,0:T(8,128)}) custom-call(s32[9]{0:T(128)S(1)} %pad_add_fusion.info, f32[4,512,4096]{2,1,0:T(8,128)} %bitcast.30, f32[4,512,4096]{2,1,0:T(8,128)} %collective-permute-done.refs_1_, f32[512,256]{1,0:T(8,128)S(1)} %collective-permute-done.23.refs_2_, f32[512,4]{1,0:T(8,128)S(1)} %bitcast.9, ...), custom_call_target="tpu_custom_call" | custom-call | flops 3221225472 | bytes 4194304 | tf_op jit(solution)/shard_map/step/pallas_call | solution.py:141
  (66 shorter events, 59.8 us)
Async XLA Ops:
  0.0 49.6 %collective-permute-start = (f32[4,512,4096]{2,1,0:T(8,128)}, f32[4,512,4096]{2,1,0:T(8,128)}, u32[]{:S(2)}, u32[]{:S(2)}) collective-permute-start(f32[4,512,4096]{2,1,0:T(8,128)} %bitcast.10), channel_id=1, source_target_pairs={{0,1},{1,0},{2,3},{3,2},{4,5},{5,4},{6,7},{7,6},{8,9},{9,8},{10,11... | collective-permute-start | bytes 100663304 | tf_op jit(solution)/shard_map/ppermute | solution.py:223
  1.7 9.8 %collective-permute-start.1 = (f32[512,256]{1,0:T(8,128)S(1)}, f32[512,256]{1,0:T(8,128)S(1)}, u32[]{:S(2)}, u32[]{:S(2)}) collective-permute-start(f32[512,256]{1,0:T(8,128)S(1)} %get-tuple-element.92.refs_1_.refs_2_), channel_id=1, source_target_pairs={{1,5},{3,1},{5,9},{7,3},{9,13},{11,7},{13,15},{15,11},{0,2},{2,6},... | collective-permute-start | bytes 1572872 | tf_op jit(solution)/shard_map/ppermute | solution.py:223
  4.3 12.8 %collective-permute-start.6 = (f32[512,256]{1,0:T(8,128)S(1)}, f32[512,256]{1,0:T(8,128)S(1)}, u32[]{:S(2)}, u32[]{:S(2)}) collective-permute-start(f32[512,256]{1,0:T(8,128)S(1)} %get-tuple-element.91.refs_2_.refs_3_), channel_id=1, source_target_pairs={{1,5},{3,1},{5,9},{7,3},{9,13},{11,7},{13,15},{15,11},{0,2},{2,6},... | collective-permute-start | bytes 1572872 | tf_op jit(solution)/shard_map/ppermute | solution.py:223
  11.5 11.2 %collective-permute-start.2 = (f32[512,256]{1,0:T(8,128)S(1)}, f32[512,256]{1,0:T(8,128)S(1)}, u32[]{:S(2)}, u32[]{:S(2)}) collective-permute-start(f32[512,256]{1,0:T(8,128)S(1)} %collective-permute-done.1.refs_1_.refs_4_), channel_id=1, source_target_pairs={{1,5},{3,1},{5,9},{7,3},{9,13},{11,7},{13,15},{15,11},{0,2},{2,6},... | collective-permute-start | bytes 1572872 | tf_op jit(solution)/shard_map/ppermute | solution.py:223
  13.5 78.9 %collective-permute-start.15 = (f32[512,4]{1,0:T(8,128)S(1)}, f32[512,4]{1,0:T(8,128)S(1)}, u32[]{:S(2)}, u32[]{:S(2)}) collective-permute-start(f32[512,4]{1,0:T(8,128)S(1)} %bitcast.6), channel_id=1, source_target_pairs={{0,1},{1,0},{2,3},{3,2},{4,5},{5,4},{6,7},{7,6},{8,9},{9,8},{10,11... | collective-permute-start | bytes 24584 | tf_op jit(solution)/shard_map/ppermute | solution.py:223
  16.1 76.3 %collective-permute-start.16 = (f32[4,1024]{1,0:T(4,128)S(1)}, f32[4,1024]{1,0:T(4,128)S(1)}, u32[]{:S(2)}, u32[]{:S(2)}) collective-permute-start(f32[4,1024]{1,0:T(4,128)S(1)} %select_reduce_fusion.refs_10_.refs_4_), channel_id=1, source_target_pairs={{0,1},{1,0},{2,3},{3,2},{4,5},{5,4},{6,7},{7,6},{8,9},{9,8},{10,11... | collective-permute-start | bytes 49160 | tf_op jit(solution)/shard_map/ppermute | solution.py:223
  17.1 11.2 %collective-permute-start.7 = (f32[512,256]{1,0:T(8,128)S(1)}, f32[512,256]{1,0:T(8,128)S(1)}, u32[]{:S(2)}, u32[]{:S(2)}) collective-permute-start(f32[512,256]{1,0:T(8,128)S(1)} %collective-permute-done.6.refs_2_.refs_5_), channel_id=1, source_target_pairs={{1,5},{3,1},{5,9},{7,3},{9,13},{11,7},{13,15},{15,11},{0,2},{2,6},... | collective-permute-start | bytes 1572872 | tf_op jit(solution)/shard_map/ppermute | solution.py:223
  22.8 11.2 %collective-permute-start.3 = (f32[512,256]{1,0:T(8,128)S(1)}, f32[512,256]{1,0:T(8,128)S(1)}, u32[]{:S(2)}, u32[]{:S(2)}) collective-permute-start(f32[512,256]{1,0:T(8,128)S(1)} %collective-permute-done.2.refs_1_.refs_2_), channel_id=1, source_target_pairs={{1,5},{3,1},{5,9},{7,3},{9,13},{11,7},{13,15},{15,11},{0,2},{2,6},... | collective-permute-start | bytes 1572872 | tf_op jit(solution)/shard_map/ppermute | solution.py:223
  28.4 11.2 %collective-permute-start.8 = (f32[512,256]{1,0:T(8,128)S(1)}, f32[512,256]{1,0:T(8,128)S(1)}, u32[]{:S(2)}, u32[]{:S(2)}) collective-permute-start(f32[512,256]{1,0:T(8,128)S(1)} %collective-permute-done.7.refs_2_.refs_3_), channel_id=1, source_target_pairs={{1,5},{3,1},{5,9},{7,3},{9,13},{11,7},{13,15},{15,11},{0,2},{2,6},... | collective-permute-start | bytes 1572872 | tf_op jit(solution)/shard_map/ppermute | solution.py:223
  34.0 11.2 %collective-permute-start.4 = (f32[512,256]{1,0:T(8,128)S(1)}, f32[512,256]{1,0:T(8,128)S(1)}, u32[]{:S(2)}, u32[]{:S(2)}) collective-permute-start(f32[512,256]{1,0:T(8,128)S(1)} %collective-permute-done.3.refs_1_.refs_4_), channel_id=1, source_target_pairs={{1,5},{3,1},{5,9},{7,3},{9,13},{11,7},{13,15},{15,11},{0,2},{2,6},... | collective-permute-start | bytes 1572872 | tf_op jit(solution)/shard_map/ppermute | solution.py:223
  39.6 19.4 %collective-permute-start.9 = (f32[512,256]{1,0:T(8,128)S(1)}, f32[512,256]{1,0:T(8,128)S(1)}, u32[]{:S(2)}, u32[]{:S(2)}) collective-permute-start(f32[512,256]{1,0:T(8,128)S(1)} %collective-permute-done.8.refs_2_.refs_5_), channel_id=1, source_target_pairs={{1,5},{3,1},{5,9},{7,3},{9,13},{11,7},{13,15},{15,11},{0,2},{2,6},... | collective-permute-start | bytes 1572872 | tf_op jit(solution)/shard_map/ppermute | solution.py:223
  45.2 16.8 %collective-permute-start.5 = (f32[512,256]{1,0:T(8,128)S(1)}, f32[512,256]{1,0:T(8,128)S(1)}, u32[]{:S(2)}, u32[]{:S(2)}) collective-permute-start(f32[512,256]{1,0:T(8,128)S(1)} %collective-permute-done.4.refs_1_.refs_2_), channel_id=1, source_target_pairs={{1,5},{3,1},{5,9},{7,3},{9,13},{11,7},{13,15},{15,11},{0,2},{2,6},... | collective-permute-start | bytes 1572872 | tf_op jit(solution)/shard_map/ppermute | solution.py:223
  59.0 15.4 %collective-permute-start.11 = (f32[512,256]{1,0:T(8,128)S(1)}, f32[512,256]{1,0:T(8,128)S(1)}, u32[]{:S(2)}, u32[]{:S(2)}) collective-permute-start(f32[512,256]{1,0:T(8,128)S(1)} %collective-permute-done.9.refs_2_.refs_3_), channel_id=1, source_target_pairs={{1,5},{3,1},{5,9},{7,3},{9,13},{11,7},{13,15},{15,11},{0,2},{2,6},... | collective-permute-start | bytes 1572872 | tf_op jit(solution)/shard_map/ppermute | solution.py:223
  62.0 14.1 %collective-permute-start.10 = (f32[512,256]{1,0:T(8,128)S(1)}, f32[512,256]{1,0:T(8,128)S(1)}, u32[]{:S(2)}, u32[]{:S(2)}) collective-permute-start(f32[512,256]{1,0:T(8,128)S(1)} %collective-permute-done.5.refs_1_.refs_2_), channel_id=1, source_target_pairs={{1,5},{3,1},{5,9},{7,3},{9,13},{11,7},{13,15},{15,11},{0,2},{2,6},... | collective-permute-start | bytes 1572872 | tf_op jit(solution)/shard_map/ppermute | solution.py:223
  74.5 10.4 %collective-permute-start.12 = (f32[512,256]{1,0:T(8,128)S(1)}, f32[512,256]{1,0:T(8,128)S(1)}, u32[]{:S(2)}, u32[]{:S(2)}) collective-permute-start(f32[512,256]{1,0:T(8,128)S(1)} %collective-permute-done.11.refs_2_.refs_3_), channel_id=1, source_target_pairs={{1,5},{3,1},{5,9},{7,3},{9,13},{11,7},{13,15},{15,11},{0,2},{2,6},... | collective-permute-start | bytes 1572872 | tf_op jit(solution)/shard_map/ppermute | solution.py:223
  76.1 16.3 %collective-permute-start.13 = (f32[512,256]{1,0:T(8,128)S(1)}, f32[512,256]{1,0:T(8,128)S(1)}, u32[]{:S(2)}, u32[]{:S(2)}) collective-permute-start(f32[512,256]{1,0:T(8,128)S(1)} %collective-permute-done.10.refs_2_), channel_id=1, source_target_pairs={{1,5},{3,1},{5,9},{7,3},{9,13},{11,7},{13,15},{15,11},{0,2},{2,6},... | collective-permute-start | bytes 1572872 | tf_op jit(solution)/shard_map/ppermute | solution.py:223
  84.9 10.0 %collective-permute-start.14 = (f32[512,256]{1,0:T(8,128)S(1)}, f32[512,256]{1,0:T(8,128)S(1)}, u32[]{:S(2)}, u32[]{:S(2)}) collective-permute-start(f32[512,256]{1,0:T(8,128)S(1)} %collective-permute-done.12.refs_3_), channel_id=1, source_target_pairs={{1,5},{3,1},{5,9},{7,3},{9,13},{11,7},{13,15},{15,11},{0,2},{2,6},... | collective-permute-start | bytes 1572872 | tf_op jit(solution)/shard_map/ppermute | solution.py:223
  104.9 9.2 %collective-permute-start.17 = (f32[512,256]{1,0:T(8,128)S(1)}, f32[512,256]{1,0:T(8,128)S(1)}, u32[]{:S(2)}, u32[]{:S(2)}) collective-permute-start(f32[512,256]{1,0:T(8,128)S(1)} %get-tuple-element.90.refs_3_.rest_4_), channel_id=1, source_target_pairs={{1,5},{3,1},{5,9},{7,3},{9,13},{11,7},{13,15},{15,11},{0,2},{2,6},... | collective-permute-start | bytes 1572872 | tf_op jit(solution)/shard_map/ppermute | solution.py:223
  106.5 13.2 %collective-permute-start.24 = (f32[512,256]{1,0:T(8,128)S(1)}, f32[512,256]{1,0:T(8,128)S(1)}, u32[]{:S(2)}, u32[]{:S(2)}) collective-permute-start(f32[512,256]{1,0:T(8,128)S(1)} %get-tuple-element.89.refs_2_.rest_3_), channel_id=1, source_target_pairs={{1,5},{3,1},{5,9},{7,3},{9,13},{11,7},{13,15},{15,11},{0,2},{2,6},... | collective-permute-start | bytes 1572872 | tf_op jit(solution)/shard_map/ppermute | solution.py:223
  114.1 14.5 %collective-permute-start.18 = (f32[512,256]{1,0:T(8,128)S(1)}, f32[512,256]{1,0:T(8,128)S(1)}, u32[]{:S(2)}, u32[]{:S(2)}) collective-permute-start(f32[512,256]{1,0:T(8,128)S(1)} %collective-permute-done.17.refs_3_), channel_id=1, source_target_pairs={{1,5},{3,1},{5,9},{7,3},{9,13},{11,7},{13,15},{15,11},{0,2},{2,6},... | collective-permute-start | bytes 1572872 | tf_op jit(solution)/shard_map/ppermute | solution.py:223
  119.7 11.2 %collective-permute-start.25 = (f32[512,256]{1,0:T(8,128)S(1)}, f32[512,256]{1,0:T(8,128)S(1)}, u32[]{:S(2)}, u32[]{:S(2)}) collective-permute-start(f32[512,256]{1,0:T(8,128)S(1)} %collective-permute-done.24.refs_2_), channel_id=1, source_target_pairs={{1,5},{3,1},{5,9},{7,3},{9,13},{11,7},{13,15},{15,11},{0,2},{2,6},... | collective-permute-start | bytes 1572872 | tf_op jit(solution)/shard_map/ppermute | solution.py:223
  127.3 70.9 %collective-permute-start.33 = (f32[512,256]{1,0:T(8,128)S(1)}, f32[512,256]{1,0:T(8,128)S(1)}, u32[]{:S(2)}, u32[]{:S(2)}) collective-permute-start(f32[512,256]{1,0:T(8,128)S(1)} %get-tuple-element.89.refs_2_.rest_3_), channel_id=1, source_target_pairs={{0,1},{2,3},{4,5},{6,7},{8,9},{10,11},{12,13},{14,15},{16,17},{18,... | collective-permute-start | bytes 1572872 | tf_op jit(solution)/shard_map/ppermute | solution.py:223
  128.6 11.2 %collective-permute-start.19 = (f32[512,256]{1,0:T(8,128)S(1)}, f32[512,256]{1,0:T(8,128)S(1)}, u32[]{:S(2)}, u32[]{:S(2)}) collective-permute-start(f32[512,256]{1,0:T(8,128)S(1)} %collective-permute-done.18.refs_3_), channel_id=1, source_target_pairs={{1,5},{3,1},{5,9},{7,3},{9,13},{11,7},{13,15},{15,11},{0,2},{2,6},... | collective-permute-start | bytes 1572872 | tf_op jit(solution)/shard_map/ppermute | solution.py:223
  131.0 12.5 %collective-permute-start.26 = (f32[512,256]{1,0:T(8,128)S(1)}, f32[512,256]{1,0:T(8,128)S(1)}, u32[]{:S(2)}, u32[]{:S(2)}) collective-permute-start(f32[512,256]{1,0:T(8,128)S(1)} %collective-permute-done.25.refs_2_), channel_id=1, source_target_pairs={{1,5},{3,1},{5,9},{7,3},{9,13},{11,7},{13,15},{15,11},{0,2},{2,6},... | collective-permute-start | bytes 1572872 | tf_op jit(solution)/shard_map/ppermute | solution.py:223
  138.5 59.6 %collective-permute-start.34 = (f32[512,256]{1,0:T(8,128)S(1)}, f32[512,256]{1,0:T(8,128)S(1)}, u32[]{:S(2)}, u32[]{:S(2)}) collective-permute-start(f32[512,256]{1,0:T(8,128)S(1)} %get-tuple-element.90.refs_3_.rest_4_), channel_id=1, source_target_pairs={{0,1},{2,3},{4,5},{6,7},{8,9},{10,11},{12,13},{14,15},{16,17},{18,... | collective-permute-start | bytes 1572872 | tf_op jit(solution)/shard_map/ppermute | solution.py:223
  139.9 11.2 %collective-permute-start.20 = (f32[512,256]{1,0:T(8,128)S(1)}, f32[512,256]{1,0:T(8,128)S(1)}, u32[]{:S(2)}, u32[]{:S(2)}) collective-permute-start(f32[512,256]{1,0:T(8,128)S(1)} %collective-permute-done.19.refs_3_), channel_id=1, source_target_pairs={{1,5},{3,1},{5,9},{7,3},{9,13},{11,7},{13,15},{15,11},{0,2},{2,6},... | collective-permute-start | bytes 1572872 | tf_op jit(solution)/shard_map/ppermute | solution.py:223
  143.5 11.2 %collective-permute-start.27 = (f32[512,256]{1,0:T(8,128)S(1)}, f32[512,256]{1,0:T(8,128)S(1)}, u32[]{:S(2)}, u32[]{:S(2)}) collective-permute-start(f32[512,256]{1,0:T(8,128)S(1)} %collective-permute-done.26.refs_2_), channel_id=1, source_target_pairs={{1,5},{3,1},{5,9},{7,3},{9,13},{11,7},{13,15},{15,11},{0,2},{2,6},... | collective-permute-start | bytes 1572872 | tf_op jit(solution)/shard_map/ppermute | solution.py:223
  151.0 11.2 %collective-permute-start.21 = (f32[512,256]{1,0:T(8,128)S(1)}, f32[512,256]{1,0:T(8,128)S(1)}, u32[]{:S(2)}, u32[]{:S(2)}) collective-permute-start(f32[512,256]{1,0:T(8,128)S(1)} %collective-permute-done.20.refs_3_), channel_id=1, source_target_pairs={{1,5},{3,1},{5,9},{7,3},{9,13},{11,7},{13,15},{15,11},{0,2},{2,6},... | collective-permute-start | bytes 1572872 | tf_op jit(solution)/shard_map/ppermute | solution.py:223
  154.7 11.2 %collective-permute-start.28 = (f32[512,256]{1,0:T(8,128)S(1)}, f32[512,256]{1,0:T(8,128)S(1)}, u32[]{:S(2)}, u32[]{:S(2)}) collective-permute-start(f32[512,256]{1,0:T(8,128)S(1)} %collective-permute-done.27.refs_2_), channel_id=1, source_target_pairs={{1,5},{3,1},{5,9},{7,3},{9,13},{11,7},{13,15},{15,11},{0,2},{2,6},... | collective-permute-start | bytes 1572872 | tf_op jit(solution)/shard_map/ppermute | solution.py:223
  162.3 16.5 %collective-permute-start.22 = (f32[512,256]{1,0:T(8,128)S(1)}, f32[512,256]{1,0:T(8,128)S(1)}, u32[]{:S(2)}, u32[]{:S(2)}) collective-permute-start(f32[512,256]{1,0:T(8,128)S(1)} %collective-permute-done.21.refs_3_), channel_id=1, source_target_pairs={{1,5},{3,1},{5,9},{7,3},{9,13},{11,7},{13,15},{15,11},{0,2},{2,6},... | collective-permute-start | bytes 1572872 | tf_op jit(solution)/shard_map/ppermute | solution.py:223
  165.9 11.2 %collective-permute-start.29 = (f32[512,256]{1,0:T(8,128)S(1)}, f32[512,256]{1,0:T(8,128)S(1)}, u32[]{:S(2)}, u32[]{:S(2)}) collective-permute-start(f32[512,256]{1,0:T(8,128)S(1)} %collective-permute-done.28.refs_2_), channel_id=1, source_target_pairs={{1,5},{3,1},{5,9},{7,3},{9,13},{11,7},{13,15},{15,11},{0,2},{2,6},... | collective-permute-start | bytes 1572872 | tf_op jit(solution)/shard_map/ppermute | solution.py:223
  178.7 13.5 %collective-permute-start.23 = (f32[512,256]{1,0:T(8,128)S(1)}, f32[512,256]{1,0:T(8,128)S(1)}, u32[]{:S(2)}, u32[]{:S(2)}) collective-permute-start(f32[512,256]{1,0:T(8,128)S(1)} %collective-permute-done.22.refs_3_), channel_id=1, source_target_pairs={{1,5},{3,1},{5,9},{7,3},{9,13},{11,7},{13,15},{15,11},{0,2},{2,6},... | collective-permute-start | bytes 1572872 | tf_op jit(solution)/shard_map/ppermute | solution.py:223
  (3 other events, 20.2 us)
